TPU v7x, 256 devices: a whole 4x4x8 slice. The times are simulated.
256 devices in a mesh: group: 4 (over y), dev: 64 (over z, x, core).
Axes of the slice: x: 4, y: 4, z: 8, core: 2. Of those that a mesh axis runs over, the one named last changes fastest.
Arguments:
- embeddings: bfloat16 [524288, 1024], P(('group', 'dev')), may hold values from -6 to 6
- pair_blocks: int32 [4096, 2], P(('group', 'dev')), may hold values from -1 to 2047, as said below
- pair_count: int32 [256], P(('group', 'dev')), may hold values from 0 to 16, as said below
Outputs:
- smoothed: bfloat16 [524288, 1024], P(('group', 'dev'))
Inputs may be any that keep to these rules, and one draw needn't show every extreme that they name: `pair_blocks`: A used slot holds two global block numbers (left, right): left is a block of the slot's device; right is another block of that device, a block of the device with the next dev index in the same group, or a block of the device with the same dev index in the next group. No unordered pair of blocks is listed twice. Unused slots hold -1 in both places. `pair_count`: some device uses all 16 of its slots.
All inputs are finite; a program needn't handle non-finite values.
Results may differ from a plain program's by a relative error of at most 0.003.
Values may be sent and summed in bfloat16 or wider, within the bound.
A program may use at most 128 MiB of HBM per device.

v0:
```python
import jax
import jax.numpy as jnp
from jax import lax
from jax.sharding import PartitionSpec as P

BLOCK = 256


scale_factor = 0.4


def shifted(shard, axis, by):
    devices = lax.axis_size(axis)
    pairs = [(i, i + by) for i in range(devices) if 0 <= i + by < devices]
    return lax.ppermute(shard, axis, pairs)


def kernel_tile(left_rows, right_rows, left_sq, right_sq):
    inner = jnp.einsum("rd,cd->rc", left_rows, right_rows, preferred_element_type=jnp.float32)
    distance = left_sq[:, None] + right_sq[None, :] - 2.0 * inner
    return jnp.exp(-distance / (scale_factor * left_rows.shape[1])).astype(jnp.bfloat16)


def row_terms(weights, partner):
    return (
        jnp.dot(weights, partner, preferred_element_type=jnp.float32),
        jnp.sum(weights, axis=1, dtype=jnp.float32),
    )


def column_terms(weights, partner):
    return (
        jnp.einsum("rc,rd->cd", weights, partner, preferred_element_type=jnp.float32),
        jnp.sum(weights, axis=0, dtype=jnp.float32),
    )


def add_block(totals, index, terms):
    return (totals[0].at[index].add(terms[0]), totals[1].at[index].add(terms[1]))


def squares_of(blocks):
    return jnp.einsum("bsd,bsd->bs", blocks, blocks, preferred_element_type=jnp.float32)


def local(embeddings, pair_blocks, pair_count):
    total_rows, width = embeddings.shape
    local_count = total_rows // BLOCK
    blocks = embeddings.reshape(local_count, BLOCK, width)
    own_sq = squares_of(blocks)
    owners = lax.axis_size("dev")
    first_block = (lax.axis_index("group") * owners + lax.axis_index("dev")) * local_count
    inner = jnp.einsum("bsd,btd->bst", blocks, blocks, preferred_element_type=jnp.float32)
    distance = own_sq[:, :, None] + own_sq[:, None, :] - 2.0 * inner
    diag_weights = jnp.exp(-distance / (scale_factor * width)).astype(jnp.bfloat16)
    diag_numer = jnp.einsum(
        "bst,btd->bsd", diag_weights, blocks, preferred_element_type=jnp.float32
    )
    diag_denom = jnp.sum(diag_weights, axis=2, dtype=jnp.float32)
    after_dev = shifted(blocks, "dev", -1)
    after_group = shifted(blocks, "group", -1)
    pool = jnp.concatenate([blocks, after_dev, after_group], axis=0)
    pool_sq = jnp.concatenate([own_sq, squares_of(after_dev), squares_of(after_group)], axis=0)
    used_slots = pair_count[0]

    def locate(global_id):
        offset = global_id - first_block
        return jnp.where(
            offset < 2 * local_count, offset, offset - owners * local_count + 2 * local_count
        )

    totals = (
        jnp.concatenate(
            [diag_numer, jnp.zeros((2 * local_count, BLOCK, width), jnp.float32)], axis=0
        ),
        jnp.concatenate([diag_denom, jnp.zeros((2 * local_count, BLOCK), jnp.float32)], axis=0),
    )

    def each_pair(position, totals):
        left_idx = locate(pair_blocks[position, 0])
        right_idx = locate(pair_blocks[position, 1])
        left_rows = pool[left_idx]
        right_rows = pool[right_idx]
        weights = kernel_tile(left_rows, right_rows, pool_sq[left_idx], pool_sq[right_idx])
        totals = add_block(totals, left_idx, row_terms(weights, right_rows))
        return add_block(totals, right_idx, column_terms(weights, left_rows))

    numer, denom = lax.fori_loop(0, used_slots, each_pair, totals)
    from_dev = (
        shifted(numer[local_count : 2 * local_count].astype(jnp.bfloat16), "dev", 1).astype(
            jnp.float32
        ),
        shifted(denom[local_count : 2 * local_count].astype(jnp.bfloat16), "dev", 1).astype(
            jnp.float32
        ),
    )
    from_group = (
        shifted(numer[2 * local_count :].astype(jnp.bfloat16), "group", 1).astype(jnp.float32),
        shifted(denom[2 * local_count :].astype(jnp.bfloat16), "group", 1).astype(jnp.float32),
    )
    numer = numer[:local_count] + from_dev[0] + from_group[0]
    denom = denom[:local_count] + from_dev[1] + from_group[1]
    smoothed = (numer / denom[:, :, None]).astype(jnp.bfloat16)
    return smoothed.reshape(total_rows, width)


def solution(mesh):
    placed = (P(("group", "dev"), None), P(("group", "dev"), None), P(("group", "dev")))
    return jax.shard_map(
        local, mesh=mesh, in_specs=placed, out_specs=P(("group", "dev"), None), check_vma=False
    )
```

profile of v0, /device:TPU:22, one launch (start us, length us, event | category | flops | bytes accessed | tf_op | source)
XLA Modules:
  0.0 441.3 jit_solution(150110292945334571)
XLA Ops:
  0.0 2.3 collective-permute-start.1
  2.4 1.9 collective-permute-start
  4.3 3.2 fusion.20
  7.7 1.7 convert_reduce_fusion.2
  9.5 1.7 fusion.21
  11.2 8.8 %concatenate.56 = f32[24,256,1024]{2,1,0:T(8,128)} pad(f32[8,256,1024]{2,1,0:T(8,128)S(1)} %fusion.21, f32[]{:T(128)} %constant.213.clone.1), padding=0_16x0_0x0_0 | pad | bytes 33554436 | tf_op jit(solution)/shard_map/concatenate | solution.py:73
  20.1 74.4 %collective-permute-done.1 = bf16[8,256,1024]{2,1,0:T(8,128)(2,1)} collective-permute-done((bf16[8,256,1024]{2,1,0:T(8,128)(2,1)}, bf16[8,256,1024]{2,1,0:T(8,128)(2,1)}, u32[]{:S(2)}, u32[]{:S(2)}) %collective-permute-start.1) | collective-permute-done | bytes 4194336 | tf_op jit(solution)/shard_map/ppermute | solution.py:15
  94.5 3.1 fusion.18
  97.6 3.1 fusion.19
  100.7 9.4 %pad_maximum_fusion = bf16[24,256,1024]{2,1,0:T(8,128)(2,1)} fusion(bf16[8,256,1024]{2,1,0:T(8,128)(2,1)} %collective-permute-done.1, bf16[8,256,1024]{2,1,0:T(8,128)(2,1)} %collective-permute-done, bf16[8,256,1024]{2,1,0:T(8,128)(2,1)S(1)} %bitcast.79), kind=kLoop, calls=%fused_computation.43 | loop fusion | flops 12582912 | bytes 25165824 | tf_op jit(solution)/shard_map/concatenate | solution.py:62
  110.1 178.1 %while.21 = (s32[]{:T(128)}, f32[24,256,1024]{2,1,0:T(8,128)}, f32[24,256]{1,0:T(8,128)S(1)}, s32[]{:T(128)}, s32[16,2]{0,1:T(2,128)S(1)}, /*index=5*/s32[]{:T(1...) while((s32[]{:T(128)}, f32[24,256,1024]{2,1,0:T(8,128)}, ...), condition=%wide.region_8.9_spmd, body=%wide.region_1.8_spmd.sunk | while | flops 404292192 | bytes 6707645 | solution.py:88
  114.1 1.6 convert_reduce_fusion.4
  117.1 3.2 fusion.46
  120.4 3.3 fusion.47
  127.7 1.6 convert_reduce_fusion.4
  130.7 3.3 fusion.46
  134.0 3.3 fusion.47
  139.8 0.8 and_reduce_fusion.7
  141.3 1.6 convert_reduce_fusion.4
  144.4 3.3 fusion.46
  147.6 3.3 fusion.47
  153.4 0.8 and_reduce_fusion.7
  155.0 1.6 convert_reduce_fusion.4
  158.0 3.3 fusion.46
  161.3 3.3 fusion.47
  168.6 1.6 convert_reduce_fusion.4
  171.6 3.3 fusion.46
  174.9 3.4 fusion.47
  182.2 1.6 convert_reduce_fusion.4
  185.3 3.2 fusion.46
  188.5 3.3 fusion.47
  194.3 0.8 and_reduce_fusion.7
  195.8 1.6 convert_reduce_fusion.4
  198.9 3.3 fusion.46
  202.2 3.3 fusion.47
  209.5 1.6 convert_reduce_fusion.4
  212.5 3.3 fusion.46
  215.8 3.3 fusion.47
  223.1 1.6 convert_reduce_fusion.4
  226.2 3.3 fusion.46
  229.5 3.5 fusion.47
  235.4 0.8 and_reduce_fusion.7
  236.9 1.6 convert_reduce_fusion.4
  240.0 3.3 fusion.46
  243.2 3.4 fusion.47
  250.6 1.6 convert_reduce_fusion.4
  253.6 3.3 fusion.46
  256.9 3.3 fusion.47
  264.3 1.6 convert_reduce_fusion.4
  267.3 3.3 fusion.46
  270.6 3.3 fusion.47
  276.3 0.8 and_reduce_fusion.7
  277.9 1.6 convert_reduce_fusion.4
  280.9 3.3 fusion.46
  284.2 3.3 fusion.47
  288.2 9.3 %convert.8 = bf16[24,256,1024]{2,1,0:T(8,128)(2,1)S(1)} convert(f32[24,256,1024]{2,1,0:T(8,128)} %get-tuple-element.246) | non-fusion elementwise | flops 6291456 | bytes 37748736 | tf_op jit(solution)/shard_map/convert.3
  297.6 0.9 fusion.29
  298.5 41.8 %collective-permute-start.2 = (bf16[8,256,1024]{2,1,0:T(8,128)(2,1)S(1)}, bf16[8,256,1024]{2,1,0:T(8,128)(2,1)S(1)}, u32[]{:S(2)}, u32[]{:S(2)}) collective-permute-start(bf16[8,256,1024]{2,1,0:T(8,128)(2,1)S(1)} %get-tuple-element.275), channel_id=1, source_target_pairs={{0,1},{1,2},{2,3},{3,4},{4,5},{5,6},{6,7},{7,8},{8,9},{9,10},{10,1... | collective-permute-start | bytes 12582920 | tf_op jit(solution)/shard_map/ppermute | solution.py:15
  340.3 1.9 collective-permute-start.3
  342.2 1.9 collective-permute-start.4
  344.2 1.9 collective-permute-start.5
  346.1 2.3 collective-permute-done.4
  348.4 86.4 %collective-permute-done.5 = bf16[8,256]{1,0:T(8,128)(2,1)S(1)} collective-permute-done((bf16[8,256]{1,0:T(8,128)(2,1)S(1)}, bf16[8,256]{1,0:T(8,128)(2,1)S(1)}, u32[]{:S(2)}, u32[]{:S(2)}) %collective-permute-start.5) | collective-permute-done | bytes 4128 | tf_op jit(solution)/shard_map/ppermute | solution.py:15
  434.8 6.6 %divide_convert_fusion = bf16[8,256,1024]{2,1,0:T(8,128)(2,1)} fusion(bf16[8,256,1024]{2,1,0:T(8,128)(2,1)S(1)} %collective-permute-done.3, bf16[8,256,1024]{2,1,0:T(8,128)(2,1)S(1)} %collective-permute-done.2, f32[24,256,1024]{2,1,0:T(8,128)} %get-tuple-element.246, f32[8,256]{1,0:T(8,128)S(1)} %convert_add_fusion), kind=kLoop, calls=%fused_computation.50 | loop fusion | flops 12582912 | bytes 20979712 | tf_op jit(solution)/shard_map/convert_element_type | solution.py:103
  (117 shorter events, 41.9 us)
Async XLA Ops:
  0.0 94.5 %collective-permute-start.1 = (bf16[8,256,1024]{2,1,0:T(8,128)(2,1)}, bf16[8,256,1024]{2,1,0:T(8,128)(2,1)}, u32[]{:S(2)}, u32[]{:S(2)}) collective-permute-start(bf16[8,256,1024]{2,1,0:T(8,128)(2,1)} %bitcast.74), channel_id=1, source_target_pairs={{64,0},{128,64},{192,128},{65,1},{129,65},{193,129},{66,2},{130,66... | collective-permute-start | bytes 12582920 | tf_op jit(solution)/shard_map/ppermute | solution.py:15
  2.4 95.2 %collective-permute-start = (bf16[8,256,1024]{2,1,0:T(8,128)(2,1)}, bf16[8,256,1024]{2,1,0:T(8,128)(2,1)}, u32[]{:S(2)}, u32[]{:S(2)}) collective-permute-start(bf16[8,256,1024]{2,1,0:T(8,128)(2,1)} %bitcast.75), channel_id=1, source_target_pairs={{1,0},{2,1},{3,2},{4,3},{5,4},{6,5},{7,6},{8,7},{9,8},{10,9},{11,1... | collective-permute-start | bytes 12582920 | tf_op jit(solution)/shard_map/ppermute | solution.py:15
  4.3 3.5 copy-start
  20.1 80.6 %copy-start.1 = (bf16[2048,1024]{1,0:T(8,128)(2,1)S(1)}, bf16[2048,1024]{1,0:T(8,128)(2,1)}, u32[]{:S(2)}) copy-start(bf16[2048,1024]{1,0:T(8,128)(2,1)} %param.13) | copy-start | bytes 12582916
  100.7 9.4 %copy-start.2 = (s32[16,2]{0,1:T(2,128)S(1)}, s32[16,2]{0,1:T(2,128)}, u32[]{:S(2)}) copy-start(s32[16,2]{0,1:T(2,128)} %param.14) | copy-start | bytes 388
  100.7 9.4 %copy-start.3 = (s32[2]{0:T(128)S(1)}, s32[2]{0:T(128)}, u32[]{:S(2)}) copy-start(s32[2]{0:T(128)} %constant.208.clone.1) | copy-start | bytes 28
  100.7 9.4 %copy-start.4 = (s32[3]{0:T(128)S(1)}, s32[3]{0:T(128)}, u32[]{:S(2)}) copy-start(s32[3]{0:T(128)} %constant.204.clone.1) | copy-start | bytes 40
  298.5 136.3 %collective-permute-start.2 = (bf16[8,256,1024]{2,1,0:T(8,128)(2,1)S(1)}, bf16[8,256,1024]{2,1,0:T(8,128)(2,1)S(1)}, u32[]{:S(2)}, u32[]{:S(2)}) collective-permute-start(bf16[8,256,1024]{2,1,0:T(8,128)(2,1)S(1)} %get-tuple-element.275), channel_id=1, source_target_pairs={{0,1},{1,2},{2,3},{3,4},{4,5},{5,6},{6,7},{7,8},{8,9},{9,10},{10,1... | collective-permute-start | bytes 12582920 | tf_op jit(solution)/shard_map/ppermute | solution.py:15
  340.3 94.5 %collective-permute-start.3 = (bf16[8,256,1024]{2,1,0:T(8,128)(2,1)S(1)}, bf16[8,256,1024]{2,1,0:T(8,128)(2,1)S(1)}, u32[]{:S(2)}, u32[]{:S(2)}) collective-permute-start(bf16[8,256,1024]{2,1,0:T(8,128)(2,1)S(1)} %get-tuple-element.276), channel_id=1, source_target_pairs={{0,64},{64,128},{128,192},{1,65},{65,129},{129,193},{2,66},{66,130... | collective-permute-start | bytes 12582920 | tf_op jit(solution)/shard_map/ppermute | solution.py:15
  342.2 6.1 %collective-permute-start.4 = (bf16[8,256]{1,0:T(8,128)(2,1)S(1)}, bf16[8,256]{1,0:T(8,128)(2,1)S(1)}, u32[]{:S(2)}, u32[]{:S(2)}) collective-permute-start(bf16[8,256]{1,0:T(8,128)(2,1)S(1)} %get-tuple-element.277), channel_id=1, source_target_pairs={{0,1},{1,2},{2,3},{3,4},{4,5},{5,6},{6,7},{7,8},{8,9},{9,10},{10,1... | collective-permute-start | bytes 12296 | tf_op jit(solution)/shard_map/ppermute | solution.py:15
  344.2 90.6 %collective-permute-start.5 = (bf16[8,256]{1,0:T(8,128)(2,1)S(1)}, bf16[8,256]{1,0:T(8,128)(2,1)S(1)}, u32[]{:S(2)}, u32[]{:S(2)}) collective-permute-start(bf16[8,256]{1,0:T(8,128)(2,1)S(1)} %get-tuple-element.278), channel_id=1, source_target_pairs={{0,64},{64,128},{128,192},{1,65},{65,129},{129,193},{2,66},{66,130... | collective-permute-start | bytes 12296 | tf_op jit(solution)/shard_map/ppermute | solution.py:15
where the time goes:
time: 444 us; the launch traced here: 441 us
  waiting for transfers between devices  163 us (37%)
  matrix products  111 us (25%)
  other arithmetic  71.2 us (16%)
  starting transfers between devices  51.8 us (12%)
  loops' own time  25.3 us (6%)
  local copies, waits for them, and re-layouts  19 us (4%)
    ppermute x6, waiting for transfers between devices, shifted(): return lax.ppermute(shard, axis, pairs)  163 us
    ppermute x6, starting transfers between devices, shifted(): return lax.ppermute(shard, axis, pairs)  51.8 us
    another operation x54, other arithmetic  45.9 us
    dot_general x13, matrix products, column_terms(): jnp.einsum('rc,rd->cd', weights, partner, preferred_element_type=jnp.floa...  43.5 us
    dot_general x13, matrix products, row_terms(): jnp.dot(weights, partner, preferred_element_type=jnp.float32)  42.5 us
    another operation x1, loops' own time, local(): numer, denom = lax.fori_loop(0, used_slots, each_pair, totals)  25.3 us
    dot_general x13, matrix products, kernel_tile(): jnp.einsum('rd,cd->rc', left_rows, right_rows, preferred_element_type=jnp...  21.2 us
    dot_general x3, other arithmetic, squares_of(): jnp.einsum('bsd,bsd->bs', blocks, blocks, preferred_element_type=jnp.floa...  9.37 us
  transfers between devices with their start and end apart: 6, of which 3 were waited for; matrix products, arithmetic and copies ran while one was open for 4% of the time, Pallas kernels for 0%

commit v1 on v0

v1 whole, which is shorter than its diff:
```python
import jax
import jax.numpy as jnp
from jax import lax
from jax.experimental import pallas as pl
from jax.experimental.pallas import tpu as pltpu
from jax.sharding import PartitionSpec as P

BLOCK = 256
scale_factor = 0.4

C_T, C_SRC, C_PROW, C_VALID, C_FIRST, C_LAST, C_IDX = 0, 1, 2, 3, 4, 5, 6
NSRC = 5
NCOL = 16


def shifted(shard, axis, by):
    devices = lax.axis_size(axis)
    pairs = [(i, i + by) for i in range(devices) if 0 <= i + by < devices]
    return lax.ppermute(shard, axis, pairs)


def squares_of(blocks):
    return jnp.einsum("bsd,bsd->bs", blocks, blocks, preferred_element_type=jnp.float32)


def build_table(own_pairs, own_count, pd_pairs, pd_count, pg_pairs, pg_count,
                first_block, nloc, owners):
    slots = own_pairs.shape[0]
    pos = jnp.arange(slots, dtype=jnp.int32)

    def locate(g):
        off = g - first_block
        src = jnp.where(off < nloc, 0, jnp.where(off < 2 * nloc, 1, 2))
        idx = jnp.where(off < nloc, off, jnp.where(off < 2 * nloc, off - nloc,
                                                   g - first_block - owners * nloc))
        return src, idx

    used = pos < own_count[0]
    left = own_pairs[:, 0] - first_block
    rsrc, ridx = locate(own_pairs[:, 1])
    t_list = [jnp.arange(nloc, dtype=jnp.int32)]
    s_list = [jnp.zeros((nloc,), jnp.int32)]
    i_list = [jnp.arange(nloc, dtype=jnp.int32)]
    v_list = [jnp.ones((nloc,), bool)]
    t_list.append(left); s_list.append(rsrc); i_list.append(ridx); v_list.append(used)
    t_list.append(ridx); s_list.append(jnp.zeros_like(left)); i_list.append(left)
    v_list.append(used & (rsrc == 0))
    for src, pairs, count, prev_first in ((3, pd_pairs, pd_count, first_block - nloc),
                                          (4, pg_pairs, pg_count, first_block - owners * nloc)):
        u = pos < count[0]
        r = pairs[:, 1] - first_block
        u = u & (r >= 0) & (r < nloc)
        t_list.append(r); s_list.append(jnp.full_like(r, src))
        i_list.append(pairs[:, 0] - prev_first); v_list.append(u)
    t = jnp.concatenate(t_list)
    s = jnp.concatenate(s_list)
    ix = jnp.concatenate(i_list)
    v = jnp.concatenate(v_list)
    n = t.shape[0]
    t = jnp.where(v, jnp.clip(t, 0, nloc - 1), nloc)
    ix = jnp.clip(ix, 0, nloc - 1)
    order = jnp.argsort(t * n + jnp.arange(n, dtype=jnp.int32))
    t, s, ix, v = t[order], s[order], ix[order], v[order]
    t = jnp.where(v, t, nloc - 1)
    prev_t = jnp.concatenate([jnp.full((1,), -1, jnp.int32), t[:-1]])
    next_t = jnp.concatenate([t[1:], jnp.full((1,), -1, jnp.int32)])
    next_v = jnp.concatenate([v[1:], jnp.zeros((1,), bool)])
    first = v & (t != prev_t)
    last = v & ((t != next_t) | ~next_v)
    steps = jnp.arange(n, dtype=jnp.int32)
    cols = [t, s, s * nloc + ix, v.astype(jnp.int32), first.astype(jnp.int32),
            last.astype(jnp.int32)]
    for src in range(NSRC):
        active = v & (s == src)
        last_pos = lax.cummax(jnp.where(active, steps, -1))
        first_idx = ix[jnp.argmax(active)]
        cols.append(jnp.where(last_pos >= 0, ix[jnp.maximum(last_pos, 0)], first_idx))
    while len(cols) < NCOL:
        cols.append(jnp.zeros_like(t))
    return jnp.stack(cols, axis=1).reshape(-1).astype(jnp.int32), n


def smooth_kernel(tab, xt_ref, sqc_ref, p0, p1, p2, p3, p4, sqr_ref, out_ref, num_acc, den_acc):
    i = pl.program_id(0)
    base = i * NCOL
    valid = tab[base + C_VALID] == 1
    src = tab[base + C_SRC]
    prow = tab[base + C_PROW]
    width = xt_ref.shape[2]

    @pl.when(tab[base + C_FIRST] == 1)
    def _():
        num_acc[...] = jnp.zeros_like(num_acc)
        den_acc[...] = jnp.zeros_like(den_acc)

    def contribute(p_ref):
        xt = xt_ref[0]
        xp = p_ref[0]
        inner = lax.dot_general(xt, xp, (((1,), (1,)), ((), ())),
                                preferred_element_type=jnp.float32)
        sq_t = sqc_ref[0]
        sq_p = sqr_ref[pl.ds(prow, 1), :]
        distance = sq_t + sq_p - 2.0 * inner
        w = jnp.exp(-distance / (scale_factor * width)).astype(jnp.bfloat16)
        num_acc[...] += jnp.dot(w, xp, preferred_element_type=jnp.float32)
        den_acc[...] += jnp.sum(w.astype(jnp.float32), axis=1, keepdims=True)

    for k, p_ref in enumerate((p0, p1, p2, p3, p4)):
        @pl.when(valid & (src == k))
        def _():
            contribute(p_ref)

    @pl.when(tab[base + C_LAST] == 1)
    def _():
        out_ref[0] = (num_acc[...] / den_acc[...]).astype(out_ref.dtype)


def local(embeddings, pair_blocks, pair_count):
    total_rows, width = embeddings.shape
    nloc = total_rows // BLOCK
    blocks = embeddings.reshape(nloc, BLOCK, width)
    own_sq = squares_of(blocks)
    owners = lax.axis_size("dev")
    first_block = (lax.axis_index("group") * owners + lax.axis_index("dev")) * nloc

    nd = shifted(blocks, "dev", -1)
    ng = shifted(blocks, "group", -1)
    pd = shifted(blocks, "dev", 1)
    pg = shifted(blocks, "group", 1)
    sq_all = jnp.concatenate([own_sq, shifted(own_sq, "dev", -1), shifted(own_sq, "group", -1),
                              shifted(own_sq, "dev", 1), shifted(own_sq, "group", 1)], axis=0)
    pd_pairs = shifted(pair_blocks, "dev", 1)
    pd_count = shifted(pair_count, "dev", 1)
    pg_pairs = shifted(pair_blocks, "group", 1)
    pg_count = shifted(pair_count, "group", 1)

    tab, steps = build_table(pair_blocks, pair_count, pd_pairs, pd_count, pg_pairs, pg_count,
                             first_block, nloc, owners)
    sq_col = own_sq[:, :, None]

    blk = (1, BLOCK, width)

    def t_map(i, tab):
        return (tab[i * NCOL + C_T], 0, 0)

    def src_map(k):
        def m(i, tab):
            return (tab[i * NCOL + C_IDX + k], 0, 0)
        return m

    grid_spec = pltpu.PrefetchScalarGridSpec(
        num_scalar_prefetch=1,
        grid=(steps,),
        in_specs=[pl.BlockSpec(blk, t_map),
                  pl.BlockSpec((1, BLOCK, 1), t_map)]
        + [pl.BlockSpec(blk, src_map(k)) for k in range(NSRC)]
        + [pl.BlockSpec(memory_space=pltpu.VMEM)],
        out_specs=pl.BlockSpec(blk, t_map),
        scratch_shapes=[pltpu.VMEM((BLOCK, width), jnp.float32),
                        pltpu.VMEM((BLOCK, 1), jnp.float32)],
    )
    flops = steps * 4 * BLOCK * BLOCK * width
    smoothed = pl.pallas_call(
        smooth_kernel,
        grid_spec=grid_spec,
        out_shape=jax.ShapeDtypeStruct((nloc, BLOCK, width), jnp.bfloat16),
        compiler_params=pltpu.CompilerParams(dimension_semantics=("arbitrary",)),
        cost_estimate=pl.CostEstimate(flops=flops, transcendentals=steps * BLOCK * BLOCK,
                                      bytes_accessed=steps * BLOCK * width * 2 * 2),
    )(tab, blocks, sq_col, blocks, nd, ng, pd, pg, sq_all)
    return smoothed.reshape(total_rows, width)


def solution(mesh):
    placed = (P(("group", "dev"), None), P(("group", "dev"), None), P(("group", "dev")))
    return jax.shard_map(
        local, mesh=mesh, in_specs=placed, out_specs=P(("group", "dev"), None), check_vma=False
    )
```

time: 444 us -> 185 us (0.42)
  the two profiles are of different devices: /device:TPU:22 before, /device:TPU:80 now
where the time goes in v1:
time: 185 us; the launch traced here: 184 us
  waiting for transfers between devices  54.3 us (29%)
  Pallas kernels  50.3 us (27%)
  starting transfers between devices  37.5 us (20%)
  local copies, waits for them, and re-layouts  16.3 us (9%)
  other arithmetic  14.7 us (8%)
  between operations  10.7 us (6%)
    ppermute x12, waiting for transfers between devices, shifted(): return lax.ppermute(shard, axis, pairs)  54.3 us
    pallas_call x1, Pallas kernels, local(): pl.pallas_call(smooth_kernel, grid_spec=grid_spec, out_shape=jax.ShapeDty...  50.3 us
    ppermute x12, starting transfers between devices, shifted(): return lax.ppermute(shard, axis, pairs)  37.5 us
    gather x10, local copies, waits for them, and re-layouts, build_table(): ix[jnp.maximum(last_pos, 0)]  6.64 us
    gather x5, local copies, waits for them, and re-layouts, build_table(): t, s, ix, v = (t[order], s[order], ix[order], v[order])  5.03 us
  transfers between devices with their start and end apart: 12, of which 3 were waited for; matrix products, arithmetic and copies ran while one was open for 17% of the time, Pallas kernels for 0%

profile of v1, /device:TPU:80, one launch (start us, length us, event | category | flops | bytes accessed | tf_op | source)
XLA Modules:
  0.0 183.8 jit_solution(1437404778125579818)
XLA Ops:
  0.0 3.3 %collective-permute-start.2 = (s32[1]{0:T(128)}, s32[1]{0:T(128)}, u32[]{:S(2)}, u32[]{:S(2)}) collective-permute-start(s32[1]{0:T(128)} %param.5), channel_id=1, source_target_pairs={{0,64},{64,128},{128,192},{1,65},{65,129},{129,193},{2,66},{66,130... | collective-permute-start | bytes 20 | tf_op jit(solution)/shard_map/ppermute | solution.py:19
  3.3 1.9 %collective-permute-start = (s32[1]{0:T(128)}, s32[1]{0:T(128)}, u32[]{:S(2)}, u32[]{:S(2)}) collective-permute-start(s32[1]{0:T(128)} %param.5), channel_id=1, source_target_pairs={{0,1},{1,2},{2,3},{3,4},{4,5},{5,6},{6,7},{7,8},{8,9},{9,10},{10,1... | collective-permute-start | bytes 20 | tf_op jit(solution)/shard_map/ppermute | solution.py:19
  5.3 3.5 %collective-permute-start.1 = (s32[16,2]{0,1:T(2,128)}, s32[16,2]{0,1:T(2,128)S(1)}, u32[]{:S(2)}, u32[]{:S(2)}) collective-permute-start(s32[16,2]{0,1:T(2,128)} %param.4), channel_id=1, source_target_pairs={{0,1},{1,2},{2,3},{3,4},{4,5},{5,6},{6,7},{7,8},{8,9},{9,10},{10,1... | collective-permute-start | bytes 392 | tf_op jit(solution)/shard_map/ppermute | solution.py:19
  8.8 1.9 %collective-permute-start.3 = (s32[16,2]{0,1:T(2,128)}, s32[16,2]{0,1:T(2,128)S(1)}, u32[]{:S(2)}, u32[]{:S(2)}) collective-permute-start(s32[16,2]{0,1:T(2,128)} %param.4), channel_id=1, source_target_pairs={{0,64},{64,128},{128,192},{1,65},{65,129},{129,193},{2,66},{66,130... | collective-permute-start | bytes 392 | tf_op jit(solution)/shard_map/ppermute | solution.py:19
  10.7 3.1 %fusion = f32[8,256]{1,0:T(8,128)S(1)} fusion(bf16[8,256,1024]{2,1,0:T(8,128)(2,1)} %bitcast.64), kind=kLoop, calls=%fused_computation.10 | loop fusion | flops 6289408 | bytes 4202496 | tf_op jit(solution)/shard_map/bsd,bsd->bs/dot_general | solution.py:23
  13.8 4.2 %collective-permute-start.8 = (f32[8,256]{1,0:T(8,128)S(1)}, f32[8,256]{1,0:T(8,128)S(1)}, u32[]{:S(2)}, u32[]{:S(2)}) collective-permute-start(f32[8,256]{1,0:T(8,128)S(1)} %fusion), channel_id=1, source_target_pairs={{1,0},{2,1},{3,2},{4,3},{5,4},{6,5},{7,6},{8,7},{9,8},{10,9},{11,1... | collective-permute-start | bytes 24584 | tf_op jit(solution)/shard_map/ppermute | solution.py:19
  18.7 1.4 copy.92.sqc_ref
  20.1 1.9 %collective-permute-start.7 = (bf16[8,256,1024]{2,1,0:T(8,128)(2,1)}, bf16[8,256,1024]{2,1,0:T(8,128)(2,1)}, u32[]{:S(2)}, u32[]{:S(2)}) collective-permute-start(bf16[8,256,1024]{2,1,0:T(8,128)(2,1)} %bitcast.65), channel_id=1, source_target_pairs={{0,64},{64,128},{128,192},{1,65},{65,129},{129,193},{2,66},{66,130... | collective-permute-start | bytes 12582920 | tf_op jit(solution)/shard_map/ppermute | solution.py:19
  22.1 1.9 %collective-permute-start.6 = (bf16[8,256,1024]{2,1,0:T(8,128)(2,1)}, bf16[8,256,1024]{2,1,0:T(8,128)(2,1)}, u32[]{:S(2)}, u32[]{:S(2)}) collective-permute-start(bf16[8,256,1024]{2,1,0:T(8,128)(2,1)} %bitcast.66), channel_id=1, source_target_pairs={{0,1},{1,2},{2,3},{3,4},{4,5},{5,6},{6,7},{7,8},{8,9},{9,10},{10,1... | collective-permute-start | bytes 12582920 | tf_op jit(solution)/shard_map/ppermute | solution.py:19
  24.0 0.6 compare_and_fusion.1
  24.6 3.9 %collective-permute-start.5 = (bf16[8,256,1024]{2,1,0:T(8,128)(2,1)}, bf16[8,256,1024]{2,1,0:T(8,128)(2,1)}, u32[]{:S(2)}, u32[]{:S(2)}) collective-permute-start(bf16[8,256,1024]{2,1,0:T(8,128)(2,1)} %bitcast.67), channel_id=1, source_target_pairs={{64,0},{128,64},{192,128},{65,1},{129,65},{193,129},{66,2},{130,66... | collective-permute-start | bytes 12582920 | tf_op jit(solution)/shard_map/ppermute | solution.py:19
  28.5 5.5 %collective-permute-start.4 = (bf16[8,256,1024]{2,1,0:T(8,128)(2,1)}, bf16[8,256,1024]{2,1,0:T(8,128)(2,1)}, u32[]{:S(2)}, u32[]{:S(2)}) collective-permute-start(bf16[8,256,1024]{2,1,0:T(8,128)(2,1)} %bitcast.68), channel_id=1, source_target_pairs={{1,0},{2,1},{3,2},{4,3},{5,4},{6,5},{7,6},{8,7},{9,8},{10,9},{11,1... | collective-permute-start | bytes 12582920 | tf_op jit(solution)/shard_map/ppermute | solution.py:19
  34.0 0.6 compare_and_fusion
  34.7 0.1 concatenate.51
  34.8 2.5 %sort.17 = (s32[72]{0:T(128)}, s32[72]{0:T(128)S(1)}) sort(s32[72]{0:T(128)S(1)} %get-tuple-element.17, s32[72]{0:T(128)S(1)} %iota.57), dimensions={0}, to_apply=%region_0.1 | sort | flops 504 | bytes 1152 | tf_op jit(solution)/shard_map/jit(argsort)/sort | solution.py:62
  37.4 1.2 gather_fusion
  38.6 1.2 gather_fusion.2
  39.8 0.7 and_reduce_fusion.1
  40.6 0.7 and_reduce_fusion.2
  41.3 0.7 and_reduce_fusion.3
  41.9 0.7 and_reduce_fusion.4
  42.7 0.7 and_reduce_fusion
  43.4 0.1 copy.72
  43.5 0.1 copy.87
  43.7 0.1 reduce-window.24
  43.8 0.1 maximum_reduce_fusion
  50.3 1.2 gather_fusion.3
  51.5 1.2 gather_fusion.1
  52.8 1.2 gather_fusion.8
  54.0 0.1 copy.85
  54.1 0.1 reduce-window.21
  54.2 0.1 maximum_reduce_fusion.1
  54.3 1.2 gather_fusion.7
  55.5 0.1 copy.82
  55.6 0.1 reduce-window.20
  55.8 0.1 maximum_reduce_fusion.2
  55.9 1.2 gather_fusion.6
  57.1 0.1 copy.79
  57.2 0.1 reduce-window.19
  57.3 0.1 reduce-window.16
  57.4 0.1 maximum_reduce_fusion.3
  57.5 1.2 gather_fusion.5
  58.8 0.1 maximum_reduce_fusion.4
  58.9 1.2 gather_fusion.4
  60.1 0.1 copy.73
  60.2 0.1 copy.76
  63.5 0.7 fusion.4
  64.5 0.7 compare_select_fusion
  65.1 0.6 compare_select_fusion.1
  65.7 0.7 compare_select_fusion.2
  66.4 0.6 compare_select_fusion.4
  67.0 0.6 compare_select_fusion.3
  67.7 0.1 copy.91
  67.8 0.1 copy.89
  68.2 0.2 stack.8
  68.4 0.7 reshape.372.tab
  69.1 5.6 %collective-permute-start.9 = (f32[8,256]{1,0:T(8,128)S(1)}, f32[8,256]{1,0:T(8,128)S(1)}, u32[]{:S(2)}, u32[]{:S(2)}) collective-permute-start(f32[8,256]{1,0:T(8,128)S(1)} %fusion), channel_id=1, source_target_pairs={{64,0},{128,64},{192,128},{65,1},{129,65},{193,129},{66,2},{130,66... | collective-permute-start | bytes 24584 | tf_op jit(solution)/shard_map/ppermute | solution.py:19
  74.7 44.2 %collective-permute-done.9 = f32[8,256]{1,0:T(8,128)S(1)} collective-permute-done((f32[8,256]{1,0:T(8,128)S(1)}, f32[8,256]{1,0:T(8,128)S(1)}, u32[]{:S(2)}, u32[]{:S(2)}) %collective-permute-start.9) | collective-permute-done | bytes 8224 | tf_op jit(solution)/shard_map/ppermute | solution.py:19
  118.8 1.9 %collective-permute-start.10 = (f32[8,256]{1,0:T(8,128)S(1)}, f32[8,256]{1,0:T(8,128)S(1)}, u32[]{:S(2)}, u32[]{:S(2)}) collective-permute-start(f32[8,256]{1,0:T(8,128)S(1)} %fusion), channel_id=1, source_target_pairs={{0,1},{1,2},{2,3},{3,4},{4,5},{5,6},{6,7},{7,8},{8,9},{9,10},{10,1... | collective-permute-start | bytes 24584 | tf_op jit(solution)/shard_map/ppermute | solution.py:19
  120.8 5.1 %collective-permute-done.10 = f32[8,256]{1,0:T(8,128)S(1)} collective-permute-done((f32[8,256]{1,0:T(8,128)S(1)}, f32[8,256]{1,0:T(8,128)S(1)}, u32[]{:S(2)}, u32[]{:S(2)}) %collective-permute-start.10) | collective-permute-done | bytes 8224 | tf_op jit(solution)/shard_map/ppermute | solution.py:19
  125.9 1.9 %collective-permute-start.11 = (f32[8,256]{1,0:T(8,128)S(1)}, f32[8,256]{1,0:T(8,128)S(1)}, u32[]{:S(2)}, u32[]{:S(2)}) collective-permute-start(f32[8,256]{1,0:T(8,128)S(1)} %fusion), channel_id=1, source_target_pairs={{0,64},{64,128},{128,192},{1,65},{65,129},{129,193},{2,66},{66,130... | collective-permute-start | bytes 24584 | tf_op jit(solution)/shard_map/ppermute | solution.py:19
  127.8 4.9 %collective-permute-done.11 = f32[8,256]{1,0:T(8,128)S(1)} collective-permute-done((f32[8,256]{1,0:T(8,128)S(1)}, f32[8,256]{1,0:T(8,128)S(1)}, u32[]{:S(2)}, u32[]{:S(2)}) %collective-permute-start.11) | collective-permute-done | bytes 8224 | tf_op jit(solution)/shard_map/ppermute | solution.py:19
  132.8 0.6 copy-done
  133.4 50.3 %shard_map.37 = bf16[8,256,1024]{2,1,0:T(8,128)(2,1)} custom-call(s32[1152]{0:T(1024)} %reshape.372.tab, bf16[8,256,1024]{2,1,0:T(8,128)(2,1)} %bitcast.69, f32[8,256,1]{2,1,0:T(8,128)} %copy.92.sqc_ref, bf16[8,256,1024]{2,1,0:T(8,128)(2,1)} %bitcast.70, bf16[8,256,1024]{2,1,0:T(8,128)(2,1)} %collective-permute-done.4.p1, ...), custom_call_target="tpu_custom_call" | custom-call | flops 19327352832 | bytes 75497472 | tf_op jit(solution)/shard_map/pallas_call | solution.py:163
  (55 shorter events, 1.0 us)
Async XLA Ops:
  0.0 18.6 %copy-start.1 = (s32[16,2]{0,1:T(2,128)S(1)}, s32[16,2]{0,1:T(2,128)}, u32[]{:S(2)}) copy-start(s32[16,2]{0,1:T(2,128)} %param.4) | copy-start | bytes 388
  0.0 24.6 %collective-permute-start.2 = (s32[1]{0:T(128)}, s32[1]{0:T(128)}, u32[]{:S(2)}, u32[]{:S(2)}) collective-permute-start(s32[1]{0:T(128)} %param.5), channel_id=1, source_target_pairs={{0,64},{64,128},{128,192},{1,65},{65,129},{129,193},{2,66},{66,130... | collective-permute-start | bytes 20 | tf_op jit(solution)/shard_map/ppermute | solution.py:19
  3.3 16.8 %collective-permute-start = (s32[1]{0:T(128)}, s32[1]{0:T(128)}, u32[]{:S(2)}, u32[]{:S(2)}) collective-permute-start(s32[1]{0:T(128)} %param.5), channel_id=1, source_target_pairs={{0,1},{1,2},{2,3},{3,4},{4,5},{5,6},{6,7},{7,8},{8,9},{9,10},{10,1... | collective-permute-start | bytes 20 | tf_op jit(solution)/shard_map/ppermute | solution.py:19
  5.3 16.8 %collective-permute-start.1 = (s32[16,2]{0,1:T(2,128)}, s32[16,2]{0,1:T(2,128)S(1)}, u32[]{:S(2)}, u32[]{:S(2)}) collective-permute-start(s32[16,2]{0,1:T(2,128)} %param.4), channel_id=1, source_target_pairs={{0,1},{1,2},{2,3},{3,4},{4,5},{5,6},{6,7},{7,8},{8,9},{9,10},{10,1... | collective-permute-start | bytes 392 | tf_op jit(solution)/shard_map/ppermute | solution.py:19
  8.8 19.8 %collective-permute-start.3 = (s32[16,2]{0,1:T(2,128)}, s32[16,2]{0,1:T(2,128)S(1)}, u32[]{:S(2)}, u32[]{:S(2)}) collective-permute-start(s32[16,2]{0,1:T(2,128)} %param.4), channel_id=1, source_target_pairs={{0,64},{64,128},{128,192},{1,65},{65,129},{129,193},{2,66},{66,130... | collective-permute-start | bytes 392 | tf_op jit(solution)/shard_map/ppermute | solution.py:19
  13.8 55.3 %collective-permute-start.8 = (f32[8,256]{1,0:T(8,128)S(1)}, f32[8,256]{1,0:T(8,128)S(1)}, u32[]{:S(2)}, u32[]{:S(2)}) collective-permute-start(f32[8,256]{1,0:T(8,128)S(1)} %fusion), channel_id=1, source_target_pairs={{1,0},{2,1},{3,2},{4,3},{5,4},{6,5},{7,6},{8,7},{9,8},{10,9},{11,1... | collective-permute-start | bytes 24584 | tf_op jit(solution)/shard_map/ppermute | solution.py:19
  20.1 112.7 %collective-permute-start.7 = (bf16[8,256,1024]{2,1,0:T(8,128)(2,1)}, bf16[8,256,1024]{2,1,0:T(8,128)(2,1)}, u32[]{:S(2)}, u32[]{:S(2)}) collective-permute-start(bf16[8,256,1024]{2,1,0:T(8,128)(2,1)} %bitcast.65), channel_id=1, source_target_pairs={{0,64},{64,128},{128,192},{1,65},{65,129},{129,193},{2,66},{66,130... | collective-permute-start | bytes 12582920 | tf_op jit(solution)/shard_map/ppermute | solution.py:19
  22.1 110.7 %collective-permute-start.6 = (bf16[8,256,1024]{2,1,0:T(8,128)(2,1)}, bf16[8,256,1024]{2,1,0:T(8,128)(2,1)}, u32[]{:S(2)}, u32[]{:S(2)}) collective-permute-start(bf16[8,256,1024]{2,1,0:T(8,128)(2,1)} %bitcast.66), channel_id=1, source_target_pairs={{0,1},{1,2},{2,3},{3,4},{4,5},{5,6},{6,7},{7,8},{8,9},{9,10},{10,1... | collective-permute-start | bytes 12582920 | tf_op jit(solution)/shard_map/ppermute | solution.py:19
  24.6 108.2 %collective-permute-start.5 = (bf16[8,256,1024]{2,1,0:T(8,128)(2,1)}, bf16[8,256,1024]{2,1,0:T(8,128)(2,1)}, u32[]{:S(2)}, u32[]{:S(2)}) collective-permute-start(bf16[8,256,1024]{2,1,0:T(8,128)(2,1)} %bitcast.67), channel_id=1, source_target_pairs={{64,0},{128,64},{192,128},{65,1},{129,65},{193,129},{66,2},{130,66... | collective-permute-start | bytes 12582920 | tf_op jit(solution)/shard_map/ppermute | solution.py:19
  28.5 104.3 %collective-permute-start.4 = (bf16[8,256,1024]{2,1,0:T(8,128)(2,1)}, bf16[8,256,1024]{2,1,0:T(8,128)(2,1)}, u32[]{:S(2)}, u32[]{:S(2)}) collective-permute-start(bf16[8,256,1024]{2,1,0:T(8,128)(2,1)} %bitcast.68), channel_id=1, source_target_pairs={{1,0},{2,1},{3,2},{4,3},{5,4},{6,5},{7,6},{8,7},{9,8},{10,9},{11,1... | collective-permute-start | bytes 12582920 | tf_op jit(solution)/shard_map/ppermute | solution.py:19
  69.1 49.8 %collective-permute-start.9 = (f32[8,256]{1,0:T(8,128)S(1)}, f32[8,256]{1,0:T(8,128)S(1)}, u32[]{:S(2)}, u32[]{:S(2)}) collective-permute-start(f32[8,256]{1,0:T(8,128)S(1)} %fusion), channel_id=1, source_target_pairs={{64,0},{128,64},{192,128},{65,1},{129,65},{193,129},{66,2},{130,66... | collective-permute-start | bytes 24584 | tf_op jit(solution)/shard_map/ppermute | solution.py:19
  118.8 7.1 %collective-permute-start.10 = (f32[8,256]{1,0:T(8,128)S(1)}, f32[8,256]{1,0:T(8,128)S(1)}, u32[]{:S(2)}, u32[]{:S(2)}) collective-permute-start(f32[8,256]{1,0:T(8,128)S(1)} %fusion), channel_id=1, source_target_pairs={{0,1},{1,2},{2,3},{3,4},{4,5},{5,6},{6,7},{7,8},{8,9},{9,10},{10,1... | collective-permute-start | bytes 24584 | tf_op jit(solution)/shard_map/ppermute | solution.py:19
  125.9 6.9 %collective-permute-start.11 = (f32[8,256]{1,0:T(8,128)S(1)}, f32[8,256]{1,0:T(8,128)S(1)}, u32[]{:S(2)}, u32[]{:S(2)}) collective-permute-start(f32[8,256]{1,0:T(8,128)S(1)} %fusion), channel_id=1, source_target_pairs={{0,64},{64,128},{128,192},{1,65},{65,129},{129,193},{2,66},{66,130... | collective-permute-start | bytes 24584 | tf_op jit(solution)/shard_map/ppermute | solution.py:19
  132.8 0.6 copy-start

commit v2 on v0

v2 whole, which is shorter than its diff:
```python
import jax
import jax.numpy as jnp
from jax import lax
from jax.experimental import pallas as pl
from jax.experimental.pallas import tpu as pltpu
from jax.sharding import PartitionSpec as P

BLOCK = 256
scale_factor = 0.4

C_T, C_SRC, C_PROW, C_COMP, C_FIRST, C_LAST, C_IDX = 0, 1, 2, 3, 4, 5, 6
NCOL = 8


def shifted(shard, axis, by):
    devices = lax.axis_size(axis)
    pairs = [(i, i + by) for i in range(devices) if 0 <= i + by < devices]
    return lax.ppermute(shard, axis, pairs)


def squares_of(blocks):
    return jnp.einsum("bsd,bsd->bs", blocks, blocks, preferred_element_type=jnp.float32)


def order_table(t, s, ix, comp, valid, nloc, nsrc):
    n = t.shape[0]
    key = jnp.where(valid, jnp.clip(t, 0, nloc - 1), nloc)
    order = jnp.argsort(key * n + jnp.arange(n, dtype=jnp.int32))
    t, s, ix, comp, valid = t[order], s[order], ix[order], comp[order], valid[order]
    t = jnp.where(valid, jnp.clip(t, 0, nloc - 1), nloc - 1)
    ix = jnp.clip(ix, 0, nloc - 1)
    comp = comp & valid
    prev_t = jnp.concatenate([jnp.full((1,), -1, jnp.int32), t[:-1]])
    next_t = jnp.concatenate([t[1:], jnp.full((1,), -1, jnp.int32)])
    next_v = jnp.concatenate([valid[1:], jnp.zeros((1,), bool)])
    first = valid & (t != prev_t)
    last = valid & ((t != next_t) | ~next_v)
    steps = jnp.arange(n, dtype=jnp.int32)
    s = jnp.clip(s, 0, nsrc - 1)
    cols = [t, s, s * nloc + ix, comp.astype(jnp.int32), first.astype(jnp.int32),
            last.astype(jnp.int32)]
    for src in range(nsrc):
        active = comp & (s == src)
        last_pos = lax.cummax(jnp.where(active, steps, -1))
        first_idx = ix[jnp.argmax(active)]
        cols.append(jnp.where(last_pos >= 0, ix[jnp.maximum(last_pos, 0)], first_idx))
    while len(cols) < NCOL:
        cols.append(jnp.zeros_like(t))
    return jnp.stack(cols, axis=1).reshape(-1).astype(jnp.int32), n


def make_kernel(nsrc, mode):
    def kernel(tab, *refs):
        if mode == "init":
            xt_ref, sqc_ref = refs[:2]
            p_refs = refs[2:2 + nsrc]
            sqr_ref = refs[2 + nsrc]
            num_out, den_out, num_acc, den_acc = refs[3 + nsrc:]
        else:
            xt_ref, sqc_ref = refs[:2]
            p_refs = refs[2:2 + nsrc]
            sqr_ref, num_in, den_in = refs[2 + nsrc:5 + nsrc]
            outs = refs[5 + nsrc:]
            num_acc, den_acc = outs[-2:]
        i = pl.program_id(0)
        base = i * NCOL
        comp = tab[base + C_COMP] == 1
        src = tab[base + C_SRC]
        prow = tab[base + C_PROW]
        width = xt_ref.shape[2]

        @pl.when(tab[base + C_FIRST] == 1)
        def _():
            if mode == "init":
                num_acc[...] = jnp.zeros_like(num_acc)
                den_acc[...] = jnp.zeros_like(den_acc)
            else:
                num_acc[...] = num_in[0]
                den_acc[...] = den_in[0]

        def contribute(p_ref):
            xt = xt_ref[0]
            xp = p_ref[0]
            inner = lax.dot_general(xt, xp, (((1,), (1,)), ((), ())),
                                    preferred_element_type=jnp.float32)
            sq_t = sqc_ref[0]
            sq_p = sqr_ref[pl.ds(prow, 1), :]
            distance = sq_t + sq_p - 2.0 * inner
            w = jnp.exp(-distance / (scale_factor * width)).astype(jnp.bfloat16)
            num_acc[...] += jnp.dot(w, xp, preferred_element_type=jnp.float32)
            den_acc[...] += jnp.sum(w.astype(jnp.float32), axis=1, keepdims=True)

        for k, p_ref in enumerate(p_refs):
            @pl.when(comp & (src == k))
            def _():
                contribute(p_ref)

        @pl.when(tab[base + C_LAST] == 1)
        def _():
            if mode == "final":
                outs[0][0] = (num_acc[...] / den_acc[...]).astype(outs[0].dtype)
            else:
                num_out = outs[0] if mode != "init" else refs[3 + nsrc]
                den_out = outs[1] if mode != "init" else refs[4 + nsrc]
                num_out[0] = num_acc[...]
                den_out[0] = den_acc[...]

    return kernel


def run_phase(mode, tab, steps, own, sq_col, sources, sq_rows, num=None, den=None):
    nloc, block, width = own.shape
    nsrc = len(sources)
    blk = (1, block, width)
    cblk = (1, block, 1)

    def t_map(i, tab):
        return (tab[i * NCOL + C_T], 0, 0)

    def src_map(k):
        def m(i, tab):
            return (tab[i * NCOL + C_IDX + k], 0, 0)
        return m

    in_specs = ([pl.BlockSpec(blk, t_map), pl.BlockSpec(cblk, t_map)]
                + [pl.BlockSpec(blk, src_map(k)) for k in range(nsrc)]
                + [pl.BlockSpec(memory_space=pltpu.VMEM)])
    args = [tab, own, sq_col, *sources, sq_rows]
    aliases = {}
    if mode != "init":
        in_specs += [pl.BlockSpec(blk, t_map), pl.BlockSpec(cblk, t_map)]
        args += [num, den]
    if mode == "final":
        out_specs = pl.BlockSpec(blk, t_map)
        out_shape = jax.ShapeDtypeStruct((nloc, block, width), jnp.bfloat16)
    else:
        out_specs = [pl.BlockSpec(blk, t_map), pl.BlockSpec(cblk, t_map)]
        out_shape = [jax.ShapeDtypeStruct((nloc, block, width), jnp.float32),
                     jax.ShapeDtypeStruct((nloc, block, 1), jnp.float32)]
        if mode == "accum":
            aliases = {len(args) - 2: 0, len(args) - 1: 1}
    grid_spec = pltpu.PrefetchScalarGridSpec(
        num_scalar_prefetch=1,
        grid=(steps,),
        in_specs=in_specs,
        out_specs=out_specs,
        scratch_shapes=[pltpu.VMEM((block, width), jnp.float32),
                        pltpu.VMEM((block, 1), jnp.float32)],
    )
    flops = steps * 4 * block * block * width
    return pl.pallas_call(
        make_kernel(nsrc, mode),
        grid_spec=grid_spec,
        out_shape=out_shape,
        input_output_aliases=aliases,
        compiler_params=pltpu.CompilerParams(dimension_semantics=("arbitrary",)),
        cost_estimate=pl.CostEstimate(flops=flops, transcendentals=steps * block * block,
                                      bytes_accessed=steps * block * width * 2 * 2),
    )(*args)


def local(embeddings, pair_blocks, pair_count):
    total_rows, width = embeddings.shape
    nloc = total_rows // BLOCK
    slots = pair_blocks.shape[0]
    blocks = embeddings.reshape(nloc, BLOCK, width)
    owners = lax.axis_size("dev")
    first_block = (lax.axis_index("group") * owners + lax.axis_index("dev")) * nloc

    nd = shifted(blocks, "dev", -1)
    pd = shifted(blocks, "dev", 1)
    ng = shifted(blocks, "group", -1)
    pg = shifted(blocks, "group", 1)

    own_sq = squares_of(blocks)
    meta = jnp.concatenate([own_sq.reshape(-1),
                            pair_blocks.reshape(-1).astype(jnp.float32),
                            pair_count.astype(jnp.float32)])
    nsq = nloc * BLOCK
    m_nd = shifted(meta, "dev", -1)
    m_pd = shifted(meta, "dev", 1)
    m_ng = shifted(meta, "group", -1)
    m_pg = shifted(meta, "group", 1)

    def sq_of(m):
        return m[:nsq].reshape(nloc, BLOCK)

    def pairs_of(m):
        return (m[nsq:nsq + 2 * slots].astype(jnp.int32).reshape(slots, 2),
                m[nsq + 2 * slots:].astype(jnp.int32))

    pos = jnp.arange(slots, dtype=jnp.int32)
    used = pos < pair_count[0]
    left = jnp.clip(pair_blocks[:, 0] - first_block, 0, nloc - 1)
    right = pair_blocks[:, 1]
    roff = right - first_block
    r_local = roff < nloc
    r_dev = (roff >= nloc) & (roff < 2 * nloc)
    r_grp = ~r_local & ~r_dev
    ridx_dev = roff - nloc
    ridx_grp = right - first_block - owners * nloc
    zeros = jnp.zeros((slots,), jnp.int32)
    sq_col = own_sq[:, :, None]

    diag = jnp.arange(nloc, dtype=jnp.int32)
    t1 = jnp.concatenate([diag, left, roff])
    i1 = jnp.concatenate([diag, roff, left])
    v1 = jnp.concatenate([jnp.ones((nloc,), bool), used & r_local, used & r_local])
    z1 = jnp.zeros_like(t1)
    tab1, n1 = order_table(t1, z1, i1, v1, v1, nloc, 1)
    num, den = run_phase("init", tab1, n1, blocks, sq_col, [blocks], own_sq)

    def prev_entries(m, prev_first, src):
        pairs, count = pairs_of(m)
        u = pos < count[0]
        r = pairs[:, 1] - first_block
        u = u & (r >= 0) & (r < nloc)
        return r, jnp.full((slots,), src, jnp.int32), pairs[:, 0] - prev_first, u

    pr, ps, pi, pu = prev_entries(m_pd, first_block - nloc, 1)
    t2 = jnp.concatenate([diag, left, pr])
    s2 = jnp.concatenate([jnp.zeros((nloc,), jnp.int32), zeros, ps])
    i2 = jnp.concatenate([diag, ridx_dev, pi])
    c2 = jnp.concatenate([jnp.zeros((nloc,), bool), used & r_dev, pu])
    v2 = jnp.concatenate([jnp.ones((nloc,), bool), used & r_dev, pu])
    tab2, n2 = order_table(t2, s2, i2, c2, v2, nloc, 2)
    sq2 = jnp.concatenate([sq_of(m_nd), sq_of(m_pd)], axis=0)
    num, den = run_phase("accum", tab2, n2, blocks, sq_col, [nd, pd], sq2, num, den)

    gr, gs, gi, gu = prev_entries(m_pg, first_block - owners * nloc, 1)
    t3 = jnp.concatenate([diag, left, gr])
    s3 = jnp.concatenate([jnp.zeros((nloc,), jnp.int32), zeros, gs])
    i3 = jnp.concatenate([diag, ridx_grp, gi])
    c3 = jnp.concatenate([jnp.zeros((nloc,), bool), used & r_grp, gu])
    v3 = jnp.concatenate([jnp.ones((nloc,), bool), used & r_grp, gu])
    tab3, n3 = order_table(t3, s3, i3, c3, v3, nloc, 2)
    sq3 = jnp.concatenate([sq_of(m_ng), sq_of(m_pg)], axis=0)
    smoothed = run_phase("final", tab3, n3, blocks, sq_col, [ng, pg], sq3, num, den)
    return smoothed.reshape(total_rows, width)


def solution(mesh):
    placed = (P(("group", "dev"), None), P(("group", "dev"), None), P(("group", "dev")))
    return jax.shard_map(
        local, mesh=mesh, in_specs=placed, out_specs=P(("group", "dev"), None), check_vma=False
    )
```

time: 444 us -> 200 us (0.45)
  the two profiles are of different devices: /device:TPU:22 before, /device:TPU:247 now
where the time goes in v2:
time: 200 us; the launch traced here: 198 us
  Pallas kernels  83.1 us (42%)
  waiting for transfers between devices  36.9 us (18%)
  local copies, waits for them, and re-layouts  23.7 us (12%)
  starting transfers between devices  23.7 us (12%)
  other arithmetic  18.7 us (9%)
  between operations  12.2 us (6%)
    pallas_call x3, Pallas kernels, run_phase(): pl.pallas_call(make_kernel(nsrc, mode), grid_spec=grid_spec, out_shape=ou...  83.1 us
    ppermute x8, waiting for transfers between devices, shifted(): return lax.ppermute(shard, axis, pairs)  36.9 us
    ppermute x8, starting transfers between devices, shifted(): return lax.ppermute(shard, axis, pairs)  23.7 us
    sort x3, other arithmetic, order_table(): order = jnp.argsort(key * n + jnp.arange(n, dtype=jnp.int32))  6.12 us
  transfers between devices with their start and end apart: 8, of which 1 were waited for; matrix products, arithmetic and copies ran while one was open for 20% of the time, Pallas kernels for 24%

profile of v2, /device:TPU:247, one launch (start us, length us, event | category | flops | bytes accessed | tf_op | source)
XLA Modules:
  0.0 198.2 jit_solution(5135814508670104007)
XLA Ops:
  0.0 3.1 %fusion.refs_3_ = f32[8,256]{1,0:T(8,128)S(1)} fusion(bf16[8,256,1024]{2,1,0:T(8,128)(2,1)} %bitcast.169), kind=kLoop, calls=%fused_computation.20 | loop fusion | flops 6289408 | bytes 4202496 | tf_op jit(solution)/shard_map/bsd,bsd->bs/dot_general | solution.py:22
  3.9 0.1 convert_element_type.120
  4.1 2.9 %collective-permute-start = (f32[2081]{0:T(1024)S(1)}, f32[2081]{0:T(1024)S(1)}, u32[]{:S(2)}, u32[]{:S(2)}) collective-permute-start(f32[2081]{0:T(1024)S(1)} %concatenate.150), channel_id=1, source_target_pairs={{0,64},{64,128},{128,192},{1,65},{65,129},{129,193},{2,66},{66,130... | collective-permute-start | bytes 24980 | tf_op jit(solution)/shard_map/ppermute | solution.py:18
  7.0 1.3 collective-permute-start.4
  8.3 3.5 %collective-permute-start.7 = (f32[2081]{0:T(1024)S(1)}, f32[2081]{0:T(1024)S(1)}, u32[]{:S(2)}, u32[]{:S(2)}) collective-permute-start(f32[2081]{0:T(1024)S(1)} %concatenate.150), channel_id=1, source_target_pairs={{1,0},{2,1},{3,2},{4,3},{5,4},{6,5},{7,6},{8,7},{9,8},{10,9},{11,1... | collective-permute-start | bytes 24980 | tf_op jit(solution)/shard_map/ppermute | solution.py:18
  11.8 5.6 %collective-permute-start.5 = (bf16[8,256,1024]{2,1,0:T(8,128)(2,1)}, bf16[8,256,1024]{2,1,0:T(8,128)(2,1)}, u32[]{:S(2)}, u32[]{:S(2)}) collective-permute-start(bf16[8,256,1024]{2,1,0:T(8,128)(2,1)} %bitcast.170), channel_id=1, source_target_pairs={{1,0},{2,1},{3,2},{4,3},{5,4},{6,5},{7,6},{8,7},{9,8},{10,9},{11,1... | collective-permute-start | bytes 12582920 | tf_op jit(solution)/shard_map/ppermute | solution.py:18
  17.3 1.3 collective-permute-start.6
  18.8 0.1 clamp_reduce_fusion
  19.0 1.4 copy.221.refs_1_
  20.4 2.4 %collective-permute-start.1 = (bf16[8,256,1024]{2,1,0:T(8,128)(2,1)}, bf16[8,256,1024]{2,1,0:T(8,128)(2,1)}, u32[]{:S(2)}, u32[]{:S(2)}) collective-permute-start(bf16[8,256,1024]{2,1,0:T(8,128)(2,1)} %bitcast.172), channel_id=1, source_target_pairs={{64,0},{128,64},{192,128},{65,1},{129,65},{193,129},{66,2},{130,66... | collective-permute-start | bytes 12582920 | tf_op jit(solution)/shard_map/ppermute | solution.py:18
  22.9 4.9 %collective-permute-start.2 = (bf16[8,256,1024]{2,1,0:T(8,128)(2,1)}, bf16[8,256,1024]{2,1,0:T(8,128)(2,1)}, u32[]{:S(2)}, u32[]{:S(2)}) collective-permute-start(bf16[8,256,1024]{2,1,0:T(8,128)(2,1)} %bitcast.173), channel_id=1, source_target_pairs={{0,64},{64,128},{128,192},{1,65},{65,129},{129,193},{2,66},{66,130... | collective-permute-start | bytes 12582920 | tf_op jit(solution)/shard_map/ppermute | solution.py:18
  27.9 0.6 slice.136
  29.1 0.2 fusion.1
  29.5 2.0 %sort.47 = (s32[40]{0:T(128)}, s32[40]{0:T(128)S(1)}) sort(s32[40]{0:T(128)S(1)} %get-tuple-element.33, s32[40]{0:T(128)S(1)} %iota.94), dimensions={0}, to_apply=%region_10.11 | sort | flops 240 | bytes 640 | tf_op jit(solution)/shard_map/jit(argsort)/sort | solution.py:28
  31.5 0.8 gather_fusion.14
  32.3 0.8 gather_fusion.16
  33.1 0.8 gather_fusion.17
  33.9 0.8 gather_fusion.15
  34.6 0.7 and_reduce_fusion
  35.5 2.0 %sort.46 = (s32[40]{0:T(128)}, s32[40]{0:T(128)S(1)}) sort(s32[40]{0:T(128)S(1)} %get-tuple-element.43, s32[40]{0:T(128)S(1)} %iota.86), dimensions={0}, to_apply=%region_5.6 | sort | flops 240 | bytes 640 | tf_op jit(solution)/shard_map/jit(argsort)/sort | solution.py:28
  37.5 0.6 slice.130
  38.8 0.8 gather_fusion.7
  39.7 0.8 gather_fusion.11
  40.4 0.8 gather_fusion.9
  41.2 0.7 and_reduce_fusion.2
  41.9 0.7 and_reduce_fusion.1
  42.7 0.8 gather_fusion.10
  43.5 0.8 gather_fusion.8
  44.4 2.0 %sort.45 = (s32[40]{0:T(128)}, s32[40]{0:T(128)S(1)}) sort(s32[40]{0:T(128)S(1)} %get-tuple-element.78, s32[40]{0:T(128)S(1)} %iota.77), dimensions={0}, to_apply=%region_0.1 | sort | flops 240 | bytes 640 | tf_op jit(solution)/shard_map/jit(argsort)/sort | solution.py:28
  46.4 0.8 gather_fusion.2
  47.2 0.8 gather_fusion.4
  48.0 0.8 gather_fusion
  48.8 0.7 and_reduce_fusion.4
  49.5 0.7 and_reduce_fusion.3
  50.2 0.8 gather_fusion.3
  51.0 0.8 gather_fusion.1
  51.8 0.1 copy.215
  52.1 0.1 copy.211
  52.4 0.1 copy.208
  52.6 0.1 copy.204
  52.9 0.1 copy.201
  60.4 0.7 dynamic_slice.19
  61.0 0.8 gather_fusion.18
  61.8 0.8 gather_fusion.13
  62.6 0.8 gather_fusion.12
  63.4 0.8 gather_fusion.6
  64.2 0.8 gather_fusion.5
  67.5 0.7 fusion.36
  68.2 0.6 fusion.37
  69.0 0.7 compare_select_fusion.3
  69.7 0.7 compare_select_fusion.4
  70.4 0.6 compare_select_fusion.5
  71.1 0.7 compare_select_fusion.6
  71.7 0.6 compare_select_fusion.7
  72.6 1.9 collective-permute-start.3
  74.7 0.7 reshape.797.tab
  75.5 0.7 reshape.794.tab
  76.3 0.7 reshape.791.tab
  77.0 36.9 %collective-permute-done.3 = f32[2081]{0:T(1024)S(1)} collective-permute-done((f32[2081]{0:T(1024)S(1)}, f32[2081]{0:T(1024)S(1)}, u32[]{:S(2)}, u32[]{:S(2)}) %collective-permute-start.3) | collective-permute-done | bytes 8356 | tf_op jit(solution)/shard_map/ppermute | solution.py:18
  113.9 0.6 pad_maximum_fusion.1.refs_4_
  114.5 0.6 pad_maximum_fusion.refs_4_
  115.1 26.3 %shard_map.37 = (f32[8,256,1024]{2,1,0:T(8,128)}, f32[8,256,1]{2,1,0:T(8,128)}) custom-call(s32[320]{0:T(512)} %reshape.797.tab, bf16[8,256,1024]{2,1,0:T(8,128)(2,1)} %bitcast.174, f32[8,256,1]{2,1,0:T(8,128)} %copy.221.refs_1_, bf16[8,256,1024]{2,1,0:T(8,128)(2,1)} %bitcast.175, f32[8,256]{1,0:T(8,128)} %copy-done.1), custom_call_target="tpu_custom_call" | custom-call | flops 10737418240 | bytes 41943040 | tf_op jit(solution)/shard_map/pallas_call | solution.py:151
  141.4 20.5 %shard_map.38 = (f32[8,256,1024]{2,1,0:T(8,128)}, f32[8,256,1]{2,1,0:T(8,128)}) custom-call(s32[320]{0:T(512)} %reshape.794.tab, bf16[8,256,1024]{2,1,0:T(8,128)(2,1)} %bitcast.176, f32[8,256,1]{2,1,0:T(8,128)} %copy.221.refs_1_, bf16[8,256,1024]{2,1,0:T(8,128)(2,1)} %collective-permute-done.5.refs_2_, ...), custom_call_target="tpu_custom_call", output_to_operand_aliasing={{0}: (6, {}), {1}: (7, {})} | custom-call | flops 10737418240 | bytes 41943040 | tf_op jit(solution)/shard_map/pallas_call | solution.py:151
  161.9 36.3 %shard_map.39 = bf16[8,256,1024]{2,1,0:T(8,128)(2,1)} custom-call(s32[320]{0:T(512)} %reshape.791.tab, bf16[8,256,1024]{2,1,0:T(8,128)(2,1)} %bitcast.177, f32[8,256,1]{2,1,0:T(8,128)} %copy.221.refs_1_, bf16[8,256,1024]{2,1,0:T(8,128)(2,1)} %collective-permute-done.1.refs_2_, bf16[8,256,1024]{2,1,0:T(8,128)(2,1)} %collective-permute-done.2.refs_3_, ...), custom_call_target="tpu_custom_call" | custom-call | flops 10737418240 | bytes 41943040 | tf_op jit(solution)/shard_map/pallas_call | solution.py:151
  (100 shorter events, 2.8 us)
Async XLA Ops:
  0.0 3.8 %copy-start.2 = (s32[16,2]{0,1:T(2,128)S(1)}, s32[16,2]{0,1:T(2,128)}, u32[]{:S(2)}) copy-start(s32[16,2]{0,1:T(2,128)} %param.4) | copy-start | bytes 388
  0.0 40.4 %copy-start = (s32[40]{0:T(128)S(1)}, s32[40]{0:T(128)}, u32[]{:S(2)}) copy-start(s32[40]{0:T(128)} %constant.74.clone.1) | copy-start | bytes 484
  3.1 48.6 %copy-start.1 = (f32[8,256]{1,0:T(8,128)}, f32[8,256]{1,0:T(8,128)S(1)}, u32[]{:S(2)}) copy-start(f32[8,256]{1,0:T(8,128)S(1)} %fusion.refs_3_) | copy-start | bytes 24580
  4.1 16.4 %collective-permute-start = (f32[2081]{0:T(1024)S(1)}, f32[2081]{0:T(1024)S(1)}, u32[]{:S(2)}, u32[]{:S(2)}) collective-permute-start(f32[2081]{0:T(1024)S(1)} %concatenate.150), channel_id=1, source_target_pairs={{0,64},{64,128},{128,192},{1,65},{65,129},{129,193},{2,66},{66,130... | collective-permute-start | bytes 24980 | tf_op jit(solution)/shard_map/ppermute | solution.py:18
  7.0 15.9 %collective-permute-start.4 = (f32[2081]{0:T(1024)S(1)}, f32[2081]{0:T(1024)S(1)}, u32[]{:S(2)}, u32[]{:S(2)}) collective-permute-start(f32[2081]{0:T(1024)S(1)} %concatenate.150), channel_id=1, source_target_pairs={{0,1},{1,2},{2,3},{3,4},{4,5},{5,6},{6,7},{7,8},{8,9},{9,10},{10,1... | collective-permute-start | bytes 24980 | tf_op jit(solution)/shard_map/ppermute | solution.py:18
  8.3 64.4 %collective-permute-start.7 = (f32[2081]{0:T(1024)S(1)}, f32[2081]{0:T(1024)S(1)}, u32[]{:S(2)}, u32[]{:S(2)}) collective-permute-start(f32[2081]{0:T(1024)S(1)} %concatenate.150), channel_id=1, source_target_pairs={{1,0},{2,1},{3,2},{4,3},{5,4},{6,5},{7,6},{8,7},{9,8},{10,9},{11,1... | collective-permute-start | bytes 24980 | tf_op jit(solution)/shard_map/ppermute | solution.py:18
  11.8 129.6 %collective-permute-start.5 = (bf16[8,256,1024]{2,1,0:T(8,128)(2,1)}, bf16[8,256,1024]{2,1,0:T(8,128)(2,1)}, u32[]{:S(2)}, u32[]{:S(2)}) collective-permute-start(bf16[8,256,1024]{2,1,0:T(8,128)(2,1)} %bitcast.170), channel_id=1, source_target_pairs={{1,0},{2,1},{3,2},{4,3},{5,4},{6,5},{7,6},{8,7},{9,8},{10,9},{11,1... | collective-permute-start | bytes 12582920 | tf_op jit(solution)/shard_map/ppermute | solution.py:18
  17.3 124.0 %collective-permute-start.6 = (bf16[8,256,1024]{2,1,0:T(8,128)(2,1)}, bf16[8,256,1024]{2,1,0:T(8,128)(2,1)}, u32[]{:S(2)}, u32[]{:S(2)}) collective-permute-start(bf16[8,256,1024]{2,1,0:T(8,128)(2,1)} %bitcast.171), channel_id=1, source_target_pairs={{0,1},{1,2},{2,3},{3,4},{4,5},{5,6},{6,7},{7,8},{8,9},{9,10},{10,1... | collective-permute-start | bytes 12582920 | tf_op jit(solution)/shard_map/ppermute | solution.py:18
  20.4 141.5 %collective-permute-start.1 = (bf16[8,256,1024]{2,1,0:T(8,128)(2,1)}, bf16[8,256,1024]{2,1,0:T(8,128)(2,1)}, u32[]{:S(2)}, u32[]{:S(2)}) collective-permute-start(bf16[8,256,1024]{2,1,0:T(8,128)(2,1)} %bitcast.172), channel_id=1, source_target_pairs={{64,0},{128,64},{192,128},{65,1},{129,65},{193,129},{66,2},{130,66... | collective-permute-start | bytes 12582920 | tf_op jit(solution)/shard_map/ppermute | solution.py:18
  22.9 139.0 %collective-permute-start.2 = (bf16[8,256,1024]{2,1,0:T(8,128)(2,1)}, bf16[8,256,1024]{2,1,0:T(8,128)(2,1)}, u32[]{:S(2)}, u32[]{:S(2)}) collective-permute-start(bf16[8,256,1024]{2,1,0:T(8,128)(2,1)} %bitcast.173), channel_id=1, source_target_pairs={{0,64},{64,128},{128,192},{1,65},{65,129},{129,193},{2,66},{66,130... | collective-permute-start | bytes 12582920 | tf_op jit(solution)/shard_map/ppermute | solution.py:18
  72.6 41.2 %collective-permute-start.3 = (f32[2081]{0:T(1024)S(1)}, f32[2081]{0:T(1024)S(1)}, u32[]{:S(2)}, u32[]{:S(2)}) collective-permute-start(f32[2081]{0:T(1024)S(1)} %concatenate.150), channel_id=1, source_target_pairs={{64,0},{128,64},{192,128},{65,1},{129,65},{193,129},{66,2},{130,66... | collective-permute-start | bytes 24980 | tf_op jit(solution)/shard_map/ppermute | solution.py:18

commit v3 on v0

v3 whole, which is shorter than its diff:
```python
import jax
import jax.numpy as jnp
from jax import lax
from jax.experimental import pallas as pl
from jax.experimental.pallas import tpu as pltpu
from jax.sharding import PartitionSpec as P

BLOCK = 256
scale_factor = 0.4
VMEM_LIMIT = 56 * 1024 * 1024


def shifted(shard, axis, by):
    devices = lax.axis_size(axis)
    pairs = [(i, i + by) for i in range(devices) if 0 <= i + by < devices]
    return lax.ppermute(shard, axis, pairs)


def squares_of(blocks):
    return jnp.einsum("bsd,bsd->bs", blocks, blocks, preferred_element_type=jnp.float32)


def pack_table(t, s, ix, v, nloc):
    t = jnp.clip(t, 0, nloc - 1)
    ix = jnp.clip(ix, 0, nloc - 1)
    return jnp.stack([t, s, ix, v.astype(jnp.int32)], axis=0).reshape(-1).astype(jnp.int32)


def make_kernel(nsrc, n, mode):
    def kernel(tab, own_ref, sqc_ref, *refs):
        src_refs = refs[:nsrc]
        sqr_ref = refs[nsrc]
        rest = refs[nsrc + 1:]
        if mode == "init":
            num_ref, den_ref = rest
        elif mode == "accum":
            num_in, den_in, num_ref, den_ref = rest
        else:
            num_in, den_in, out_ref, num_ref, den_ref = rest
        nloc = own_ref.shape[0]
        width = own_ref.shape[2]

        if mode == "accum":
            num_ref[...] = num_in[...]
            den_ref[...] = den_in[...]
        else:
            num_ref[...] = jnp.zeros_like(num_ref)
            den_ref[...] = jnp.zeros_like(den_ref)

        def contribute(t, prow, p_ref, ix):
            xt = own_ref[t]
            xp = p_ref[ix]
            inner = lax.dot_general(xt, xp, (((1,), (1,)), ((), ())),
                                    preferred_element_type=jnp.float32)
            sq_t = sqc_ref[t]
            sq_p = sqr_ref[pl.ds(prow, 1), :]
            distance = sq_t + sq_p - 2.0 * inner
            w = jnp.exp(-distance / (scale_factor * width)).astype(jnp.bfloat16)
            num_ref[t] += jnp.dot(w, xp, preferred_element_type=jnp.float32)
            den_ref[t] += jnp.sum(w.astype(jnp.float32), axis=1, keepdims=True)

        def body(j, carry):
            t = tab[j]
            s = tab[n + j]
            ix = tab[2 * n + j]
            used = tab[3 * n + j] == 1
            for k, p_ref in enumerate(src_refs):
                @pl.when(used & (s == k))
                def _():
                    contribute(t, k * nloc + ix, p_ref, ix)
            return carry

        lax.fori_loop(0, n, body, 0)

        if mode == "final":
            def fin(b, carry):
                out_ref[b] = ((num_in[b] + num_ref[b]) / (den_in[b] + den_ref[b])).astype(
                    out_ref.dtype)
                return carry
            lax.fori_loop(0, nloc, fin, 0)

    return kernel


def run_phase(mode, tab, n, own, sq_col, sources, sq_rows, num=None, den=None):
    nloc, block, width = own.shape
    nsrc = len(sources)
    vm = pl.BlockSpec(memory_space=pltpu.VMEM)
    in_specs = [pl.BlockSpec(memory_space=pltpu.SMEM), vm, vm] + [vm] * nsrc + [vm]
    args = [tab, own, sq_col, *sources, sq_rows]
    acc_shapes = [jax.ShapeDtypeStruct((nloc, block, width), jnp.float32),
                  jax.ShapeDtypeStruct((nloc, block, 1), jnp.float32)]
    scratch = []
    if mode != "init":
        in_specs += [vm, vm]
        args += [num, den]
    if mode == "final":
        out_shape = jax.ShapeDtypeStruct((nloc, block, width), jnp.bfloat16)
        out_specs = vm
        scratch = [pltpu.VMEM((nloc, block, width), jnp.float32),
                   pltpu.VMEM((nloc, block, 1), jnp.float32)]
    else:
        out_shape = acc_shapes
        out_specs = [vm, vm]
    flops = n * 4 * block * block * width
    return pl.pallas_call(
        make_kernel(nsrc, n, mode),
        in_specs=in_specs,
        out_specs=out_specs,
        out_shape=out_shape,
        scratch_shapes=scratch,
        compiler_params=pltpu.CompilerParams(vmem_limit_bytes=VMEM_LIMIT),
        cost_estimate=pl.CostEstimate(flops=flops, transcendentals=n * block * block,
                                      bytes_accessed=(nsrc + 3) * nloc * block * width * 2),
    )(*args)


def local(embeddings, pair_blocks, pair_count):
    total_rows, width = embeddings.shape
    nloc = total_rows // BLOCK
    slots = pair_blocks.shape[0]
    blocks = embeddings.reshape(nloc, BLOCK, width)
    owners = lax.axis_size("dev")
    first_block = (lax.axis_index("group") * owners + lax.axis_index("dev")) * nloc

    own_sq = squares_of(blocks)
    meta = jnp.concatenate([own_sq.reshape(-1),
                            pair_blocks.reshape(-1).astype(jnp.float32),
                            pair_count.astype(jnp.float32)])
    nsq = nloc * BLOCK
    m_nd = shifted(meta, "dev", -1)
    m_pd = shifted(meta, "dev", 1)
    m_ng = shifted(meta, "group", -1)
    m_pg = shifted(meta, "group", 1)
    blocks_after, m_nd, m_pd, m_ng, m_pg = lax.optimization_barrier(
        (blocks, m_nd, m_pd, m_ng, m_pg))

    nd = shifted(blocks_after, "dev", -1)
    pd = shifted(blocks_after, "dev", 1)
    ng = shifted(blocks_after, "group", -1)
    pg = shifted(blocks_after, "group", 1)

    def sq_of(m):
        return m[:nsq].reshape(nloc, BLOCK)

    def pairs_of(m):
        return (m[nsq:nsq + 2 * slots].astype(jnp.int32).reshape(slots, 2),
                m[nsq + 2 * slots:].astype(jnp.int32))

    pos = jnp.arange(slots, dtype=jnp.int32)
    used = pos < pair_count[0]
    left = pair_blocks[:, 0] - first_block
    right = pair_blocks[:, 1]
    roff = right - first_block
    r_local = roff < nloc
    r_dev = (roff >= nloc) & (roff < 2 * nloc)
    r_grp = ~r_local & ~r_dev
    ridx_dev = roff - nloc
    ridx_grp = right - first_block - owners * nloc
    zeros = jnp.zeros((slots,), jnp.int32)
    ones = jnp.ones((slots,), jnp.int32)
    sq_col = own_sq[:, :, None]

    diag = jnp.arange(nloc, dtype=jnp.int32)
    t1 = jnp.concatenate([diag, left, roff])
    i1 = jnp.concatenate([diag, roff, left])
    v1 = jnp.concatenate([jnp.ones((nloc,), bool), used & r_local, used & r_local])
    tab1 = pack_table(t1, jnp.zeros_like(t1), i1, v1, nloc)
    num, den = run_phase("init", tab1, t1.shape[0], blocks, sq_col, [blocks], own_sq)

    def prev_entries(m, prev_first):
        pairs, count = pairs_of(m)
        u = pos < count[0]
        r = pairs[:, 1] - first_block
        u = u & (r >= 0) & (r < nloc)
        return r, pairs[:, 0] - prev_first, u

    pr, pi, pu = prev_entries(m_pd, first_block - nloc)
    t2 = jnp.concatenate([left, pr])
    s2 = jnp.concatenate([zeros, ones])
    i2 = jnp.concatenate([ridx_dev, pi])
    v2 = jnp.concatenate([used & r_dev, pu])
    tab2 = pack_table(t2, s2, i2, v2, nloc)
    sq2 = jnp.concatenate([sq_of(m_nd), sq_of(m_pd)], axis=0)
    num, den = run_phase("accum", tab2, t2.shape[0], blocks, sq_col, [nd, pd], sq2, num, den)

    gr, gi, gu = prev_entries(m_pg, first_block - owners * nloc)
    t3 = jnp.concatenate([left, gr])
    s3 = jnp.concatenate([zeros, ones])
    i3 = jnp.concatenate([ridx_grp, gi])
    v3 = jnp.concatenate([used & r_grp, gu])
    tab3 = pack_table(t3, s3, i3, v3, nloc)
    sq3 = jnp.concatenate([sq_of(m_ng), sq_of(m_pg)], axis=0)
    smoothed = run_phase("final", tab3, t3.shape[0], blocks, sq_col, [ng, pg], sq3, num, den)
    return smoothed.reshape(total_rows, width)


def solution(mesh):
    placed = (P(("group", "dev"), None), P(("group", "dev"), None), P(("group", "dev")))
    return jax.shard_map(
        local, mesh=mesh, in_specs=placed, out_specs=P(("group", "dev"), None), check_vma=False
    )
```

time: 444 us -> 145 us (0.33)
  the two profiles are of different devices: /device:TPU:22 before, /device:TPU:85 now
where the time goes in v3:
time: 145 us
  Pallas kernels  67.8 us (47%)
  waiting for transfers between devices  40.6 us (28%)
  starting transfers between devices  23.6 us (16%)
  other arithmetic  5.89 us (4%)
  local copies, waits for them, and re-layouts  4.97 us (3%)
  between operations  2.04 us (1%)
    pallas_call x3, Pallas kernels, run_phase(): pl.pallas_call(make_kernel(nsrc, n, mode), in_specs=in_specs, out_specs=o...  67.8 us
    ppermute x8, waiting for transfers between devices, shifted(): return lax.ppermute(shard, axis, pairs)  40.6 us
    ppermute x8, starting transfers between devices, shifted(): return lax.ppermute(shard, axis, pairs)  23.6 us
    dot_general x1, other arithmetic, squares_of(): jnp.einsum('bsd,bsd->bs', blocks, blocks, preferred_element_type=jnp.floa...  3.09 us
  transfers between devices with their start and end apart: 8, of which 5 were waited for; matrix products, arithmetic and copies ran while one was open for 5% of the time, Pallas kernels for 29%

profile of v3, /device:TPU:85, one launch (start us, length us, event | category | flops | bytes accessed | tf_op | source)
XLA Modules:
  0.0 145.0 jit_solution(12389110747063813181)
XLA Ops:
  0.0 0.0 copy-start.1
  0.0 3.1 %fusion.refs_1_ = f32[8,256]{1,0:T(8,128)S(1)} fusion(bf16[8,256,1024]{2,1,0:T(8,128)(2,1)} %bitcast.33), kind=kLoop, calls=%fused_computation.1 | loop fusion | flops 6289408 | bytes 4202496 | tf_op jit(solution)/shard_map/bsd,bsd->bs/dot_general | solution.py:20
  3.1 0.0 copy-start
  3.8 0.0 copy-done.1
  3.8 0.1 copy.8
  3.9 0.1 convert_element_type.60
  4.0 0.1 concatenate.128
  4.0 2.6 %collective-permute-start = (f32[2081]{0:T(1024)S(1)}, f32[2081]{0:T(1024)S(1)}, u32[]{:S(2)}, u32[]{:S(2)}) collective-permute-start(f32[2081]{0:T(1024)S(1)} %concatenate.128), channel_id=1, source_target_pairs={{1,0},{2,1},{3,2},{4,3},{5,4},{6,5},{7,6},{8,7},{9,8},{10,9},{11,1... | collective-permute-start | bytes 24980 | tf_op jit(solution)/shard_map/ppermute | solution.py:16
  6.6 3.0 %collective-permute-start.1 = (f32[2081]{0:T(1024)S(1)}, f32[2081]{0:T(1024)S(1)}, u32[]{:S(2)}, u32[]{:S(2)}) collective-permute-start(f32[2081]{0:T(1024)S(1)} %concatenate.128), channel_id=1, source_target_pairs={{0,1},{1,2},{2,3},{3,4},{4,5},{5,6},{6,7},{7,8},{8,9},{9,10},{10,1... | collective-permute-start | bytes 24980 | tf_op jit(solution)/shard_map/ppermute | solution.py:16
  9.6 2.1 %collective-permute-start.2 = (f32[2081]{0:T(1024)S(1)}, f32[2081]{0:T(1024)S(1)}, u32[]{:S(2)}, u32[]{:S(2)}) collective-permute-start(f32[2081]{0:T(1024)S(1)} %concatenate.128), channel_id=1, source_target_pairs={{64,0},{128,64},{192,128},{65,1},{129,65},{193,129},{66,2},{130,66... | collective-permute-start | bytes 24980 | tf_op jit(solution)/shard_map/ppermute | solution.py:16
  11.7 3.2 %collective-permute-start.3 = (f32[2081]{0:T(1024)S(1)}, f32[2081]{0:T(1024)S(1)}, u32[]{:S(2)}, u32[]{:S(2)}) collective-permute-start(f32[2081]{0:T(1024)S(1)} %concatenate.128), channel_id=1, source_target_pairs={{0,64},{64,128},{128,192},{1,65},{65,129},{129,193},{2,66},{66,130... | collective-permute-start | bytes 24980 | tf_op jit(solution)/shard_map/ppermute | solution.py:16
  14.9 0.0 collective-permute-done
  14.9 0.0 collective-permute-done.1
  14.9 0.0 collective-permute-done.2
  14.9 1.2 collective-permute-done.3
  16.1 2.8 %collective-permute-start.6 = (bf16[8,256,1024]{2,1,0:T(8,128)(2,1)}, bf16[8,256,1024]{2,1,0:T(8,128)(2,1)}, u32[]{:S(2)}, u32[]{:S(2)}) collective-permute-start(bf16[8,256,1024]{2,1,0:T(8,128)(2,1)} %bitcast.34), channel_id=1, source_target_pairs={{1,0},{2,1},{3,2},{4,3},{5,4},{6,5},{7,6},{8,7},{9,8},{10,9},{11,1... | collective-permute-start | bytes 12582920 | tf_op jit(solution)/shard_map/ppermute | solution.py:16
  18.9 2.8 %collective-permute-start.7 = (bf16[8,256,1024]{2,1,0:T(8,128)(2,1)}, bf16[8,256,1024]{2,1,0:T(8,128)(2,1)}, u32[]{:S(2)}, u32[]{:S(2)}) collective-permute-start(bf16[8,256,1024]{2,1,0:T(8,128)(2,1)} %bitcast.35), channel_id=1, source_target_pairs={{0,1},{1,2},{2,3},{3,4},{4,5},{5,6},{6,7},{7,8},{8,9},{9,10},{10,1... | collective-permute-start | bytes 12582920 | tf_op jit(solution)/shard_map/ppermute | solution.py:16
  21.7 0.1 copy.9
  21.8 0.1 compare_reduce_fusion.4
  22.0 2.1 %collective-permute-start.4 = (bf16[8,256,1024]{2,1,0:T(8,128)(2,1)}, bf16[8,256,1024]{2,1,0:T(8,128)(2,1)}, u32[]{:S(2)}, u32[]{:S(2)}) collective-permute-start(bf16[8,256,1024]{2,1,0:T(8,128)(2,1)} %bitcast.36), channel_id=1, source_target_pairs={{64,0},{128,64},{192,128},{65,1},{129,65},{193,129},{66,2},{130,66... | collective-permute-start | bytes 12582920 | tf_op jit(solution)/shard_map/ppermute | solution.py:16
  24.0 5.1 %collective-permute-start.5 = (bf16[8,256,1024]{2,1,0:T(8,128)(2,1)}, bf16[8,256,1024]{2,1,0:T(8,128)(2,1)}, u32[]{:S(2)}, u32[]{:S(2)}) collective-permute-start(bf16[8,256,1024]{2,1,0:T(8,128)(2,1)} %bitcast.37), channel_id=1, source_target_pairs={{0,64},{64,128},{128,192},{1,65},{65,129},{129,193},{2,66},{66,130... | collective-permute-start | bytes 12582920 | tf_op jit(solution)/shard_map/ppermute | solution.py:16
  29.2 0.1 fusion.10
  29.3 0.1 copy.7
  29.3 0.2 subtract_reduce_fusion.1
  29.5 0.1 add_clamp_fusion.4
  29.6 0.6 reshape.367.tab
  30.2 1.4 copy.12.sqc_ref
  31.6 0.0 copy-done
  31.6 0.0 copy-start.2
  31.6 21.3 %shard_map.37 = (f32[8,256,1024]{2,1,0:T(8,128)}, f32[8,256,1]{2,1,0:T(8,128)}) custom-call(s32[160]{0:T(256)} %reshape.367.tab, bf16[8,256,1024]{2,1,0:T(8,128)(2,1)} %bitcast.38, f32[8,256,1]{2,1,0:T(8,128)} %copy.12.sqc_ref, bf16[8,256,1024]{2,1,0:T(8,128)(2,1)} %bitcast.39, f32[8,256]{1,0:T(8,128)} %copy-done), custom_call_target="tpu_custom_call" | custom-call | flops 10737418240 | bytes 16777216 | tf_op jit(solution)/shard_map/pallas_call | solution.py:106
  52.9 0.6 slice.53
  53.4 0.6 slice.47
  54.0 0.1 convert_element_type.63
  54.7 0.1 convert_element_type.67
  55.3 0.2 compare_reduce_fusion.3
  55.5 0.1 add_convert_fusion
  55.6 0.2 compare_reduce_fusion.1
  55.8 0.1 add_convert_fusion.1
  55.9 0.2 fusion.3
  56.1 0.1 add_clamp_fusion.1
  56.2 0.2 fusion.4
  56.3 0.1 add_clamp_fusion.3
  56.4 0.1 add_clamp_fusion.2
  56.5 0.0 copy-done.2
  56.5 0.6 reshape.364.tab
  57.2 0.6 reshape.361.tab
  57.8 0.6 pad_maximum_fusion.1.refs_2_
  58.4 0.6 pad_maximum_fusion.refs_2_
  59.0 7.6 %collective-permute-done.6.refs_0_ = bf16[8,256,1024]{2,1,0:T(8,128)(2,1)} collective-permute-done((bf16[8,256,1024]{2,1,0:T(8,128)(2,1)}, bf16[8,256,1024]{2,1,0:T(8,128)(2,1)}, u32[]{:S(2)}, u32[]{:S(2)}) %collective-permute-start.6) | collective-permute-done | bytes 4194336 | tf_op jit(solution)/shard_map/ppermute | solution.py:16
  66.6 0.9 collective-permute-done.7.refs_1_
  67.5 21.1 %shard_map.38 = (f32[8,256,1024]{2,1,0:T(8,128)}, f32[8,256,1]{2,1,0:T(8,128)}) custom-call(s32[128]{0:T(128)} %reshape.364.tab, bf16[8,256,1024]{2,1,0:T(8,128)(2,1)} %bitcast.40, f32[8,256,1]{2,1,0:T(8,128)} %copy.12.sqc_ref, bf16[8,256,1024]{2,1,0:T(8,128)(2,1)} %collective-permute-done.6.refs_0_, bf16[8,256,1024]{2,1,0:T(8,128)(2,1)} %collective-permute-done.7.refs_1_, ...), custom_call_target="tpu_custom_call" | custom-call | flops 8589934592 | bytes 20971520 | tf_op jit(solution)/shard_map/pallas_call | solution.py:106
  88.5 28.1 %collective-permute-done.4.refs_0_ = bf16[8,256,1024]{2,1,0:T(8,128)(2,1)} collective-permute-done((bf16[8,256,1024]{2,1,0:T(8,128)(2,1)}, bf16[8,256,1024]{2,1,0:T(8,128)(2,1)}, u32[]{:S(2)}, u32[]{:S(2)}) %collective-permute-start.4) | collective-permute-done | bytes 4194336 | tf_op jit(solution)/shard_map/ppermute | solution.py:16
  116.7 2.8 %collective-permute-done.5.refs_1_ = bf16[8,256,1024]{2,1,0:T(8,128)(2,1)} collective-permute-done((bf16[8,256,1024]{2,1,0:T(8,128)(2,1)}, bf16[8,256,1024]{2,1,0:T(8,128)(2,1)}, u32[]{:S(2)}, u32[]{:S(2)}) %collective-permute-start.5) | collective-permute-done | bytes 4194336 | tf_op jit(solution)/shard_map/ppermute | solution.py:16
  119.5 25.5 %shard_map.39 = bf16[8,256,1024]{2,1,0:T(8,128)(2,1)} custom-call(s32[128]{0:T(128)} %reshape.361.tab, bf16[8,256,1024]{2,1,0:T(8,128)(2,1)} %bitcast.41, f32[8,256,1]{2,1,0:T(8,128)} %copy.12.sqc_ref, bf16[8,256,1024]{2,1,0:T(8,128)(2,1)} %collective-permute-done.4.refs_0_, bf16[8,256,1024]{2,1,0:T(8,128)(2,1)} %collective-permute-done.5.refs_1_, ...), custom_call_target="tpu_custom_call" | custom-call | flops 8589934592 | bytes 20971520 | tf_op jit(solution)/shard_map/pallas_call | solution.py:106
  (20 shorter events, 0.1 us)
Async XLA Ops:
  0.0 3.8 %copy-start.1 = (s32[16,2]{0,1:T(2,128)S(1)}, s32[16,2]{0,1:T(2,128)}, u32[]{:S(2)}) copy-start(s32[16,2]{0,1:T(2,128)} %param.4) | copy-start | bytes 388
  3.1 28.5 %copy-start = (f32[8,256]{1,0:T(8,128)}, f32[8,256]{1,0:T(8,128)S(1)}, u32[]{:S(2)}) copy-start(f32[8,256]{1,0:T(8,128)S(1)} %fusion.refs_1_) | copy-start | bytes 24580
  4.0 10.9 %collective-permute-start = (f32[2081]{0:T(1024)S(1)}, f32[2081]{0:T(1024)S(1)}, u32[]{:S(2)}, u32[]{:S(2)}) collective-permute-start(f32[2081]{0:T(1024)S(1)} %concatenate.128), channel_id=1, source_target_pairs={{1,0},{2,1},{3,2},{4,3},{5,4},{6,5},{7,6},{8,7},{9,8},{10,9},{11,1... | collective-permute-start | bytes 24980 | tf_op jit(solution)/shard_map/ppermute | solution.py:16
  6.6 8.3 %collective-permute-start.1 = (f32[2081]{0:T(1024)S(1)}, f32[2081]{0:T(1024)S(1)}, u32[]{:S(2)}, u32[]{:S(2)}) collective-permute-start(f32[2081]{0:T(1024)S(1)} %concatenate.128), channel_id=1, source_target_pairs={{0,1},{1,2},{2,3},{3,4},{4,5},{5,6},{6,7},{7,8},{8,9},{9,10},{10,1... | collective-permute-start | bytes 24980 | tf_op jit(solution)/shard_map/ppermute | solution.py:16
  9.6 5.3 %collective-permute-start.2 = (f32[2081]{0:T(1024)S(1)}, f32[2081]{0:T(1024)S(1)}, u32[]{:S(2)}, u32[]{:S(2)}) collective-permute-start(f32[2081]{0:T(1024)S(1)} %concatenate.128), channel_id=1, source_target_pairs={{64,0},{128,64},{192,128},{65,1},{129,65},{193,129},{66,2},{130,66... | collective-permute-start | bytes 24980 | tf_op jit(solution)/shard_map/ppermute | solution.py:16
  11.7 4.4 %collective-permute-start.3 = (f32[2081]{0:T(1024)S(1)}, f32[2081]{0:T(1024)S(1)}, u32[]{:S(2)}, u32[]{:S(2)}) collective-permute-start(f32[2081]{0:T(1024)S(1)} %concatenate.128), channel_id=1, source_target_pairs={{0,64},{64,128},{128,192},{1,65},{65,129},{129,193},{2,66},{66,130... | collective-permute-start | bytes 24980 | tf_op jit(solution)/shard_map/ppermute | solution.py:16
  16.1 50.4 %collective-permute-start.6 = (bf16[8,256,1024]{2,1,0:T(8,128)(2,1)}, bf16[8,256,1024]{2,1,0:T(8,128)(2,1)}, u32[]{:S(2)}, u32[]{:S(2)}) collective-permute-start(bf16[8,256,1024]{2,1,0:T(8,128)(2,1)} %bitcast.34), channel_id=1, source_target_pairs={{1,0},{2,1},{3,2},{4,3},{5,4},{6,5},{7,6},{8,7},{9,8},{10,9},{11,1... | collective-permute-start | bytes 12582920 | tf_op jit(solution)/shard_map/ppermute | solution.py:16
  18.9 48.5 %collective-permute-start.7 = (bf16[8,256,1024]{2,1,0:T(8,128)(2,1)}, bf16[8,256,1024]{2,1,0:T(8,128)(2,1)}, u32[]{:S(2)}, u32[]{:S(2)}) collective-permute-start(bf16[8,256,1024]{2,1,0:T(8,128)(2,1)} %bitcast.35), channel_id=1, source_target_pairs={{0,1},{1,2},{2,3},{3,4},{4,5},{5,6},{6,7},{7,8},{8,9},{9,10},{10,1... | collective-permute-start | bytes 12582920 | tf_op jit(solution)/shard_map/ppermute | solution.py:16
  22.0 94.7 %collective-permute-start.4 = (bf16[8,256,1024]{2,1,0:T(8,128)(2,1)}, bf16[8,256,1024]{2,1,0:T(8,128)(2,1)}, u32[]{:S(2)}, u32[]{:S(2)}) collective-permute-start(bf16[8,256,1024]{2,1,0:T(8,128)(2,1)} %bitcast.36), channel_id=1, source_target_pairs={{64,0},{128,64},{192,128},{65,1},{129,65},{193,129},{66,2},{130,66... | collective-permute-start | bytes 12582920 | tf_op jit(solution)/shard_map/ppermute | solution.py:16
  24.0 95.4 %collective-permute-start.5 = (bf16[8,256,1024]{2,1,0:T(8,128)(2,1)}, bf16[8,256,1024]{2,1,0:T(8,128)(2,1)}, u32[]{:S(2)}, u32[]{:S(2)}) collective-permute-start(bf16[8,256,1024]{2,1,0:T(8,128)(2,1)} %bitcast.37), channel_id=1, source_target_pairs={{0,64},{64,128},{128,192},{1,65},{65,129},{129,193},{2,66},{66,130... | collective-permute-start | bytes 12582920 | tf_op jit(solution)/shard_map/ppermute | solution.py:16
  31.6 24.9 %copy-start.2 = (s32[1,32]{1,0:T(1,128)S(1)}, s32[1,32]{1,0:T(1,128)}, u32[]{:S(2)}) copy-start(s32[1,32]{1,0:T(1,128)} %constant.11.clone.1) | copy-start | bytes 388

commit v4 on v3

--- a/solution.py
+++ b/solution.py
@@ -37,8 +37,8 @@
             num_in, den_in, num_ref, den_ref = rest
         else:
             num_in, den_in, out_ref, num_ref, den_ref = rest
-        nloc = own_ref.shape[0]
-        width = own_ref.shape[2]
+        nloc = own_ref.shape[0] // BLOCK
+        width = own_ref.shape[1]
 
         if mode == "accum":
             num_ref[...] = num_in[...]
@@ -48,8 +48,8 @@
             den_ref[...] = jnp.zeros_like(den_ref)
 
         def contribute(t, prow, p_ref, ix):
-            xt = own_ref[t]
-            xp = p_ref[ix]
+            xt = own_ref[pl.ds(pl.multiple_of(t * BLOCK, BLOCK), BLOCK), :]
+            xp = p_ref[pl.ds(pl.multiple_of(ix * BLOCK, BLOCK), BLOCK), :]
             inner = lax.dot_general(xt, xp, (((1,), (1,)), ((), ())),
                                     preferred_element_type=jnp.float32)
             sq_t = sqc_ref[t]
@@ -83,7 +83,9 @@
 
 
 def run_phase(mode, tab, n, own, sq_col, sources, sq_rows, num=None, den=None):
-    nloc, block, width = own.shape
+    rows, width = own.shape
+    block = BLOCK
+    nloc = rows // block
     nsrc = len(sources)
     vm = pl.BlockSpec(memory_space=pltpu.VMEM)
     in_specs = [pl.BlockSpec(memory_space=pltpu.SMEM), vm, vm] + [vm] * nsrc + [vm]
@@ -115,6 +117,33 @@
     )(*args)
 
 
+def encode_meta(own_sq, pair_blocks, pair_count, width):
+    nloc = own_sq.shape[0]
+    hi = lax.reduce_precision(own_sq, exponent_bits=8, mantissa_bits=7)
+    r1 = own_sq - hi
+    mid = lax.reduce_precision(r1, exponent_bits=8, mantissa_bits=7)
+    lo = r1 - mid
+    pieces = jnp.concatenate([hi, mid, lo], axis=0)
+    pieces = jnp.pad(pieces, ((0, 0), (0, width - pieces.shape[1])))
+    ids = pair_blocks.reshape(1, -1) + 1
+    ints = jnp.concatenate([ids // 64, ids % 64], axis=0)
+    ints = jnp.pad(ints, ((0, 0), (0, width - ints.shape[1])))
+    cnt = jnp.pad(pair_count.reshape(1, 1), ((0, 0), (0, width - 1)))
+    meta = jnp.concatenate([pieces, ints.astype(jnp.float32), cnt.astype(jnp.float32)], axis=0)
+    pad_rows = -meta.shape[0] % 16
+    meta = jnp.pad(meta, ((0, pad_rows), (0, 0)))
+    return meta.astype(jnp.bfloat16)
+
+
+def decode_meta(recv, nloc, slots):
+    meta = recv[nloc * BLOCK:].astype(jnp.float32)
+    sq = (meta[:nloc, :BLOCK] + meta[nloc:2 * nloc, :BLOCK]) + meta[2 * nloc:3 * nloc, :BLOCK]
+    ids = meta[3 * nloc, :2 * slots] * 64.0 + meta[3 * nloc + 1, :2 * slots]
+    pairs = ids.astype(jnp.int32).reshape(slots, 2) - 1
+    count = meta[3 * nloc + 2, :1].astype(jnp.int32)
+    return sq, pairs, count
+
+
 def local(embeddings, pair_blocks, pair_count):
     total_rows, width = embeddings.shape
     nloc = total_rows // BLOCK
@@ -124,28 +153,12 @@
     first_block = (lax.axis_index("group") * owners + lax.axis_index("dev")) * nloc
 
     own_sq = squares_of(blocks)
-    meta = jnp.concatenate([own_sq.reshape(-1),
-                            pair_blocks.reshape(-1).astype(jnp.float32),
-                            pair_count.astype(jnp.float32)])
-    nsq = nloc * BLOCK
-    m_nd = shifted(meta, "dev", -1)
-    m_pd = shifted(meta, "dev", 1)
-    m_ng = shifted(meta, "group", -1)
-    m_pg = shifted(meta, "group", 1)
-    blocks_after, m_nd, m_pd, m_ng, m_pg = lax.optimization_barrier(
-        (blocks, m_nd, m_pd, m_ng, m_pg))
-
-    nd = shifted(blocks_after, "dev", -1)
-    pd = shifted(blocks_after, "dev", 1)
-    ng = shifted(blocks_after, "group", -1)
-    pg = shifted(blocks_after, "group", 1)
-
-    def sq_of(m):
-        return m[:nsq].reshape(nloc, BLOCK)
-
-    def pairs_of(m):
-        return (m[nsq:nsq + 2 * slots].astype(jnp.int32).reshape(slots, 2),
-                m[nsq + 2 * slots:].astype(jnp.int32))
+    payload = jnp.concatenate(
+        [embeddings, encode_meta(own_sq, pair_blocks, pair_count, width)], axis=0)
+    nd = shifted(payload, "dev", -1)
+    pd = shifted(payload, "dev", 1)
+    ng = shifted(payload, "group", -1)
+    pg = shifted(payload, "group", 1)
 
     pos = jnp.arange(slots, dtype=jnp.int32)
     used = pos < pair_count[0]
@@ -166,32 +179,37 @@
     i1 = jnp.concatenate([diag, roff, left])
     v1 = jnp.concatenate([jnp.ones((nloc,), bool), used & r_local, used & r_local])
     tab1 = pack_table(t1, jnp.zeros_like(t1), i1, v1, nloc)
-    num, den = run_phase("init", tab1, t1.shape[0], blocks, sq_col, [blocks], own_sq)
-
-    def prev_entries(m, prev_first):
-        pairs, count = pairs_of(m)
+    num, den = run_phase("init", tab1, t1.shape[0], embeddings, sq_col, [embeddings], own_sq)
+
+    def prev_entries(pairs, count, prev_first):
         u = pos < count[0]
         r = pairs[:, 1] - first_block
         u = u & (r >= 0) & (r < nloc)
         return r, pairs[:, 0] - prev_first, u
 
-    pr, pi, pu = prev_entries(m_pd, first_block - nloc)
+    nd, pd, num, den = lax.optimization_barrier((nd, pd, num, den))
+    sq_nd, _, _ = decode_meta(nd, nloc, slots)
+    sq_pd, pd_pairs, pd_count = decode_meta(pd, nloc, slots)
+    pr, pi, pu = prev_entries(pd_pairs, pd_count, first_block - nloc)
     t2 = jnp.concatenate([left, pr])
     s2 = jnp.concatenate([zeros, ones])
     i2 = jnp.concatenate([ridx_dev, pi])
     v2 = jnp.concatenate([used & r_dev, pu])
     tab2 = pack_table(t2, s2, i2, v2, nloc)
-    sq2 = jnp.concatenate([sq_of(m_nd), sq_of(m_pd)], axis=0)
-    num, den = run_phase("accum", tab2, t2.shape[0], blocks, sq_col, [nd, pd], sq2, num, den)
-
-    gr, gi, gu = prev_entries(m_pg, first_block - owners * nloc)
+    sq2 = jnp.concatenate([sq_nd, sq_pd], axis=0)
+    num, den = run_phase("accum", tab2, t2.shape[0], embeddings, sq_col, [nd, pd], sq2, num, den)
+
+    ng, pg, num, den = lax.optimization_barrier((ng, pg, num, den))
+    sq_ng, _, _ = decode_meta(ng, nloc, slots)
+    sq_pg, pg_pairs, pg_count = decode_meta(pg, nloc, slots)
+    gr, gi, gu = prev_entries(pg_pairs, pg_count, first_block - owners * nloc)
     t3 = jnp.concatenate([left, gr])
     s3 = jnp.concatenate([zeros, ones])
     i3 = jnp.concatenate([ridx_grp, gi])
     v3 = jnp.concatenate([used & r_grp, gu])
     tab3 = pack_table(t3, s3, i3, v3, nloc)
-    sq3 = jnp.concatenate([sq_of(m_ng), sq_of(m_pg)], axis=0)
-    smoothed = run_phase("final", tab3, t3.shape[0], blocks, sq_col, [ng, pg], sq3, num, den)
+    sq3 = jnp.concatenate([sq_ng, sq_pg], axis=0)
+    smoothed = run_phase("final", tab3, t3.shape[0], embeddings, sq_col, [ng, pg], sq3, num, den)
     return smoothed.reshape(total_rows, width)
 
 

time: 145 us -> 146 us (level)
  the two profiles are of different devices: /device:TPU:85 before, /device:TPU:79 now
where the time goes in v4:
time: 146 us
  Pallas kernels  64 us (44%)
  waiting for transfers between devices  47 us (32%)
  other arithmetic  14.8 us (10%)
  starting transfers between devices  12.9 us (9%)
  local copies, waits for them, and re-layouts  4.87 us (3%)
  between operations  2.26 us (2%)
    pallas_call x3, Pallas kernels, run_phase(): pl.pallas_call(make_kernel(nsrc, n, mode), in_specs=in_specs, out_specs=o...  64 us
    ppermute x4, waiting for transfers between devices, shifted(): return lax.ppermute(shard, axis, pairs)  47 us
    ppermute x4, starting transfers between devices, shifted(): return lax.ppermute(shard, axis, pairs)  12.9 us
    concatenate x1, other arithmetic, local(): jnp.concatenate([embeddings, encode_meta(own_sq, pair_blocks, pair_count,...  4.62 us
    convert_element_type x4, other arithmetic, decode_meta(): meta = recv[nloc * BLOCK:].astype(jnp.float32)  3.4 us
    dot_general x1, other arithmetic, squares_of(): jnp.einsum('bsd,bsd->bs', blocks, blocks, preferred_element_type=jnp.floa...  3.08 us
  transfers between devices with their start and end apart: 4, of which 4 were waited for; matrix products, arithmetic and copies ran while one was open for 5% of the time, Pallas kernels for 25%

profile of v4, /device:TPU:79, one launch (start us, length us, event | category | flops | bytes accessed | tf_op | source)
XLA Modules:
  0.0 145.8 jit_solution(14274794011281416880)
XLA Ops:
  0.7 3.1 %fusion.refs_1_ = f32[8,256]{1,0:T(8,128)S(1)} fusion(bf16[8,256,1024]{2,1,0:T(8,128)(2,1)} %bitcast.33), kind=kLoop, calls=%fused_computation.1 | loop fusion | flops 6289408 | bytes 4202496 | tf_op jit(solution)/shard_map/bsd,bsd->bs/dot_general | solution.py:20
  3.7 0.0 copy-start
  3.8 0.7 broadcast_add_fusion
  4.4 0.1 copy.11
  4.5 0.1 add.116
  4.7 0.0 copy-start.1
  4.7 4.6 %pad_maximum_fusion = bf16[2080,1024]{1,0:T(8,128)(2,1)} fusion(bf16[32,1024]{1,0:T(8,128)(2,1)S(1)} %fusion.8, bf16[2048,1024]{1,0:T(8,128)(2,1)} %own_ref.5), kind=kLoop, calls=%fused_computation.2 | loop fusion | flops 8519680 | bytes 8519680 | tf_op jit(solution)/shard_map/concatenate | solution.py:156
  9.3 2.6 %collective-permute-start.2 = (bf16[2080,1024]{1,0:T(8,128)(2,1)}, bf16[2080,1024]{1,0:T(8,128)(2,1)}, u32[]{:S(2)}, u32[]{:S(2)}) collective-permute-start(bf16[2080,1024]{1,0:T(8,128)(2,1)} %pad_maximum_fusion), channel_id=1, source_target_pairs={{1,0},{2,1},{3,2},{4,3},{5,4},{6,5},{7,6},{8,7},{9,8},{10,9},{11,1... | collective-permute-start | bytes 12779528 | tf_op jit(solution)/shard_map/ppermute | solution.py:16
  11.9 5.1 %collective-permute-start.3 = (bf16[2080,1024]{1,0:T(8,128)(2,1)}, bf16[2080,1024]{1,0:T(8,128)(2,1)}, u32[]{:S(2)}, u32[]{:S(2)}) collective-permute-start(bf16[2080,1024]{1,0:T(8,128)(2,1)} %pad_maximum_fusion), channel_id=1, source_target_pairs={{0,1},{1,2},{2,3},{3,4},{4,5},{5,6},{6,7},{7,8},{8,9},{9,10},{10,1... | collective-permute-start | bytes 12779528 | tf_op jit(solution)/shard_map/ppermute | solution.py:16
  17.0 2.1 %collective-permute-start = (bf16[2080,1024]{1,0:T(8,128)(2,1)}, bf16[2080,1024]{1,0:T(8,128)(2,1)}, u32[]{:S(2)}, u32[]{:S(2)}) collective-permute-start(bf16[2080,1024]{1,0:T(8,128)(2,1)} %pad_maximum_fusion), channel_id=1, source_target_pairs={{64,0},{128,64},{192,128},{65,1},{129,65},{193,129},{66,2},{130,66... | collective-permute-start | bytes 12779528 | tf_op jit(solution)/shard_map/ppermute | solution.py:16
  19.1 3.2 %collective-permute-start.1 = (bf16[2080,1024]{1,0:T(8,128)(2,1)}, bf16[2080,1024]{1,0:T(8,128)(2,1)}, u32[]{:S(2)}, u32[]{:S(2)}) collective-permute-start(bf16[2080,1024]{1,0:T(8,128)(2,1)} %pad_maximum_fusion), channel_id=1, source_target_pairs={{0,64},{64,128},{128,192},{1,65},{65,129},{129,193},{2,66},{66,130... | collective-permute-start | bytes 12779528 | tf_op jit(solution)/shard_map/ppermute | solution.py:16
  22.3 0.0 copy-done.1
  22.4 0.1 copy.12
  22.4 0.1 copy.10
  22.5 0.1 and_reduce_fusion
  22.7 0.1 fusion.21
  22.7 0.1 add_reduce_fusion
  22.9 0.1 add_clamp_fusion
  23.0 0.7 reshape.470.tab
  23.7 0.0 copy-done
  23.7 1.4 copy.13.sqc_ref
  25.0 0.0 copy-start.2
  25.0 18.2 %shard_map.37 = (f32[8,256,1024]{2,1,0:T(8,128)}, f32[8,256,1]{2,1,0:T(8,128)}) custom-call(s32[160]{0:T(256)} %reshape.470.tab, bf16[2048,1024]{1,0:T(8,128)(2,1)} %own_ref.5, f32[8,256,1]{2,1,0:T(8,128)} %copy.13.sqc_ref, bf16[2048,1024]{1,0:T(8,128)(2,1)} %own_ref.5, f32[8,256]{1,0:T(8,128)} %copy-done), custom_call_target="tpu_custom_call" | custom-call | flops 10737418240 | bytes 16777216 | tf_op jit(solution)/shard_map/pallas_call | solution.py:108
  43.2 19.1 %collective-permute-done.2.refs_0_ = bf16[2080,1024]{1,0:T(8,128)(2,1)} collective-permute-done((bf16[2080,1024]{1,0:T(8,128)(2,1)}, bf16[2080,1024]{1,0:T(8,128)(2,1)}, u32[]{:S(2)}, u32[]{:S(2)}) %collective-permute-start.2) | collective-permute-done | bytes 4259872 | tf_op jit(solution)/shard_map/ppermute | solution.py:16
  62.3 1.2 collective-permute-done.3.refs_1_
  63.5 0.8 slice_convert_fusion.3
  64.3 0.6 slice.116
  64.9 0.1 sub.172
  65.7 0.2 fusion.14
  65.9 0.1 add_clamp_fusion.2
  66.0 0.1 add_clamp_fusion.3
  66.1 0.2 compare_reduce_fusion.3
  66.3 0.1 add_convert_fusion
  66.4 0.0 copy-done.2
  66.4 0.6 reshape.471.tab
  67.0 0.8 slice_convert_fusion.2
  67.8 0.6 pad_maximum_fusion.1.refs_2_
  68.4 18.0 %shard_map.38 = (f32[8,256,1024]{2,1,0:T(8,128)}, f32[8,256,1]{2,1,0:T(8,128)}) custom-call(s32[128]{0:T(128)} %reshape.471.tab, bf16[2048,1024]{1,0:T(8,128)(2,1)} %own_ref.5, f32[8,256,1]{2,1,0:T(8,128)} %copy.13.sqc_ref, bf16[2080,1024]{1,0:T(8,128)(2,1)} %collective-permute-done.2.refs_0_, bf16[2080,1024]{1,0:T(8,128)(2,1)} %collective-permute-done.3.refs_1_, ...), custom_call_target="tpu_custom_call" | custom-call | flops 8589934592 | bytes 20971520 | tf_op jit(solution)/shard_map/pallas_call | solution.py:108
  86.4 24.6 %collective-permute-done.refs_0_ = bf16[2080,1024]{1,0:T(8,128)(2,1)} collective-permute-done((bf16[2080,1024]{1,0:T(8,128)(2,1)}, bf16[2080,1024]{1,0:T(8,128)(2,1)}, u32[]{:S(2)}, u32[]{:S(2)}) %collective-permute-start) | collective-permute-done | bytes 4259872 | tf_op jit(solution)/shard_map/ppermute | solution.py:16
  111.0 2.1 %collective-permute-done.1.refs_1_ = bf16[2080,1024]{1,0:T(8,128)(2,1)} collective-permute-done((bf16[2080,1024]{1,0:T(8,128)(2,1)}, bf16[2080,1024]{1,0:T(8,128)(2,1)}, u32[]{:S(2)}, u32[]{:S(2)}) %collective-permute-start.1) | collective-permute-done | bytes 4259872 | tf_op jit(solution)/shard_map/ppermute | solution.py:16
  113.1 0.8 slice_convert_fusion.1
  114.0 0.5 slice.127
  114.5 0.8 slice_convert_fusion
  115.4 0.1 sub.179
  115.4 0.2 compare_reduce_fusion.1
  115.6 0.2 fusion.15
  115.8 0.1 add_clamp_fusion.4
  116.6 0.1 add_clamp_fusion.5
  116.7 0.1 add_convert_fusion.1
  116.7 0.6 reshape.472.tab
  117.4 0.6 pad_maximum_fusion.2.refs_2_
  118.0 27.9 %shard_map.39 = bf16[8,256,1024]{2,1,0:T(8,128)(2,1)} custom-call(s32[128]{0:T(128)} %reshape.472.tab, bf16[2048,1024]{1,0:T(8,128)(2,1)} %own_ref.5, f32[8,256,1]{2,1,0:T(8,128)} %copy.13.sqc_ref, bf16[2080,1024]{1,0:T(8,128)(2,1)} %collective-permute-done.refs_0_, bf16[2080,1024]{1,0:T(8,128)(2,1)} %collective-permute-done.1.refs_1_, ...), custom_call_target="tpu_custom_call" | custom-call | flops 8589934592 | bytes 20971520 | tf_op jit(solution)/shard_map/pallas_call | solution.py:108
  (23 shorter events, 0.2 us)
Async XLA Ops:
  3.7 19.9 %copy-start = (f32[8,256]{1,0:T(8,128)}, f32[8,256]{1,0:T(8,128)S(1)}, u32[]{:S(2)}) copy-start(f32[8,256]{1,0:T(8,128)S(1)} %fusion.refs_1_) | copy-start | bytes 24580
  4.7 17.6 %copy-start.1 = (s32[16,2]{0,1:T(2,128)S(1)}, s32[16,2]{0,1:T(2,128)}, u32[]{:S(2)}) copy-start(s32[16,2]{0,1:T(2,128)} %param.4) | copy-start | bytes 388
  9.3 52.9 %collective-permute-start.2 = (bf16[2080,1024]{1,0:T(8,128)(2,1)}, bf16[2080,1024]{1,0:T(8,128)(2,1)}, u32[]{:S(2)}, u32[]{:S(2)}) collective-permute-start(bf16[2080,1024]{1,0:T(8,128)(2,1)} %pad_maximum_fusion), channel_id=1, source_target_pairs={{1,0},{2,1},{3,2},{4,3},{5,4},{6,5},{7,6},{8,7},{9,8},{10,9},{11,1... | collective-permute-start | bytes 12779528 | tf_op jit(solution)/shard_map/ppermute | solution.py:16
  11.9 51.5 %collective-permute-start.3 = (bf16[2080,1024]{1,0:T(8,128)(2,1)}, bf16[2080,1024]{1,0:T(8,128)(2,1)}, u32[]{:S(2)}, u32[]{:S(2)}) collective-permute-start(bf16[2080,1024]{1,0:T(8,128)(2,1)} %pad_maximum_fusion), channel_id=1, source_target_pairs={{0,1},{1,2},{2,3},{3,4},{4,5},{5,6},{6,7},{7,8},{8,9},{9,10},{10,1... | collective-permute-start | bytes 12779528 | tf_op jit(solution)/shard_map/ppermute | solution.py:16
  17.0 94.0 %collective-permute-start = (bf16[2080,1024]{1,0:T(8,128)(2,1)}, bf16[2080,1024]{1,0:T(8,128)(2,1)}, u32[]{:S(2)}, u32[]{:S(2)}) collective-permute-start(bf16[2080,1024]{1,0:T(8,128)(2,1)} %pad_maximum_fusion), channel_id=1, source_target_pairs={{64,0},{128,64},{192,128},{65,1},{129,65},{193,129},{66,2},{130,66... | collective-permute-start | bytes 12779528 | tf_op jit(solution)/shard_map/ppermute | solution.py:16
  19.1 94.0 %collective-permute-start.1 = (bf16[2080,1024]{1,0:T(8,128)(2,1)}, bf16[2080,1024]{1,0:T(8,128)(2,1)}, u32[]{:S(2)}, u32[]{:S(2)}) collective-permute-start(bf16[2080,1024]{1,0:T(8,128)(2,1)} %pad_maximum_fusion), channel_id=1, source_target_pairs={{0,64},{64,128},{128,192},{1,65},{65,129},{129,193},{2,66},{66,130... | collective-permute-start | bytes 12779528 | tf_op jit(solution)/shard_map/ppermute | solution.py:16
  25.0 41.3 %copy-start.2 = (s32[1,32]{1,0:T(1,128)S(1)}, s32[1,32]{1,0:T(1,128)}, u32[]{:S(2)}) copy-start(s32[1,32]{1,0:T(1,128)} %constant.64.clone.1) | copy-start | bytes 388

commit v5 on v4

--- a/solution.py
+++ b/solution.py
@@ -1,3 +1,5 @@
+import functools
+
 import jax
 import jax.numpy as jnp
 from jax import lax
@@ -117,6 +119,77 @@
     )(*args)
 
 
+def final_kernel(n, tab, own_ref, sqc_ref, sqr_ref, num_ref, den_ref, src0, src1,
+                 out_ref, xp_buf, sem, acc, dacc):
+    b = pl.program_id(0)
+    nloc = sqr_ref.shape[0] // 2
+    width = own_ref.shape[1]
+    acc[...] = num_ref[0]
+    dacc[...] = den_ref[0]
+
+    def body(j, carry):
+        t = tab[j]
+        s = tab[n + j]
+        ix = tab[2 * n + j]
+        hit = (tab[3 * n + j] == 1) & (t == b)
+        rows = pl.ds(pl.multiple_of(ix * BLOCK, BLOCK), BLOCK)
+
+        for k, src in enumerate((src0, src1)):
+            @pl.when(hit & (s == k))
+            def _():
+                cp = pltpu.make_async_copy(src.at[rows], xp_buf, sem.at[0])
+                cp.start()
+                cp.wait()
+
+        @pl.when(hit)
+        def _():
+            xt = own_ref[...]
+            xp = xp_buf[...]
+            inner = lax.dot_general(xt, xp, (((1,), (1,)), ((), ())),
+                                    preferred_element_type=jnp.float32)
+            sq_p = sqr_ref[pl.ds(s * nloc + ix, 1), :]
+            distance = sqc_ref[0] + sq_p - 2.0 * inner
+            w = jnp.exp(-distance / (scale_factor * width)).astype(jnp.bfloat16)
+            acc[...] += jnp.dot(w, xp, preferred_element_type=jnp.float32)
+            dacc[...] += jnp.sum(w.astype(jnp.float32), axis=1, keepdims=True)
+        return carry
+
+    lax.fori_loop(0, n, body, 0)
+    out_ref[0] = (acc[...] / dacc[...]).astype(out_ref.dtype)
+
+
+def run_final(tab, n, own, sq_col, sources, sq_rows, num, den):
+    rows, width = own.shape
+    nloc = rows // BLOCK
+    blk = (1, BLOCK, width)
+    cblk = (1, BLOCK, 1)
+    grid_spec = pltpu.PrefetchScalarGridSpec(
+        num_scalar_prefetch=1,
+        grid=(nloc,),
+        in_specs=[pl.BlockSpec((BLOCK, width), lambda b, tab: (b, 0)),
+                  pl.BlockSpec(cblk, lambda b, tab: (b, 0, 0)),
+                  pl.BlockSpec(memory_space=pltpu.VMEM),
+                  pl.BlockSpec(blk, lambda b, tab: (b, 0, 0)),
+                  pl.BlockSpec(cblk, lambda b, tab: (b, 0, 0)),
+                  pl.BlockSpec(memory_space=pl.ANY),
+                  pl.BlockSpec(memory_space=pl.ANY)],
+        out_specs=pl.BlockSpec(blk, lambda b, tab: (b, 0, 0)),
+        scratch_shapes=[pltpu.VMEM((BLOCK, width), jnp.bfloat16),
+                        pltpu.SemaphoreType.DMA((1,)),
+                        pltpu.VMEM((BLOCK, width), jnp.float32),
+                        pltpu.VMEM((BLOCK, 1), jnp.float32)],
+    )
+    flops = n * 4 * BLOCK * BLOCK * width
+    return pl.pallas_call(
+        functools.partial(final_kernel, n),
+        grid_spec=grid_spec,
+        out_shape=jax.ShapeDtypeStruct((nloc, BLOCK, width), jnp.bfloat16),
+        compiler_params=pltpu.CompilerParams(dimension_semantics=("arbitrary",)),
+        cost_estimate=pl.CostEstimate(flops=flops, transcendentals=n * BLOCK * BLOCK,
+                                      bytes_accessed=nloc * BLOCK * width * 8),
+    )(tab, own, sq_col, sq_rows, num, den, *sources)
+
+
 def encode_meta(own_sq, pair_blocks, pair_count, width):
     nloc = own_sq.shape[0]
     hi = lax.reduce_precision(own_sq, exponent_bits=8, mantissa_bits=7)
@@ -209,7 +282,7 @@
     v3 = jnp.concatenate([used & r_grp, gu])
     tab3 = pack_table(t3, s3, i3, v3, nloc)
     sq3 = jnp.concatenate([sq_ng, sq_pg], axis=0)
-    smoothed = run_phase("final", tab3, t3.shape[0], embeddings, sq_col, [ng, pg], sq3, num, den)
+    smoothed = run_final(tab3, t3.shape[0], embeddings, sq_col, [ng, pg], sq3, num, den)
     return smoothed.reshape(total_rows, width)
 
 

time: 146 us -> 167 us (1.14)
  the two profiles are of different devices: /device:TPU:79 before, /device:TPU:49 now
where the time goes in v5:
time: 167 us; the launch traced here: 165 us
  Pallas kernels  82.3 us (49%)
  waiting for transfers between devices  48.5 us (29%)
  other arithmetic  14.8 us (9%)
  starting transfers between devices  12.9 us (8%)
  local copies, waits for them, and re-layouts  4.87 us (3%)
  between operations  2.26 us (1%)
    ppermute x4, waiting for transfers between devices, shifted(): return lax.ppermute(shard, axis, pairs)  48.5 us
    pallas_call x1, Pallas kernels, run_final(): pl.pallas_call(functools.partial(final_kernel, n), grid_spec=grid_spec, o...  47.7 us
    pallas_call x2, Pallas kernels, run_phase(): pl.pallas_call(make_kernel(nsrc, n, mode), in_specs=in_specs, out_specs=o...  34.6 us
    ppermute x4, starting transfers between devices, shifted(): return lax.ppermute(shard, axis, pairs)  12.9 us
    concatenate x1, other arithmetic, local(): jnp.concatenate([embeddings, encode_meta(own_sq, pair_blocks, pair_count,...  4.62 us
    convert_element_type x4, other arithmetic, decode_meta(): meta = recv[nloc * BLOCK:].astype(jnp.float32)  3.4 us
  transfers between devices with their start and end apart: 4, of which 4 were waited for; matrix products, arithmetic and copies ran while one was open for 4% of the time, Pallas kernels for 21%

profile of v5, /device:TPU:49, one launch (start us, length us, event | category | flops | bytes accessed | tf_op | source)
XLA Modules:
  0.0 165.5 jit_solution(17306140491056105591)
XLA Ops:
  0.7 3.1 %fusion.refs_1_ = f32[8,256]{1,0:T(8,128)S(1)} fusion(bf16[8,256,1024]{2,1,0:T(8,128)(2,1)} %bitcast.33), kind=kLoop, calls=%fused_computation.1 | loop fusion | flops 6289408 | bytes 4202496 | tf_op jit(solution)/shard_map/bsd,bsd->bs/dot_general | solution.py:22
  3.7 0.0 copy-start
  3.8 0.7 broadcast_add_fusion
  4.4 0.1 copy.11
  4.5 0.1 add.116
  4.7 0.0 copy-start.1
  4.7 4.6 %pad_maximum_fusion = bf16[2080,1024]{1,0:T(8,128)(2,1)} fusion(bf16[32,1024]{1,0:T(8,128)(2,1)S(1)} %fusion.8, bf16[2048,1024]{1,0:T(8,128)(2,1)} %own_ref.5), kind=kLoop, calls=%fused_computation.2 | loop fusion | flops 8519680 | bytes 8519680 | tf_op jit(solution)/shard_map/concatenate | solution.py:229
  9.3 2.6 %collective-permute-start.2 = (bf16[2080,1024]{1,0:T(8,128)(2,1)}, bf16[2080,1024]{1,0:T(8,128)(2,1)}, u32[]{:S(2)}, u32[]{:S(2)}) collective-permute-start(bf16[2080,1024]{1,0:T(8,128)(2,1)} %pad_maximum_fusion), channel_id=1, source_target_pairs={{1,0},{2,1},{3,2},{4,3},{5,4},{6,5},{7,6},{8,7},{9,8},{10,9},{11,1... | collective-permute-start | bytes 12779528 | tf_op jit(solution)/shard_map/ppermute | solution.py:18
  11.9 3.0 %collective-permute-start.3 = (bf16[2080,1024]{1,0:T(8,128)(2,1)}, bf16[2080,1024]{1,0:T(8,128)(2,1)}, u32[]{:S(2)}, u32[]{:S(2)}) collective-permute-start(bf16[2080,1024]{1,0:T(8,128)(2,1)} %pad_maximum_fusion), channel_id=1, source_target_pairs={{0,1},{1,2},{2,3},{3,4},{4,5},{5,6},{6,7},{7,8},{8,9},{9,10},{10,1... | collective-permute-start | bytes 12779528 | tf_op jit(solution)/shard_map/ppermute | solution.py:18
  15.0 2.1 %collective-permute-start = (bf16[2080,1024]{1,0:T(8,128)(2,1)}, bf16[2080,1024]{1,0:T(8,128)(2,1)}, u32[]{:S(2)}, u32[]{:S(2)}) collective-permute-start(bf16[2080,1024]{1,0:T(8,128)(2,1)} %pad_maximum_fusion), channel_id=1, source_target_pairs={{64,0},{128,64},{192,128},{65,1},{129,65},{193,129},{66,2},{130,66... | collective-permute-start | bytes 12779528 | tf_op jit(solution)/shard_map/ppermute | solution.py:18
  17.0 5.2 %collective-permute-start.1 = (bf16[2080,1024]{1,0:T(8,128)(2,1)}, bf16[2080,1024]{1,0:T(8,128)(2,1)}, u32[]{:S(2)}, u32[]{:S(2)}) collective-permute-start(bf16[2080,1024]{1,0:T(8,128)(2,1)} %pad_maximum_fusion), channel_id=1, source_target_pairs={{0,64},{64,128},{128,192},{1,65},{65,129},{129,193},{2,66},{66,130... | collective-permute-start | bytes 12779528 | tf_op jit(solution)/shard_map/ppermute | solution.py:18
  22.2 0.0 copy-done.1
  22.3 0.1 copy.12
  22.4 0.1 copy.10
  22.4 0.1 and_reduce_fusion
  22.6 0.1 fusion.21
  22.7 0.1 add_reduce_fusion
  22.8 0.1 add_clamp_fusion
  22.9 0.7 reshape.470.tab
  23.6 0.0 copy-done
  23.6 1.4 copy.13.sqc_ref
  25.0 0.0 copy-start.2
  25.0 16.6 %shard_map.37 = (f32[8,256,1024]{2,1,0:T(8,128)}, f32[8,256,1]{2,1,0:T(8,128)}) custom-call(s32[160]{0:T(256)} %reshape.470.tab, bf16[2048,1024]{1,0:T(8,128)(2,1)} %own_ref.5, f32[8,256,1]{2,1,0:T(8,128)} %copy.13.sqc_ref, bf16[2048,1024]{1,0:T(8,128)(2,1)} %own_ref.5, f32[8,256]{1,0:T(8,128)} %copy-done), custom_call_target="tpu_custom_call" | custom-call | flops 10737418240 | bytes 16777216 | tf_op jit(solution)/shard_map/pallas_call | solution.py:110
  41.5 19.0 %collective-permute-done.2.refs_0_ = bf16[2080,1024]{1,0:T(8,128)(2,1)} collective-permute-done((bf16[2080,1024]{1,0:T(8,128)(2,1)}, bf16[2080,1024]{1,0:T(8,128)(2,1)}, u32[]{:S(2)}, u32[]{:S(2)}) %collective-permute-start.2) | collective-permute-done | bytes 4259872 | tf_op jit(solution)/shard_map/ppermute | solution.py:18
  60.5 0.9 collective-permute-done.3.refs_1_
  61.4 0.8 slice_convert_fusion.3
  62.3 0.6 slice.116
  62.9 0.1 sub.172
  63.7 0.2 fusion.14
  63.8 0.1 add_clamp_fusion.2
  63.9 0.1 add_clamp_fusion.3
  64.0 0.2 compare_reduce_fusion.3
  64.2 0.1 add_convert_fusion
  64.3 0.0 copy-done.2
  64.3 0.6 reshape.471.tab
  64.9 0.8 slice_convert_fusion.2
  65.8 0.6 pad_maximum_fusion.1.refs_2_
  66.4 18.0 %shard_map.38 = (f32[8,256,1024]{2,1,0:T(8,128)}, f32[8,256,1]{2,1,0:T(8,128)}) custom-call(s32[128]{0:T(128)} %reshape.471.tab, bf16[2048,1024]{1,0:T(8,128)(2,1)} %own_ref.5, f32[8,256,1]{2,1,0:T(8,128)} %copy.13.sqc_ref, bf16[2080,1024]{1,0:T(8,128)(2,1)} %collective-permute-done.2.refs_0_, bf16[2080,1024]{1,0:T(8,128)(2,1)} %collective-permute-done.3.refs_1_, ...), custom_call_target="tpu_custom_call" | custom-call | flops 8589934592 | bytes 20971520 | tf_op jit(solution)/shard_map/pallas_call | solution.py:110
  84.3 25.7 %collective-permute-done.src0 = bf16[2080,1024]{1,0:T(8,128)(2,1)} collective-permute-done((bf16[2080,1024]{1,0:T(8,128)(2,1)}, bf16[2080,1024]{1,0:T(8,128)(2,1)}, u32[]{:S(2)}, u32[]{:S(2)}) %collective-permute-start) | collective-permute-done | bytes 4259872 | tf_op jit(solution)/shard_map/ppermute | solution.py:18
  110.1 2.9 %collective-permute-done.1.src1 = bf16[2080,1024]{1,0:T(8,128)(2,1)} collective-permute-done((bf16[2080,1024]{1,0:T(8,128)(2,1)}, bf16[2080,1024]{1,0:T(8,128)(2,1)}, u32[]{:S(2)}, u32[]{:S(2)}) %collective-permute-start.1) | collective-permute-done | bytes 4259872 | tf_op jit(solution)/shard_map/ppermute | solution.py:18
  112.9 0.8 slice_convert_fusion.1
  113.8 0.5 slice.127
  114.3 0.8 slice_convert_fusion
  115.2 0.1 sub.179
  115.3 0.2 compare_reduce_fusion.1
  115.5 0.2 fusion.15
  115.7 0.1 add_clamp_fusion.4
  116.4 0.1 add_clamp_fusion.5
  116.5 0.1 add_convert_fusion.1
  116.6 0.6 reshape.472.tab
  117.2 0.6 pad_maximum_fusion.2.sqr_ref
  117.8 47.7 %shard_map.39 = bf16[8,256,1024]{2,1,0:T(8,128)(2,1)} custom-call(s32[128]{0:T(128)} %reshape.472.tab, bf16[2048,1024]{1,0:T(8,128)(2,1)} %own_ref.5, f32[8,256,1]{2,1,0:T(8,128)} %copy.13.sqc_ref, f32[16,256]{1,0:T(8,128)} %pad_maximum_fusion.2.sqr_ref, f32[8,256,1024]{2,1,0:T(8,128)} %get-tuple-element.27.num_ref, f32[8,256,1]{2,1,0:T(8,128)} %get-tuple-element.28.den_ref, ...), custom_call_target="tpu_custom_call" | custom-call | flops 8589934592 | bytes 16777216 | tf_op jit(solution)/shard_map/pallas_call | solution.py:183
  (23 shorter events, 0.2 us)
Async XLA Ops:
  3.7 19.9 %copy-start = (f32[8,256]{1,0:T(8,128)}, f32[8,256]{1,0:T(8,128)S(1)}, u32[]{:S(2)}) copy-start(f32[8,256]{1,0:T(8,128)S(1)} %fusion.refs_1_) | copy-start | bytes 24580
  4.7 17.5 %copy-start.1 = (s32[16,2]{0,1:T(2,128)S(1)}, s32[16,2]{0,1:T(2,128)}, u32[]{:S(2)}) copy-start(s32[16,2]{0,1:T(2,128)} %param.4) | copy-start | bytes 388
  9.3 51.2 %collective-permute-start.2 = (bf16[2080,1024]{1,0:T(8,128)(2,1)}, bf16[2080,1024]{1,0:T(8,128)(2,1)}, u32[]{:S(2)}, u32[]{:S(2)}) collective-permute-start(bf16[2080,1024]{1,0:T(8,128)(2,1)} %pad_maximum_fusion), channel_id=1, source_target_pairs={{1,0},{2,1},{3,2},{4,3},{5,4},{6,5},{7,6},{8,7},{9,8},{10,9},{11,1... | collective-permute-start | bytes 12779528 | tf_op jit(solution)/shard_map/ppermute | solution.py:18
  11.9 49.5 %collective-permute-start.3 = (bf16[2080,1024]{1,0:T(8,128)(2,1)}, bf16[2080,1024]{1,0:T(8,128)(2,1)}, u32[]{:S(2)}, u32[]{:S(2)}) collective-permute-start(bf16[2080,1024]{1,0:T(8,128)(2,1)} %pad_maximum_fusion), channel_id=1, source_target_pairs={{0,1},{1,2},{2,3},{3,4},{4,5},{5,6},{6,7},{7,8},{8,9},{9,10},{10,1... | collective-permute-start | bytes 12779528 | tf_op jit(solution)/shard_map/ppermute | solution.py:18
  15.0 95.1 %collective-permute-start = (bf16[2080,1024]{1,0:T(8,128)(2,1)}, bf16[2080,1024]{1,0:T(8,128)(2,1)}, u32[]{:S(2)}, u32[]{:S(2)}) collective-permute-start(bf16[2080,1024]{1,0:T(8,128)(2,1)} %pad_maximum_fusion), channel_id=1, source_target_pairs={{64,0},{128,64},{192,128},{65,1},{129,65},{193,129},{66,2},{130,66... | collective-permute-start | bytes 12779528 | tf_op jit(solution)/shard_map/ppermute | solution.py:18
  17.0 95.9 %collective-permute-start.1 = (bf16[2080,1024]{1,0:T(8,128)(2,1)}, bf16[2080,1024]{1,0:T(8,128)(2,1)}, u32[]{:S(2)}, u32[]{:S(2)}) collective-permute-start(bf16[2080,1024]{1,0:T(8,128)(2,1)} %pad_maximum_fusion), channel_id=1, source_target_pairs={{0,64},{64,128},{128,192},{1,65},{65,129},{129,193},{2,66},{66,130... | collective-permute-start | bytes 12779528 | tf_op jit(solution)/shard_map/ppermute | solution.py:18
  25.0 39.3 %copy-start.2 = (s32[1,32]{1,0:T(1,128)S(1)}, s32[1,32]{1,0:T(1,128)}, u32[]{:S(2)}) copy-start(s32[1,32]{1,0:T(1,128)} %constant.64.clone.1) | copy-start | bytes 388

commit v6 on v4

--- a/solution.py
+++ b/solution.py
@@ -36,11 +36,11 @@
         elif mode == "accum":
             num_in, den_in, num_ref, den_ref = rest
         else:
-            num_in, den_in, out_ref, num_ref, den_ref = rest
+            num_in, den_in, out_ref, num_ref, den_ref, xp_buf, sem = rest
         nloc = own_ref.shape[0] // BLOCK
         width = own_ref.shape[1]
 
-        if mode == "accum":
+        if mode != "init":
             num_ref[...] = num_in[...]
             den_ref[...] = den_in[...]
         else:
@@ -64,18 +64,30 @@
             s = tab[n + j]
             ix = tab[2 * n + j]
             used = tab[3 * n + j] == 1
-            for k, p_ref in enumerate(src_refs):
-                @pl.when(used & (s == k))
+            if mode == "final":
+                for k, p_ref in enumerate(src_refs):
+                    @pl.when(used & (s == k))
+                    def _():
+                        rows = pl.ds(pl.multiple_of(ix * BLOCK, BLOCK), BLOCK)
+                        cp = pltpu.make_async_copy(p_ref.at[rows], xp_buf, sem.at[0])
+                        cp.start()
+                        cp.wait()
+
+                @pl.when(used)
                 def _():
-                    contribute(t, k * nloc + ix, p_ref, ix)
+                    contribute(t, s * nloc + ix, xp_buf, 0)
+            else:
+                for k, p_ref in enumerate(src_refs):
+                    @pl.when(used & (s == k))
+                    def _():
+                        contribute(t, k * nloc + ix, p_ref, ix)
             return carry
 
         lax.fori_loop(0, n, body, 0)
 
         if mode == "final":
             def fin(b, carry):
-                out_ref[b] = ((num_in[b] + num_ref[b]) / (den_in[b] + den_ref[b])).astype(
-                    out_ref.dtype)
+                out_ref[b] = (num_ref[b] / den_ref[b]).astype(out_ref.dtype)
                 return carry
             lax.fori_loop(0, nloc, fin, 0)
 
@@ -88,7 +100,8 @@
     nloc = rows // block
     nsrc = len(sources)
     vm = pl.BlockSpec(memory_space=pltpu.VMEM)
-    in_specs = [pl.BlockSpec(memory_space=pltpu.SMEM), vm, vm] + [vm] * nsrc + [vm]
+    src_space = pl.BlockSpec(memory_space=pl.ANY) if mode == "final" else vm
+    in_specs = [pl.BlockSpec(memory_space=pltpu.SMEM), vm, vm] + [src_space] * nsrc + [vm]
     args = [tab, own, sq_col, *sources, sq_rows]
     acc_shapes = [jax.ShapeDtypeStruct((nloc, block, width), jnp.float32),
                   jax.ShapeDtypeStruct((nloc, block, 1), jnp.float32)]
@@ -100,7 +113,9 @@
         out_shape = jax.ShapeDtypeStruct((nloc, block, width), jnp.bfloat16)
         out_specs = vm
         scratch = [pltpu.VMEM((nloc, block, width), jnp.float32),
-                   pltpu.VMEM((nloc, block, 1), jnp.float32)]
+                   pltpu.VMEM((nloc, block, 1), jnp.float32),
+                   pltpu.VMEM((block, width), jnp.bfloat16),
+                   pltpu.SemaphoreType.DMA((1,))]
     else:
         out_shape = acc_shapes
         out_specs = [vm, vm]

time: 146 us -> 158 us (1.082)
  the two profiles are of different devices: /device:TPU:79 before, /device:TPU:239 now
where the time goes in v6:
time: 158 us; the launch traced here: 157 us
  Pallas kernels  72.6 us (46%)
  waiting for transfers between devices  51.2 us (32%)
  other arithmetic  14.8 us (9%)
  starting transfers between devices  11.2 us (7%)
  local copies, waits for them, and re-layouts  4.87 us (3%)
  between operations  2.25 us (1%)
    pallas_call x3, Pallas kernels, run_phase(): pl.pallas_call(make_kernel(nsrc, n, mode), in_specs=in_specs, out_specs=o...  72.6 us
    ppermute x4, waiting for transfers between devices, shifted(): return lax.ppermute(shard, axis, pairs)  51.2 us
    ppermute x4, starting transfers between devices, shifted(): return lax.ppermute(shard, axis, pairs)  11.2 us
    concatenate x1, other arithmetic, local(): jnp.concatenate([embeddings, encode_meta(own_sq, pair_blocks, pair_count,...  4.62 us
    convert_element_type x4, other arithmetic, decode_meta(): meta = recv[nloc * BLOCK:].astype(jnp.float32)  3.4 us
  transfers between devices with their start and end apart: 4, of which 2 were waited for; matrix products, arithmetic and copies ran while one was open for 4% of the time, Pallas kernels for 21%

profile of v6, /device:TPU:239, one launch (start us, length us, event | category | flops | bytes accessed | tf_op | source)
XLA Modules:
  0.0 157.0 jit_solution(5999315960707560391)
XLA Ops:
  0.7 3.1 %fusion.refs_1_ = f32[8,256]{1,0:T(8,128)S(1)} fusion(bf16[8,256,1024]{2,1,0:T(8,128)(2,1)} %bitcast.33), kind=kLoop, calls=%fused_computation.1 | loop fusion | flops 6289408 | bytes 4202496 | tf_op jit(solution)/shard_map/bsd,bsd->bs/dot_general | solution.py:20
  3.7 0.0 copy-start
  3.8 0.7 broadcast_add_fusion
  4.4 0.1 copy.11
  4.5 0.1 add.116
  4.7 0.0 copy-start.1
  4.7 4.6 %pad_maximum_fusion = bf16[2080,1024]{1,0:T(8,128)(2,1)} fusion(bf16[32,1024]{1,0:T(8,128)(2,1)S(1)} %fusion.8, bf16[2048,1024]{1,0:T(8,128)(2,1)} %own_ref.5), kind=kLoop, calls=%fused_computation.2 | loop fusion | flops 8519680 | bytes 8519680 | tf_op jit(solution)/shard_map/concatenate | solution.py:171
  9.3 4.7 %collective-permute-start.2 = (bf16[2080,1024]{1,0:T(8,128)(2,1)}, bf16[2080,1024]{1,0:T(8,128)(2,1)}, u32[]{:S(2)}, u32[]{:S(2)}) collective-permute-start(bf16[2080,1024]{1,0:T(8,128)(2,1)} %pad_maximum_fusion), channel_id=1, source_target_pairs={{1,0},{2,1},{3,2},{4,3},{5,4},{6,5},{7,6},{8,7},{9,8},{10,9},{11,1... | collective-permute-start | bytes 12779528 | tf_op jit(solution)/shard_map/ppermute | solution.py:16
  14.0 1.3 collective-permute-start.3
  15.3 2.1 %collective-permute-start = (bf16[2080,1024]{1,0:T(8,128)(2,1)}, bf16[2080,1024]{1,0:T(8,128)(2,1)}, u32[]{:S(2)}, u32[]{:S(2)}) collective-permute-start(bf16[2080,1024]{1,0:T(8,128)(2,1)} %pad_maximum_fusion), channel_id=1, source_target_pairs={{64,0},{128,64},{192,128},{65,1},{129,65},{193,129},{66,2},{130,66... | collective-permute-start | bytes 12779528 | tf_op jit(solution)/shard_map/ppermute | solution.py:16
  17.4 3.2 %collective-permute-start.1 = (bf16[2080,1024]{1,0:T(8,128)(2,1)}, bf16[2080,1024]{1,0:T(8,128)(2,1)}, u32[]{:S(2)}, u32[]{:S(2)}) collective-permute-start(bf16[2080,1024]{1,0:T(8,128)(2,1)} %pad_maximum_fusion), channel_id=1, source_target_pairs={{0,64},{64,128},{128,192},{1,65},{65,129},{129,193},{2,66},{66,130... | collective-permute-start | bytes 12779528 | tf_op jit(solution)/shard_map/ppermute | solution.py:16
  20.6 0.0 copy-done.1
  20.6 0.1 copy.12
  20.7 0.1 copy.10
  20.8 0.1 and_reduce_fusion
  21.0 0.1 fusion.21
  21.0 0.1 add_reduce_fusion
  21.2 0.1 add_clamp_fusion
  21.3 0.7 reshape.470.tab
  21.9 0.0 copy-done
  21.9 1.4 copy.13.sqc_ref
  23.3 0.0 copy-start.2
  23.3 16.6 %shard_map.37 = (f32[8,256,1024]{2,1,0:T(8,128)}, f32[8,256,1]{2,1,0:T(8,128)}) custom-call(s32[160]{0:T(256)} %reshape.470.tab, bf16[2048,1024]{1,0:T(8,128)(2,1)} %own_ref.5, f32[8,256,1]{2,1,0:T(8,128)} %copy.13.sqc_ref, bf16[2048,1024]{1,0:T(8,128)(2,1)} %own_ref.5, f32[8,256]{1,0:T(8,128)} %copy-done), custom_call_target="tpu_custom_call" | custom-call | flops 10737418240 | bytes 16777216 | tf_op jit(solution)/shard_map/pallas_call | solution.py:123
  39.9 0.0 collective-permute-done.2.refs_0_
  39.9 0.0 collective-permute-done.3.refs_1_
  39.9 0.9 slice_convert_fusion.3
  40.8 0.6 slice.116
  41.4 0.1 sub.172
  42.2 0.2 fusion.14
  42.4 0.1 add_clamp_fusion.2
  42.4 0.1 add_clamp_fusion.3
  42.5 0.2 compare_reduce_fusion.3
  42.7 0.1 add_convert_fusion
  42.8 0.0 copy-done.2
  42.8 0.6 reshape.471.tab
  43.4 0.8 slice_convert_fusion.2
  44.3 0.6 pad_maximum_fusion.1.refs_2_
  44.9 15.6 %shard_map.38 = (f32[8,256,1024]{2,1,0:T(8,128)}, f32[8,256,1]{2,1,0:T(8,128)}) custom-call(s32[128]{0:T(128)} %reshape.471.tab, bf16[2048,1024]{1,0:T(8,128)(2,1)} %own_ref.5, f32[8,256,1]{2,1,0:T(8,128)} %copy.13.sqc_ref, bf16[2080,1024]{1,0:T(8,128)(2,1)} %collective-permute-done.2.refs_0_, bf16[2080,1024]{1,0:T(8,128)(2,1)} %collective-permute-done.3.refs_1_, ...), custom_call_target="tpu_custom_call" | custom-call | flops 8589934592 | bytes 20971520 | tf_op jit(solution)/shard_map/pallas_call | solution.py:123
  60.5 49.4 %collective-permute-done.refs_0_ = bf16[2080,1024]{1,0:T(8,128)(2,1)} collective-permute-done((bf16[2080,1024]{1,0:T(8,128)(2,1)}, bf16[2080,1024]{1,0:T(8,128)(2,1)}, u32[]{:S(2)}, u32[]{:S(2)}) %collective-permute-start) | collective-permute-done | bytes 4259872 | tf_op jit(solution)/shard_map/ppermute | solution.py:16
  109.9 1.8 %collective-permute-done.1.refs_1_ = bf16[2080,1024]{1,0:T(8,128)(2,1)} collective-permute-done((bf16[2080,1024]{1,0:T(8,128)(2,1)}, bf16[2080,1024]{1,0:T(8,128)(2,1)}, u32[]{:S(2)}, u32[]{:S(2)}) %collective-permute-start.1) | collective-permute-done | bytes 4259872 | tf_op jit(solution)/shard_map/ppermute | solution.py:16
  111.7 0.8 slice_convert_fusion.1
  112.6 0.5 slice.127
  113.1 0.8 slice_convert_fusion
  114.0 0.1 sub.179
  114.1 0.2 compare_reduce_fusion.1
  114.3 0.2 fusion.15
  114.5 0.1 add_clamp_fusion.4
  115.2 0.1 add_clamp_fusion.5
  115.3 0.1 add_convert_fusion.1
  115.4 0.6 reshape.472.tab
  116.0 0.6 pad_maximum_fusion.2.refs_2_
  116.6 40.4 %shard_map.39 = bf16[8,256,1024]{2,1,0:T(8,128)(2,1)} custom-call(s32[128]{0:T(128)} %reshape.472.tab, bf16[2048,1024]{1,0:T(8,128)(2,1)} %own_ref.5, f32[8,256,1]{2,1,0:T(8,128)} %copy.13.sqc_ref, bf16[2080,1024]{1,0:T(8,128)(2,1)} %collective-permute-done.refs_0_, bf16[2080,1024]{1,0:T(8,128)(2,1)} %collective-permute-done.1.refs_1_, ...), custom_call_target="tpu_custom_call" | custom-call | flops 8589934592 | bytes 20971520 | tf_op jit(solution)/shard_map/pallas_call | solution.py:123
  (23 shorter events, 0.2 us)
Async XLA Ops:
  3.7 18.2 %copy-start = (f32[8,256]{1,0:T(8,128)}, f32[8,256]{1,0:T(8,128)S(1)}, u32[]{:S(2)}) copy-start(f32[8,256]{1,0:T(8,128)S(1)} %fusion.refs_1_) | copy-start | bytes 24580
  4.7 15.9 %copy-start.1 = (s32[16,2]{0,1:T(2,128)S(1)}, s32[16,2]{0,1:T(2,128)}, u32[]{:S(2)}) copy-start(s32[16,2]{0,1:T(2,128)} %param.4) | copy-start | bytes 388
  9.3 30.6 %collective-permute-start.2 = (bf16[2080,1024]{1,0:T(8,128)(2,1)}, bf16[2080,1024]{1,0:T(8,128)(2,1)}, u32[]{:S(2)}, u32[]{:S(2)}) collective-permute-start(bf16[2080,1024]{1,0:T(8,128)(2,1)} %pad_maximum_fusion), channel_id=1, source_target_pairs={{1,0},{2,1},{3,2},{4,3},{5,4},{6,5},{7,6},{8,7},{9,8},{10,9},{11,1... | collective-permute-start | bytes 12779528 | tf_op jit(solution)/shard_map/ppermute | solution.py:16
  14.0 25.9 %collective-permute-start.3 = (bf16[2080,1024]{1,0:T(8,128)(2,1)}, bf16[2080,1024]{1,0:T(8,128)(2,1)}, u32[]{:S(2)}, u32[]{:S(2)}) collective-permute-start(bf16[2080,1024]{1,0:T(8,128)(2,1)} %pad_maximum_fusion), channel_id=1, source_target_pairs={{0,1},{1,2},{2,3},{3,4},{4,5},{5,6},{6,7},{7,8},{8,9},{9,10},{10,1... | collective-permute-start | bytes 12779528 | tf_op jit(solution)/shard_map/ppermute | solution.py:16
  15.3 94.6 %collective-permute-start = (bf16[2080,1024]{1,0:T(8,128)(2,1)}, bf16[2080,1024]{1,0:T(8,128)(2,1)}, u32[]{:S(2)}, u32[]{:S(2)}) collective-permute-start(bf16[2080,1024]{1,0:T(8,128)(2,1)} %pad_maximum_fusion), channel_id=1, source_target_pairs={{64,0},{128,64},{192,128},{65,1},{129,65},{193,129},{66,2},{130,66... | collective-permute-start | bytes 12779528 | tf_op jit(solution)/shard_map/ppermute | solution.py:16
  17.4 94.3 %collective-permute-start.1 = (bf16[2080,1024]{1,0:T(8,128)(2,1)}, bf16[2080,1024]{1,0:T(8,128)(2,1)}, u32[]{:S(2)}, u32[]{:S(2)}) collective-permute-start(bf16[2080,1024]{1,0:T(8,128)(2,1)} %pad_maximum_fusion), channel_id=1, source_target_pairs={{0,64},{64,128},{128,192},{1,65},{65,129},{129,193},{2,66},{66,130... | collective-permute-start | bytes 12779528 | tf_op jit(solution)/shard_map/ppermute | solution.py:16
  23.3 19.5 %copy-start.2 = (s32[1,32]{1,0:T(1,128)S(1)}, s32[1,32]{1,0:T(1,128)}, u32[]{:S(2)}) copy-start(s32[1,32]{1,0:T(1,128)} %constant.64.clone.1) | copy-start | bytes 388

commit v7 on v4

--- a/solution.py
+++ b/solution.py
@@ -117,30 +117,11 @@
     )(*args)
 
 
-def encode_meta(own_sq, pair_blocks, pair_count, width):
-    nloc = own_sq.shape[0]
-    hi = lax.reduce_precision(own_sq, exponent_bits=8, mantissa_bits=7)
-    r1 = own_sq - hi
-    mid = lax.reduce_precision(r1, exponent_bits=8, mantissa_bits=7)
-    lo = r1 - mid
-    pieces = jnp.concatenate([hi, mid, lo], axis=0)
-    pieces = jnp.pad(pieces, ((0, 0), (0, width - pieces.shape[1])))
-    ids = pair_blocks.reshape(1, -1) + 1
-    ints = jnp.concatenate([ids // 64, ids % 64], axis=0)
-    ints = jnp.pad(ints, ((0, 0), (0, width - ints.shape[1])))
-    cnt = jnp.pad(pair_count.reshape(1, 1), ((0, 0), (0, width - 1)))
-    meta = jnp.concatenate([pieces, ints.astype(jnp.float32), cnt.astype(jnp.float32)], axis=0)
-    pad_rows = -meta.shape[0] % 16
-    meta = jnp.pad(meta, ((0, pad_rows), (0, 0)))
-    return meta.astype(jnp.bfloat16)
-
-
-def decode_meta(recv, nloc, slots):
-    meta = recv[nloc * BLOCK:].astype(jnp.float32)
-    sq = (meta[:nloc, :BLOCK] + meta[nloc:2 * nloc, :BLOCK]) + meta[2 * nloc:3 * nloc, :BLOCK]
-    ids = meta[3 * nloc, :2 * slots] * 64.0 + meta[3 * nloc + 1, :2 * slots]
-    pairs = ids.astype(jnp.int32).reshape(slots, 2) - 1
-    count = meta[3 * nloc + 2, :1].astype(jnp.int32)
+def decode_meta(m, nloc, slots):
+    nsq = nloc * BLOCK
+    sq = m[:nsq].reshape(nloc, BLOCK)
+    pairs = m[nsq:nsq + 2 * slots].astype(jnp.int32).reshape(slots, 2)
+    count = m[nsq + 2 * slots:].astype(jnp.int32)
     return sq, pairs, count
 
 
@@ -152,13 +133,18 @@
     owners = lax.axis_size("dev")
     first_block = (lax.axis_index("group") * owners + lax.axis_index("dev")) * nloc
 
+    nd = shifted(embeddings, "dev", -1)
+    pd = shifted(embeddings, "dev", 1)
+    ng = shifted(embeddings, "group", -1)
+    pg = shifted(embeddings, "group", 1)
     own_sq = squares_of(blocks)
-    payload = jnp.concatenate(
-        [embeddings, encode_meta(own_sq, pair_blocks, pair_count, width)], axis=0)
-    nd = shifted(payload, "dev", -1)
-    pd = shifted(payload, "dev", 1)
-    ng = shifted(payload, "group", -1)
-    pg = shifted(payload, "group", 1)
+    meta = jnp.concatenate([own_sq.reshape(-1),
+                            pair_blocks.reshape(-1).astype(jnp.float32),
+                            pair_count.astype(jnp.float32)])
+    m_nd = shifted(meta, "dev", -1)
+    m_pd = shifted(meta, "dev", 1)
+    m_ng = shifted(meta, "group", -1)
+    m_pg = shifted(meta, "group", 1)
 
     pos = jnp.arange(slots, dtype=jnp.int32)
     used = pos < pair_count[0]
@@ -187,9 +173,9 @@
         u = u & (r >= 0) & (r < nloc)
         return r, pairs[:, 0] - prev_first, u
 
-    nd, pd, num, den = lax.optimization_barrier((nd, pd, num, den))
-    sq_nd, _, _ = decode_meta(nd, nloc, slots)
-    sq_pd, pd_pairs, pd_count = decode_meta(pd, nloc, slots)
+    nd, pd, m_nd, m_pd, num, den = lax.optimization_barrier((nd, pd, m_nd, m_pd, num, den))
+    sq_nd, _, _ = decode_meta(m_nd, nloc, slots)
+    sq_pd, pd_pairs, pd_count = decode_meta(m_pd, nloc, slots)
     pr, pi, pu = prev_entries(pd_pairs, pd_count, first_block - nloc)
     t2 = jnp.concatenate([left, pr])
     s2 = jnp.concatenate([zeros, ones])
@@ -199,9 +185,9 @@
     sq2 = jnp.concatenate([sq_nd, sq_pd], axis=0)
     num, den = run_phase("accum", tab2, t2.shape[0], embeddings, sq_col, [nd, pd], sq2, num, den)
 
-    ng, pg, num, den = lax.optimization_barrier((ng, pg, num, den))
-    sq_ng, _, _ = decode_meta(ng, nloc, slots)
-    sq_pg, pg_pairs, pg_count = decode_meta(pg, nloc, slots)
+    ng, pg, m_ng, m_pg, num, den = lax.optimization_barrier((ng, pg, m_ng, m_pg, num, den))
+    sq_ng, _, _ = decode_meta(m_ng, nloc, slots)
+    sq_pg, pg_pairs, pg_count = decode_meta(m_pg, nloc, slots)
     gr, gi, gu = prev_entries(pg_pairs, pg_count, first_block - owners * nloc)
     t3 = jnp.concatenate([left, gr])
     s3 = jnp.concatenate([zeros, ones])

time: 146 us -> 136 us (0.932)
  the two profiles are of different devices: /device:TPU:79 before, /device:TPU:22 now
where the time goes in v7:
time: 136 us; the launch traced here: 135 us
  Pallas kernels  62.4 us (46%)
  starting transfers between devices  32.8 us (24%)
  waiting for transfers between devices  26.8 us (20%)
  other arithmetic  5.97 us (4%)
  local copies, waits for them, and re-layouts  5.19 us (4%)
  between operations  2.29 us (2%)
    pallas_call x3, Pallas kernels, run_phase(): pl.pallas_call(make_kernel(nsrc, n, mode), in_specs=in_specs, out_specs=o...  62.4 us
    ppermute x8, starting transfers between devices, shifted(): return lax.ppermute(shard, axis, pairs)  32.8 us
    ppermute x8, waiting for transfers between devices, shifted(): return lax.ppermute(shard, axis, pairs)  26.8 us
    dot_general x1, other arithmetic, squares_of(): jnp.einsum('bsd,bsd->bs', blocks, blocks, preferred_element_type=jnp.floa...  3.08 us
  transfers between devices with their start and end apart: 8, of which 1 were waited for; matrix products, arithmetic and copies ran while one was open for 6% of the time, Pallas kernels for 32%

profile of v7, /device:TPU:22, one launch (start us, length us, event | category | flops | bytes accessed | tf_op | source)
XLA Modules:
  0.0 135.5 jit_solution(1317118873285227116)
XLA Ops:
  0.0 0.0 copy-start.1
  0.0 2.3 %collective-permute-start.4 = (bf16[2048,1024]{1,0:T(8,128)(2,1)}, bf16[2048,1024]{1,0:T(8,128)(2,1)}, u32[]{:S(2)}, u32[]{:S(2)}) collective-permute-start(bf16[2048,1024]{1,0:T(8,128)(2,1)} %own_ref.5), channel_id=1, source_target_pairs={{1,0},{2,1},{3,2},{4,3},{5,4},{6,5},{7,6},{8,7},{9,8},{10,9},{11,1... | collective-permute-start | bytes 12582920 | tf_op jit(solution)/shard_map/ppermute | solution.py:16
  2.3 2.2 %collective-permute-start.5 = (bf16[2048,1024]{1,0:T(8,128)(2,1)}, bf16[2048,1024]{1,0:T(8,128)(2,1)}, u32[]{:S(2)}, u32[]{:S(2)}) collective-permute-start(bf16[2048,1024]{1,0:T(8,128)(2,1)} %own_ref.5), channel_id=1, source_target_pairs={{0,1},{1,2},{2,3},{3,4},{4,5},{5,6},{6,7},{7,8},{8,9},{9,10},{10,1... | collective-permute-start | bytes 12582920 | tf_op jit(solution)/shard_map/ppermute | solution.py:16
  4.5 2.4 %collective-permute-start = (bf16[2048,1024]{1,0:T(8,128)(2,1)}, bf16[2048,1024]{1,0:T(8,128)(2,1)}, u32[]{:S(2)}, u32[]{:S(2)}) collective-permute-start(bf16[2048,1024]{1,0:T(8,128)(2,1)} %own_ref.5), channel_id=1, source_target_pairs={{64,0},{128,64},{192,128},{65,1},{129,65},{193,129},{66,2},{130,66... | collective-permute-start | bytes 12582920 | tf_op jit(solution)/shard_map/ppermute | solution.py:16
  6.8 5.4 %collective-permute-start.1 = (bf16[2048,1024]{1,0:T(8,128)(2,1)}, bf16[2048,1024]{1,0:T(8,128)(2,1)}, u32[]{:S(2)}, u32[]{:S(2)}) collective-permute-start(bf16[2048,1024]{1,0:T(8,128)(2,1)} %own_ref.5), channel_id=1, source_target_pairs={{0,64},{64,128},{128,192},{1,65},{65,129},{129,193},{2,66},{66,130... | collective-permute-start | bytes 12582920 | tf_op jit(solution)/shard_map/ppermute | solution.py:16
  12.2 3.1 %fusion.refs_1_ = f32[8,256]{1,0:T(8,128)S(1)} fusion(bf16[8,256,1024]{2,1,0:T(8,128)(2,1)} %bitcast.33), kind=kLoop, calls=%fused_computation.1 | loop fusion | flops 6289408 | bytes 4202496 | tf_op jit(solution)/shard_map/bsd,bsd->bs/dot_general | solution.py:20
  15.3 0.0 copy-start
  16.0 0.0 copy-done.1
  16.0 0.1 copy.8
  16.1 0.1 convert_element_type.60
  16.2 0.1 concatenate.128
  16.3 2.8 %collective-permute-start.6 = (f32[2081]{0:T(1024)S(1)}, f32[2081]{0:T(1024)S(1)}, u32[]{:S(2)}, u32[]{:S(2)}) collective-permute-start(f32[2081]{0:T(1024)S(1)} %concatenate.128), channel_id=1, source_target_pairs={{1,0},{2,1},{3,2},{4,3},{5,4},{6,5},{7,6},{8,7},{9,8},{10,9},{11,1... | collective-permute-start | bytes 24980 | tf_op jit(solution)/shard_map/ppermute | solution.py:16
  19.2 0.1 copy.9
  19.2 0.1 copy.7
  19.3 0.1 and_reduce_fusion
  19.5 0.1 fusion.10
  19.5 0.1 add_reduce_fusion
  19.7 0.1 add_clamp_fusion
  19.8 0.7 reshape.361.tab
  20.5 1.4 %copy.10.sqc_ref = f32[8,256,1]{2,1,0:T(8,128)} copy(f32[8,256,1]{1,0,2:T(8,128)S(1)} %bitcast.35) | data formatting | bytes 16384 | tf_op jit(solution)/shard_map/broadcast_in_dim | solution.py:161
  21.8 0.0 copy-start.2
  21.8 26.8 %collective-permute-done.6 = f32[2081]{0:T(1024)S(1)} collective-permute-done((f32[2081]{0:T(1024)S(1)}, f32[2081]{0:T(1024)S(1)}, u32[]{:S(2)}, u32[]{:S(2)}) %collective-permute-start.6) | collective-permute-done | bytes 8356 | tf_op jit(solution)/shard_map/ppermute | solution.py:16
  48.7 5.5 %collective-permute-start.7 = (f32[2081]{0:T(1024)S(1)}, f32[2081]{0:T(1024)S(1)}, u32[]{:S(2)}, u32[]{:S(2)}) collective-permute-start(f32[2081]{0:T(1024)S(1)} %concatenate.128), channel_id=1, source_target_pairs={{0,1},{1,2},{2,3},{3,4},{4,5},{5,6},{6,7},{7,8},{8,9},{9,10},{10,1... | collective-permute-start | bytes 24980 | tf_op jit(solution)/shard_map/ppermute | solution.py:16
  54.1 0.0 copy-done
  54.2 18.2 %shard_map.37 = (f32[8,256,1024]{2,1,0:T(8,128)}, f32[8,256,1]{2,1,0:T(8,128)}) custom-call(s32[160]{0:T(256)} %reshape.361.tab, bf16[2048,1024]{1,0:T(8,128)(2,1)} %own_ref.5, f32[8,256,1]{2,1,0:T(8,128)} %copy.10.sqc_ref, bf16[2048,1024]{1,0:T(8,128)(2,1)} %own_ref.5, f32[8,256]{1,0:T(8,128)} %copy-done), custom_call_target="tpu_custom_call" | custom-call | flops 10737418240 | bytes 16777216 | tf_op jit(solution)/shard_map/pallas_call | solution.py:108
  72.3 0.0 collective-permute-done.7
  72.3 1.9 %collective-permute-start.2 = (f32[2081]{0:T(1024)S(1)}, f32[2081]{0:T(1024)S(1)}, u32[]{:S(2)}, u32[]{:S(2)}) collective-permute-start(f32[2081]{0:T(1024)S(1)} %concatenate.128), channel_id=1, source_target_pairs={{64,0},{128,64},{192,128},{65,1},{129,65},{193,129},{66,2},{130,66... | collective-permute-start | bytes 24980 | tf_op jit(solution)/shard_map/ppermute | solution.py:16
  74.2 0.0 collective-permute-done.4.refs_0_
  74.2 10.4 %collective-permute-start.3 = (f32[2081]{0:T(1024)S(1)}, f32[2081]{0:T(1024)S(1)}, u32[]{:S(2)}, u32[]{:S(2)}) collective-permute-start(f32[2081]{0:T(1024)S(1)} %concatenate.128), channel_id=1, source_target_pairs={{0,64},{64,128},{128,192},{1,65},{65,129},{129,193},{2,66},{66,130... | collective-permute-start | bytes 24980 | tf_op jit(solution)/shard_map/ppermute | solution.py:16
  84.6 0.0 collective-permute-done.5.refs_1_
  84.7 0.7 slice.47
  85.4 0.1 convert_element_type.64
  86.1 0.2 fusion.3
  86.3 0.1 add_clamp_fusion.2
  86.4 0.1 add_clamp_fusion.3
  86.5 0.2 compare_reduce_fusion.3
  86.7 0.1 add_convert_fusion
  86.8 0.0 copy-done.2
  86.8 0.7 reshape.362.tab
  87.5 0.6 pad_maximum_fusion.refs_2_
  88.1 25.0 %shard_map.38 = (f32[8,256,1024]{2,1,0:T(8,128)}, f32[8,256,1]{2,1,0:T(8,128)}) custom-call(s32[128]{0:T(128)} %reshape.362.tab, bf16[2048,1024]{1,0:T(8,128)(2,1)} %own_ref.5, f32[8,256,1]{2,1,0:T(8,128)} %copy.10.sqc_ref, bf16[2048,1024]{1,0:T(8,128)(2,1)} %collective-permute-done.4.refs_0_, bf16[2048,1024]{1,0:T(8,128)(2,1)} %collective-permute-done.5.refs_1_, ...), custom_call_target="tpu_custom_call" | custom-call | flops 8589934592 | bytes 20971520 | tf_op jit(solution)/shard_map/pallas_call | solution.py:108
  113.0 0.0 collective-permute-done.2
  113.0 0.0 collective-permute-done.3
  113.0 0.0 collective-permute-done.refs_0_
  113.1 0.0 collective-permute-done.1.refs_1_
  113.1 0.6 slice.53
  113.7 0.1 convert_element_type.68
  113.8 0.2 compare_reduce_fusion.1
  114.0 0.2 fusion.4
  114.1 0.1 add_clamp_fusion.4
  114.9 0.1 add_clamp_fusion.5
  115.0 0.1 add_convert_fusion.1
  115.1 0.6 reshape.365.tab
  115.7 0.6 pad_maximum_fusion.1.refs_2_
  116.3 19.2 %shard_map.39 = bf16[8,256,1024]{2,1,0:T(8,128)(2,1)} custom-call(s32[128]{0:T(128)} %reshape.365.tab, bf16[2048,1024]{1,0:T(8,128)(2,1)} %own_ref.5, f32[8,256,1]{2,1,0:T(8,128)} %copy.10.sqc_ref, bf16[2048,1024]{1,0:T(8,128)(2,1)} %collective-permute-done.refs_0_, bf16[2048,1024]{1,0:T(8,128)(2,1)} %collective-permute-done.1.refs_1_, ...), custom_call_target="tpu_custom_call" | custom-call | flops 8589934592 | bytes 20971520 | tf_op jit(solution)/shard_map/pallas_call | solution.py:108
  (22 shorter events, 0.1 us)
Async XLA Ops:
  0.0 16.0 %copy-start.1 = (s32[16,2]{0,1:T(2,128)S(1)}, s32[16,2]{0,1:T(2,128)}, u32[]{:S(2)}) copy-start(s32[16,2]{0,1:T(2,128)} %param.4) | copy-start | bytes 388
  0.0 74.2 %collective-permute-start.4 = (bf16[2048,1024]{1,0:T(8,128)(2,1)}, bf16[2048,1024]{1,0:T(8,128)(2,1)}, u32[]{:S(2)}, u32[]{:S(2)}) collective-permute-start(bf16[2048,1024]{1,0:T(8,128)(2,1)} %own_ref.5), channel_id=1, source_target_pairs={{1,0},{2,1},{3,2},{4,3},{5,4},{6,5},{7,6},{8,7},{9,8},{10,9},{11,1... | collective-permute-start | bytes 12582920 | tf_op jit(solution)/shard_map/ppermute | solution.py:16
  2.3 82.3 %collective-permute-start.5 = (bf16[2048,1024]{1,0:T(8,128)(2,1)}, bf16[2048,1024]{1,0:T(8,128)(2,1)}, u32[]{:S(2)}, u32[]{:S(2)}) collective-permute-start(bf16[2048,1024]{1,0:T(8,128)(2,1)} %own_ref.5), channel_id=1, source_target_pairs={{0,1},{1,2},{2,3},{3,4},{4,5},{5,6},{6,7},{7,8},{8,9},{9,10},{10,1... | collective-permute-start | bytes 12582920 | tf_op jit(solution)/shard_map/ppermute | solution.py:16
  4.5 108.6 %collective-permute-start = (bf16[2048,1024]{1,0:T(8,128)(2,1)}, bf16[2048,1024]{1,0:T(8,128)(2,1)}, u32[]{:S(2)}, u32[]{:S(2)}) collective-permute-start(bf16[2048,1024]{1,0:T(8,128)(2,1)} %own_ref.5), channel_id=1, source_target_pairs={{64,0},{128,64},{192,128},{65,1},{129,65},{193,129},{66,2},{130,66... | collective-permute-start | bytes 12582920 | tf_op jit(solution)/shard_map/ppermute | solution.py:16
  6.8 106.2 %collective-permute-start.1 = (bf16[2048,1024]{1,0:T(8,128)(2,1)}, bf16[2048,1024]{1,0:T(8,128)(2,1)}, u32[]{:S(2)}, u32[]{:S(2)}) collective-permute-start(bf16[2048,1024]{1,0:T(8,128)(2,1)} %own_ref.5), channel_id=1, source_target_pairs={{0,64},{64,128},{128,192},{1,65},{65,129},{129,193},{2,66},{66,130... | collective-permute-start | bytes 12582920 | tf_op jit(solution)/shard_map/ppermute | solution.py:16
  15.3 38.8 %copy-start = (f32[8,256]{1,0:T(8,128)}, f32[8,256]{1,0:T(8,128)S(1)}, u32[]{:S(2)}) copy-start(f32[8,256]{1,0:T(8,128)S(1)} %fusion.refs_1_) | copy-start | bytes 24580
  16.3 32.4 %collective-permute-start.6 = (f32[2081]{0:T(1024)S(1)}, f32[2081]{0:T(1024)S(1)}, u32[]{:S(2)}, u32[]{:S(2)}) collective-permute-start(f32[2081]{0:T(1024)S(1)} %concatenate.128), channel_id=1, source_target_pairs={{1,0},{2,1},{3,2},{4,3},{5,4},{6,5},{7,6},{8,7},{9,8},{10,9},{11,1... | collective-permute-start | bytes 24980 | tf_op jit(solution)/shard_map/ppermute | solution.py:16
  21.8 64.9 %copy-start.2 = (s32[1,32]{1,0:T(1,128)S(1)}, s32[1,32]{1,0:T(1,128)}, u32[]{:S(2)}) copy-start(s32[1,32]{1,0:T(1,128)} %constant.30.clone.1) | copy-start | bytes 388
  48.7 23.7 %collective-permute-start.7 = (f32[2081]{0:T(1024)S(1)}, f32[2081]{0:T(1024)S(1)}, u32[]{:S(2)}, u32[]{:S(2)}) collective-permute-start(f32[2081]{0:T(1024)S(1)} %concatenate.128), channel_id=1, source_target_pairs={{0,1},{1,2},{2,3},{3,4},{4,5},{5,6},{6,7},{7,8},{8,9},{9,10},{10,1... | collective-permute-start | bytes 24980 | tf_op jit(solution)/shard_map/ppermute | solution.py:16
  72.3 40.7 %collective-permute-start.2 = (f32[2081]{0:T(1024)S(1)}, f32[2081]{0:T(1024)S(1)}, u32[]{:S(2)}, u32[]{:S(2)}) collective-permute-start(f32[2081]{0:T(1024)S(1)} %concatenate.128), channel_id=1, source_target_pairs={{64,0},{128,64},{192,128},{65,1},{129,65},{193,129},{66,2},{130,66... | collective-permute-start | bytes 24980 | tf_op jit(solution)/shard_map/ppermute | solution.py:16
  74.2 38.8 %collective-permute-start.3 = (f32[2081]{0:T(1024)S(1)}, f32[2081]{0:T(1024)S(1)}, u32[]{:S(2)}, u32[]{:S(2)}) collective-permute-start(f32[2081]{0:T(1024)S(1)} %concatenate.128), channel_id=1, source_target_pairs={{0,64},{64,128},{128,192},{1,65},{65,129},{129,193},{2,66},{66,130... | collective-permute-start | bytes 24980 | tf_op jit(solution)/shard_map/ppermute | solution.py:16

commit v8 on v7

--- a/solution.py
+++ b/solution.py
@@ -40,7 +40,7 @@
         nloc = own_ref.shape[0] // BLOCK
         width = own_ref.shape[1]
 
-        if mode == "accum":
+        if mode != "init":
             num_ref[...] = num_in[...]
             den_ref[...] = den_in[...]
         else:
@@ -74,8 +74,7 @@
 
         if mode == "final":
             def fin(b, carry):
-                out_ref[b] = ((num_in[b] + num_ref[b]) / (den_in[b] + den_ref[b])).astype(
-                    out_ref.dtype)
+                out_ref[b] = (num_ref[b] / den_ref[b]).astype(out_ref.dtype)
                 return carry
             lax.fori_loop(0, nloc, fin, 0)
 

time: 136 us -> 133 us (0.978)
  starting transfers between devices: 32.8 us -> 31.3 us
    ppermute x8, starting transfers between devices: 32.8 us -> 31.3 us  [shifted(): return lax.ppermute(shard, axis, pairs)]
  transfers between devices with their start and end apart: 8 -> 8, of which waited for: 1 -> 1; matrix products, arithmetic and copies ran while one was open for 6% -> 7% of each run, Pallas kernels for 32% -> 31%
where the time goes in v8:
time: 133 us
  Pallas kernels  61.4 us (46%)
  starting transfers between devices  31.3 us (24%)
  waiting for transfers between devices  26.8 us (20%)
  other arithmetic  5.97 us (4%)
  local copies, waits for them, and re-layouts  5.19 us (4%)
  between operations  2.29 us (2%)
    pallas_call x3, Pallas kernels, run_phase(): pl.pallas_call(make_kernel(nsrc, n, mode), in_specs=in_specs, out_specs=o...  61.4 us
    ppermute x8, starting transfers between devices, shifted(): return lax.ppermute(shard, axis, pairs)  31.3 us
    ppermute x8, waiting for transfers between devices, shifted(): return lax.ppermute(shard, axis, pairs)  26.8 us
    dot_general x1, other arithmetic, squares_of(): jnp.einsum('bsd,bsd->bs', blocks, blocks, preferred_element_type=jnp.floa...  3.08 us
  transfers between devices with their start and end apart: 8, of which 1 were waited for; matrix products, arithmetic and copies ran while one was open for 7% of the time, Pallas kernels for 31%

profile of v8, /device:TPU:22, one launch (start us, length us, event | category | flops | bytes accessed | tf_op | source)
XLA Modules:
  0.0 132.9 jit_solution(16082844882836089264)
XLA Ops:
  0.0 0.0 copy-start.1
  0.0 2.3 %collective-permute-start.4 = (bf16[2048,1024]{1,0:T(8,128)(2,1)}, bf16[2048,1024]{1,0:T(8,128)(2,1)}, u32[]{:S(2)}, u32[]{:S(2)}) collective-permute-start(bf16[2048,1024]{1,0:T(8,128)(2,1)} %own_ref.5), channel_id=1, source_target_pairs={{1,0},{2,1},{3,2},{4,3},{5,4},{6,5},{7,6},{8,7},{9,8},{10,9},{11,1... | collective-permute-start | bytes 12582920 | tf_op jit(solution)/shard_map/ppermute | solution.py:16
  2.3 2.2 %collective-permute-start.5 = (bf16[2048,1024]{1,0:T(8,128)(2,1)}, bf16[2048,1024]{1,0:T(8,128)(2,1)}, u32[]{:S(2)}, u32[]{:S(2)}) collective-permute-start(bf16[2048,1024]{1,0:T(8,128)(2,1)} %own_ref.5), channel_id=1, source_target_pairs={{0,1},{1,2},{2,3},{3,4},{4,5},{5,6},{6,7},{7,8},{8,9},{9,10},{10,1... | collective-permute-start | bytes 12582920 | tf_op jit(solution)/shard_map/ppermute | solution.py:16
  4.5 2.4 %collective-permute-start = (bf16[2048,1024]{1,0:T(8,128)(2,1)}, bf16[2048,1024]{1,0:T(8,128)(2,1)}, u32[]{:S(2)}, u32[]{:S(2)}) collective-permute-start(bf16[2048,1024]{1,0:T(8,128)(2,1)} %own_ref.5), channel_id=1, source_target_pairs={{64,0},{128,64},{192,128},{65,1},{129,65},{193,129},{66,2},{130,66... | collective-permute-start | bytes 12582920 | tf_op jit(solution)/shard_map/ppermute | solution.py:16
  6.8 5.4 %collective-permute-start.1 = (bf16[2048,1024]{1,0:T(8,128)(2,1)}, bf16[2048,1024]{1,0:T(8,128)(2,1)}, u32[]{:S(2)}, u32[]{:S(2)}) collective-permute-start(bf16[2048,1024]{1,0:T(8,128)(2,1)} %own_ref.5), channel_id=1, source_target_pairs={{0,64},{64,128},{128,192},{1,65},{65,129},{129,193},{2,66},{66,130... | collective-permute-start | bytes 12582920 | tf_op jit(solution)/shard_map/ppermute | solution.py:16
  12.2 3.1 %fusion.refs_1_ = f32[8,256]{1,0:T(8,128)S(1)} fusion(bf16[8,256,1024]{2,1,0:T(8,128)(2,1)} %bitcast.33), kind=kLoop, calls=%fused_computation.1 | loop fusion | flops 6289408 | bytes 4202496 | tf_op jit(solution)/shard_map/bsd,bsd->bs/dot_general | solution.py:20
  15.3 0.0 copy-start
  16.0 0.0 copy-done.1
  16.0 0.1 copy.8
  16.1 0.1 convert_element_type.60
  16.2 0.1 concatenate.128
  16.3 2.8 %collective-permute-start.6 = (f32[2081]{0:T(1024)S(1)}, f32[2081]{0:T(1024)S(1)}, u32[]{:S(2)}, u32[]{:S(2)}) collective-permute-start(f32[2081]{0:T(1024)S(1)} %concatenate.128), channel_id=1, source_target_pairs={{1,0},{2,1},{3,2},{4,3},{5,4},{6,5},{7,6},{8,7},{9,8},{10,9},{11,1... | collective-permute-start | bytes 24980 | tf_op jit(solution)/shard_map/ppermute | solution.py:16
  19.2 0.1 copy.9
  19.2 0.1 copy.7
  19.3 0.1 and_reduce_fusion
  19.5 0.1 fusion.10
  19.5 0.1 add_reduce_fusion
  19.7 0.1 add_clamp_fusion
  19.8 0.7 reshape.361.tab
  20.5 1.4 %copy.10.sqc_ref = f32[8,256,1]{2,1,0:T(8,128)} copy(f32[8,256,1]{1,0,2:T(8,128)S(1)} %bitcast.35) | data formatting | bytes 16384 | tf_op jit(solution)/shard_map/broadcast_in_dim | solution.py:160
  21.8 0.0 copy-start.2
  21.8 26.8 %collective-permute-done.6 = f32[2081]{0:T(1024)S(1)} collective-permute-done((f32[2081]{0:T(1024)S(1)}, f32[2081]{0:T(1024)S(1)}, u32[]{:S(2)}, u32[]{:S(2)}) %collective-permute-start.6) | collective-permute-done | bytes 8356 | tf_op jit(solution)/shard_map/ppermute | solution.py:16
  48.7 5.5 %collective-permute-start.7 = (f32[2081]{0:T(1024)S(1)}, f32[2081]{0:T(1024)S(1)}, u32[]{:S(2)}, u32[]{:S(2)}) collective-permute-start(f32[2081]{0:T(1024)S(1)} %concatenate.128), channel_id=1, source_target_pairs={{0,1},{1,2},{2,3},{3,4},{4,5},{5,6},{6,7},{7,8},{8,9},{9,10},{10,1... | collective-permute-start | bytes 24980 | tf_op jit(solution)/shard_map/ppermute | solution.py:16
  54.1 0.0 copy-done
  54.2 16.6 %shard_map.37 = (f32[8,256,1024]{2,1,0:T(8,128)}, f32[8,256,1]{2,1,0:T(8,128)}) custom-call(s32[160]{0:T(256)} %reshape.361.tab, bf16[2048,1024]{1,0:T(8,128)(2,1)} %own_ref.5, f32[8,256,1]{2,1,0:T(8,128)} %copy.10.sqc_ref, bf16[2048,1024]{1,0:T(8,128)(2,1)} %own_ref.5, f32[8,256]{1,0:T(8,128)} %copy-done), custom_call_target="tpu_custom_call" | custom-call | flops 10737418240 | bytes 16777216 | tf_op jit(solution)/shard_map/pallas_call | solution.py:107
  70.7 0.0 collective-permute-done.7
  70.7 5.5 %collective-permute-start.2 = (f32[2081]{0:T(1024)S(1)}, f32[2081]{0:T(1024)S(1)}, u32[]{:S(2)}, u32[]{:S(2)}) collective-permute-start(f32[2081]{0:T(1024)S(1)} %concatenate.128), channel_id=1, source_target_pairs={{64,0},{128,64},{192,128},{65,1},{129,65},{193,129},{66,2},{130,66... | collective-permute-start | bytes 24980 | tf_op jit(solution)/shard_map/ppermute | solution.py:16
  76.2 0.0 collective-permute-done.4.refs_0_
  76.2 5.3 %collective-permute-start.3 = (f32[2081]{0:T(1024)S(1)}, f32[2081]{0:T(1024)S(1)}, u32[]{:S(2)}, u32[]{:S(2)}) collective-permute-start(f32[2081]{0:T(1024)S(1)} %concatenate.128), channel_id=1, source_target_pairs={{0,64},{64,128},{128,192},{1,65},{65,129},{129,193},{2,66},{66,130... | collective-permute-start | bytes 24980 | tf_op jit(solution)/shard_map/ppermute | solution.py:16
  81.5 0.0 collective-permute-done.5.refs_1_
  81.5 0.7 slice.47
  82.2 0.1 convert_element_type.64
  83.0 0.2 fusion.3
  83.2 0.1 add_clamp_fusion.2
  83.3 0.1 add_clamp_fusion.3
  83.3 0.2 compare_reduce_fusion.3
  83.5 0.1 add_convert_fusion
  83.6 0.0 copy-done.2
  83.6 0.7 reshape.362.tab
  84.3 0.6 pad_maximum_fusion.refs_2_
  84.9 24.2 %shard_map.38 = (f32[8,256,1024]{2,1,0:T(8,128)}, f32[8,256,1]{2,1,0:T(8,128)}) custom-call(s32[128]{0:T(128)} %reshape.362.tab, bf16[2048,1024]{1,0:T(8,128)(2,1)} %own_ref.5, f32[8,256,1]{2,1,0:T(8,128)} %copy.10.sqc_ref, bf16[2048,1024]{1,0:T(8,128)(2,1)} %collective-permute-done.4.refs_0_, bf16[2048,1024]{1,0:T(8,128)(2,1)} %collective-permute-done.5.refs_1_, ...), custom_call_target="tpu_custom_call" | custom-call | flops 8589934592 | bytes 20971520 | tf_op jit(solution)/shard_map/pallas_call | solution.py:107
  109.1 0.0 collective-permute-done.2
  109.1 0.0 collective-permute-done.3
  109.1 0.0 collective-permute-done.refs_0_
  109.1 0.0 collective-permute-done.1.refs_1_
  109.2 0.6 slice.53
  109.8 0.1 convert_element_type.68
  109.8 0.2 compare_reduce_fusion.1
  110.0 0.2 fusion.4
  110.2 0.1 add_clamp_fusion.4
  111.0 0.1 add_clamp_fusion.5
  111.0 0.1 add_convert_fusion.1
  111.1 0.6 reshape.365.tab
  111.7 0.6 pad_maximum_fusion.1.refs_2_
  112.3 20.6 %shard_map.39 = bf16[8,256,1024]{2,1,0:T(8,128)(2,1)} custom-call(s32[128]{0:T(128)} %reshape.365.tab, bf16[2048,1024]{1,0:T(8,128)(2,1)} %own_ref.5, f32[8,256,1]{2,1,0:T(8,128)} %copy.10.sqc_ref, bf16[2048,1024]{1,0:T(8,128)(2,1)} %collective-permute-done.refs_0_, bf16[2048,1024]{1,0:T(8,128)(2,1)} %collective-permute-done.1.refs_1_, ...), custom_call_target="tpu_custom_call" | custom-call | flops 8589934592 | bytes 20971520 | tf_op jit(solution)/shard_map/pallas_call | solution.py:107
  (22 shorter events, 0.1 us)
Async XLA Ops:
  0.0 16.0 %copy-start.1 = (s32[16,2]{0,1:T(2,128)S(1)}, s32[16,2]{0,1:T(2,128)}, u32[]{:S(2)}) copy-start(s32[16,2]{0,1:T(2,128)} %param.4) | copy-start | bytes 388
  0.0 76.2 %collective-permute-start.4 = (bf16[2048,1024]{1,0:T(8,128)(2,1)}, bf16[2048,1024]{1,0:T(8,128)(2,1)}, u32[]{:S(2)}, u32[]{:S(2)}) collective-permute-start(bf16[2048,1024]{1,0:T(8,128)(2,1)} %own_ref.5), channel_id=1, source_target_pairs={{1,0},{2,1},{3,2},{4,3},{5,4},{6,5},{7,6},{8,7},{9,8},{10,9},{11,1... | collective-permute-start | bytes 12582920 | tf_op jit(solution)/shard_map/ppermute | solution.py:16
  2.3 79.2 %collective-permute-start.5 = (bf16[2048,1024]{1,0:T(8,128)(2,1)}, bf16[2048,1024]{1,0:T(8,128)(2,1)}, u32[]{:S(2)}, u32[]{:S(2)}) collective-permute-start(bf16[2048,1024]{1,0:T(8,128)(2,1)} %own_ref.5), channel_id=1, source_target_pairs={{0,1},{1,2},{2,3},{3,4},{4,5},{5,6},{6,7},{7,8},{8,9},{9,10},{10,1... | collective-permute-start | bytes 12582920 | tf_op jit(solution)/shard_map/ppermute | solution.py:16
  4.5 104.7 %collective-permute-start = (bf16[2048,1024]{1,0:T(8,128)(2,1)}, bf16[2048,1024]{1,0:T(8,128)(2,1)}, u32[]{:S(2)}, u32[]{:S(2)}) collective-permute-start(bf16[2048,1024]{1,0:T(8,128)(2,1)} %own_ref.5), channel_id=1, source_target_pairs={{64,0},{128,64},{192,128},{65,1},{129,65},{193,129},{66,2},{130,66... | collective-permute-start | bytes 12582920 | tf_op jit(solution)/shard_map/ppermute | solution.py:16
  6.8 102.3 %collective-permute-start.1 = (bf16[2048,1024]{1,0:T(8,128)(2,1)}, bf16[2048,1024]{1,0:T(8,128)(2,1)}, u32[]{:S(2)}, u32[]{:S(2)}) collective-permute-start(bf16[2048,1024]{1,0:T(8,128)(2,1)} %own_ref.5), channel_id=1, source_target_pairs={{0,64},{64,128},{128,192},{1,65},{65,129},{129,193},{2,66},{66,130... | collective-permute-start | bytes 12582920 | tf_op jit(solution)/shard_map/ppermute | solution.py:16
  15.3 38.8 %copy-start = (f32[8,256]{1,0:T(8,128)}, f32[8,256]{1,0:T(8,128)S(1)}, u32[]{:S(2)}) copy-start(f32[8,256]{1,0:T(8,128)S(1)} %fusion.refs_1_) | copy-start | bytes 24580
  16.3 32.4 %collective-permute-start.6 = (f32[2081]{0:T(1024)S(1)}, f32[2081]{0:T(1024)S(1)}, u32[]{:S(2)}, u32[]{:S(2)}) collective-permute-start(f32[2081]{0:T(1024)S(1)} %concatenate.128), channel_id=1, source_target_pairs={{1,0},{2,1},{3,2},{4,3},{5,4},{6,5},{7,6},{8,7},{9,8},{10,9},{11,1... | collective-permute-start | bytes 24980 | tf_op jit(solution)/shard_map/ppermute | solution.py:16
  21.8 61.8 %copy-start.2 = (s32[1,32]{1,0:T(1,128)S(1)}, s32[1,32]{1,0:T(1,128)}, u32[]{:S(2)}) copy-start(s32[1,32]{1,0:T(1,128)} %constant.30.clone.1) | copy-start | bytes 388
  48.7 22.1 %collective-permute-start.7 = (f32[2081]{0:T(1024)S(1)}, f32[2081]{0:T(1024)S(1)}, u32[]{:S(2)}, u32[]{:S(2)}) collective-permute-start(f32[2081]{0:T(1024)S(1)} %concatenate.128), channel_id=1, source_target_pairs={{0,1},{1,2},{2,3},{3,4},{4,5},{5,6},{6,7},{7,8},{8,9},{9,10},{10,1... | collective-permute-start | bytes 24980 | tf_op jit(solution)/shard_map/ppermute | solution.py:16
  70.7 38.4 %collective-permute-start.2 = (f32[2081]{0:T(1024)S(1)}, f32[2081]{0:T(1024)S(1)}, u32[]{:S(2)}, u32[]{:S(2)}) collective-permute-start(f32[2081]{0:T(1024)S(1)} %concatenate.128), channel_id=1, source_target_pairs={{64,0},{128,64},{192,128},{65,1},{129,65},{193,129},{66,2},{130,66... | collective-permute-start | bytes 24980 | tf_op jit(solution)/shard_map/ppermute | solution.py:16
  76.2 32.9 %collective-permute-start.3 = (f32[2081]{0:T(1024)S(1)}, f32[2081]{0:T(1024)S(1)}, u32[]{:S(2)}, u32[]{:S(2)}) collective-permute-start(f32[2081]{0:T(1024)S(1)} %concatenate.128), channel_id=1, source_target_pairs={{0,64},{64,128},{128,192},{1,65},{65,129},{129,193},{2,66},{66,130... | collective-permute-start | bytes 24980 | tf_op jit(solution)/shard_map/ppermute | solution.py:16

commit v9 on v8

--- a/solution.py
+++ b/solution.py
@@ -36,7 +36,7 @@
         elif mode == "accum":
             num_in, den_in, num_ref, den_ref = rest
         else:
-            num_in, den_in, out_ref, num_ref, den_ref = rest
+            num_in, den_in, out_ref, num_ref, den_ref, stage, out_sem = rest
         nloc = own_ref.shape[0] // BLOCK
         width = own_ref.shape[1]
 
@@ -73,10 +73,14 @@
         lax.fori_loop(0, n, body, 0)
 
         if mode == "final":
-            def fin(b, carry):
-                out_ref[b] = (num_ref[b] / den_ref[b]).astype(out_ref.dtype)
-                return carry
-            lax.fori_loop(0, nloc, fin, 0)
+            copies = []
+            for b in range(nloc):
+                stage[b] = (num_ref[b] / den_ref[b]).astype(stage.dtype)
+                cp = pltpu.make_async_copy(stage.at[b], out_ref.at[b], out_sem.at[b])
+                cp.start()
+                copies.append(cp)
+            for cp in copies:
+                cp.wait()
 
     return kernel
 
@@ -97,9 +101,11 @@
         args += [num, den]
     if mode == "final":
         out_shape = jax.ShapeDtypeStruct((nloc, block, width), jnp.bfloat16)
-        out_specs = vm
+        out_specs = pl.BlockSpec(memory_space=pl.ANY)
         scratch = [pltpu.VMEM((nloc, block, width), jnp.float32),
-                   pltpu.VMEM((nloc, block, 1), jnp.float32)]
+                   pltpu.VMEM((nloc, block, 1), jnp.float32),
+                   pltpu.VMEM((nloc, block, width), jnp.bfloat16),
+                   pltpu.SemaphoreType.DMA((nloc,))]
     else:
         out_shape = acc_shapes
         out_specs = [vm, vm]

time: 133 us -> 133 us (level)
  the two profiles are of different devices: /device:TPU:22 before, /device:TPU:27 now
where the time goes in v9:
time: 133 us
  Pallas kernels  71.4 us (54%)
  waiting for transfers between devices  30.8 us (23%)
  starting transfers between devices  17.7 us (13%)
  other arithmetic  5.96 us (4%)
  local copies, waits for them, and re-layouts  5.19 us (4%)
  between operations  2.28 us (2%)
    pallas_call x3, Pallas kernels, run_phase(): pl.pallas_call(make_kernel(nsrc, n, mode), in_specs=in_specs, out_specs=o...  71.4 us
    ppermute x8, waiting for transfers between devices, shifted(): return lax.ppermute(shard, axis, pairs)  30.8 us
    ppermute x8, starting transfers between devices, shifted(): return lax.ppermute(shard, axis, pairs)  17.7 us
    dot_general x1, other arithmetic, squares_of(): jnp.einsum('bsd,bsd->bs', blocks, blocks, preferred_element_type=jnp.floa...  3.08 us
  transfers between devices with their start and end apart: 8, of which 1 were waited for; matrix products, arithmetic and copies ran while one was open for 6% of the time, Pallas kernels for 42%

profile of v9, /device:TPU:27, one launch (start us, length us, event | category | flops | bytes accessed | tf_op | source)
XLA Modules:
  0.0 133.3 jit_solution(9691142398757865956)
XLA Ops:
  0.0 0.0 copy-start.1
  0.0 2.7 %collective-permute-start.4 = (bf16[2048,1024]{1,0:T(8,128)(2,1)}, bf16[2048,1024]{1,0:T(8,128)(2,1)}, u32[]{:S(2)}, u32[]{:S(2)}) collective-permute-start(bf16[2048,1024]{1,0:T(8,128)(2,1)} %own_ref.5), channel_id=1, source_target_pairs={{1,0},{2,1},{3,2},{4,3},{5,4},{6,5},{7,6},{8,7},{9,8},{10,9},{11,1... | collective-permute-start | bytes 12582920 | tf_op jit(solution)/shard_map/ppermute | solution.py:16
  2.7 3.0 %collective-permute-start.5 = (bf16[2048,1024]{1,0:T(8,128)(2,1)}, bf16[2048,1024]{1,0:T(8,128)(2,1)}, u32[]{:S(2)}, u32[]{:S(2)}) collective-permute-start(bf16[2048,1024]{1,0:T(8,128)(2,1)} %own_ref.5), channel_id=1, source_target_pairs={{0,1},{1,2},{2,3},{3,4},{4,5},{5,6},{6,7},{7,8},{8,9},{9,10},{10,1... | collective-permute-start | bytes 12582920 | tf_op jit(solution)/shard_map/ppermute | solution.py:16
  5.7 4.3 %collective-permute-start = (bf16[2048,1024]{1,0:T(8,128)(2,1)}, bf16[2048,1024]{1,0:T(8,128)(2,1)}, u32[]{:S(2)}, u32[]{:S(2)}) collective-permute-start(bf16[2048,1024]{1,0:T(8,128)(2,1)} %own_ref.5), channel_id=1, source_target_pairs={{64,0},{128,64},{192,128},{65,1},{129,65},{193,129},{66,2},{130,66... | collective-permute-start | bytes 12582920 | tf_op jit(solution)/shard_map/ppermute | solution.py:16
  10.0 1.3 collective-permute-start.1
  11.3 3.1 %fusion.refs_1_ = f32[8,256]{1,0:T(8,128)S(1)} fusion(bf16[8,256,1024]{2,1,0:T(8,128)(2,1)} %bitcast.33), kind=kLoop, calls=%fused_computation.1 | loop fusion | flops 6289408 | bytes 4202496 | tf_op jit(solution)/shard_map/bsd,bsd->bs/dot_general | solution.py:20
  14.4 0.0 copy-start
  15.1 0.0 copy-done.1
  15.1 0.1 copy.8
  15.2 0.1 convert_element_type.60
  15.3 0.1 concatenate.128
  15.4 1.9 %collective-permute-start.6 = (f32[2081]{0:T(1024)S(1)}, f32[2081]{0:T(1024)S(1)}, u32[]{:S(2)}, u32[]{:S(2)}) collective-permute-start(f32[2081]{0:T(1024)S(1)} %concatenate.128), channel_id=1, source_target_pairs={{1,0},{2,1},{3,2},{4,3},{5,4},{6,5},{7,6},{8,7},{9,8},{10,9},{11,1... | collective-permute-start | bytes 24980 | tf_op jit(solution)/shard_map/ppermute | solution.py:16
  17.3 0.1 copy.9
  17.4 0.1 copy.7
  17.5 0.1 and_reduce_fusion
  17.6 0.1 fusion.10
  17.7 0.1 add_reduce_fusion
  17.9 0.1 add_clamp_fusion
  18.0 0.7 reshape.361.tab
  18.6 1.4 %copy.10.sqc_ref = f32[8,256,1]{2,1,0:T(8,128)} copy(f32[8,256,1]{1,0,2:T(8,128)S(1)} %bitcast.35) | data formatting | bytes 16384 | tf_op jit(solution)/shard_map/broadcast_in_dim | solution.py:166
  20.0 0.0 copy-start.2
  20.0 30.8 %collective-permute-done.6 = f32[2081]{0:T(1024)S(1)} collective-permute-done((f32[2081]{0:T(1024)S(1)}, f32[2081]{0:T(1024)S(1)}, u32[]{:S(2)}, u32[]{:S(2)}) %collective-permute-start.6) | collective-permute-done | bytes 8356 | tf_op jit(solution)/shard_map/ppermute | solution.py:16
  50.7 1.9 %collective-permute-start.7 = (f32[2081]{0:T(1024)S(1)}, f32[2081]{0:T(1024)S(1)}, u32[]{:S(2)}, u32[]{:S(2)}) collective-permute-start(f32[2081]{0:T(1024)S(1)} %concatenate.128), channel_id=1, source_target_pairs={{0,1},{1,2},{2,3},{3,4},{4,5},{5,6},{6,7},{7,8},{8,9},{9,10},{10,1... | collective-permute-start | bytes 24980 | tf_op jit(solution)/shard_map/ppermute | solution.py:16
  52.6 0.0 copy-done
  52.7 22.9 %shard_map.37 = (f32[8,256,1024]{2,1,0:T(8,128)}, f32[8,256,1]{2,1,0:T(8,128)}) custom-call(s32[160]{0:T(256)} %reshape.361.tab, bf16[2048,1024]{1,0:T(8,128)(2,1)} %own_ref.5, f32[8,256,1]{2,1,0:T(8,128)} %copy.10.sqc_ref, bf16[2048,1024]{1,0:T(8,128)(2,1)} %own_ref.5, f32[8,256]{1,0:T(8,128)} %copy-done), custom_call_target="tpu_custom_call" | custom-call | flops 10737418240 | bytes 16777216 | tf_op jit(solution)/shard_map/pallas_call | solution.py:113
  75.5 0.0 collective-permute-done.7
  75.5 1.3 collective-permute-start.2
  76.8 0.0 collective-permute-done.4.refs_0_
  76.8 1.3 collective-permute-start.3
  78.1 0.0 collective-permute-done.5.refs_1_
  78.1 0.7 slice.47
  78.8 0.1 convert_element_type.64
  79.6 0.2 fusion.3
  79.8 0.1 add_clamp_fusion.2
  79.9 0.1 add_clamp_fusion.3
  79.9 0.2 compare_reduce_fusion.3
  80.2 0.1 add_convert_fusion
  80.2 0.0 copy-done.2
  80.3 0.7 reshape.362.tab
  80.9 0.6 pad_maximum_fusion.refs_2_
  81.5 32.8 %shard_map.38 = (f32[8,256,1024]{2,1,0:T(8,128)}, f32[8,256,1]{2,1,0:T(8,128)}) custom-call(s32[128]{0:T(128)} %reshape.362.tab, bf16[2048,1024]{1,0:T(8,128)(2,1)} %own_ref.5, f32[8,256,1]{2,1,0:T(8,128)} %copy.10.sqc_ref, bf16[2048,1024]{1,0:T(8,128)(2,1)} %collective-permute-done.4.refs_0_, bf16[2048,1024]{1,0:T(8,128)(2,1)} %collective-permute-done.5.refs_1_, ...), custom_call_target="tpu_custom_call" | custom-call | flops 8589934592 | bytes 20971520 | tf_op jit(solution)/shard_map/pallas_call | solution.py:113
  114.3 0.0 collective-permute-done.2
  114.3 0.0 collective-permute-done.3
  114.4 0.0 collective-permute-done.refs_0_
  114.4 0.0 collective-permute-done.1.refs_1_
  114.4 0.6 slice.53
  115.0 0.1 convert_element_type.68
  115.1 0.2 compare_reduce_fusion.1
  115.3 0.2 fusion.4
  115.4 0.1 add_clamp_fusion.4
  116.2 0.1 add_clamp_fusion.5
  116.3 0.1 add_convert_fusion.1
  116.4 0.6 reshape.365.tab
  117.0 0.6 pad_maximum_fusion.1.refs_2_
  117.6 15.8 %shard_map.39 = bf16[8,256,1024]{2,1,0:T(8,128)(2,1)} custom-call(s32[128]{0:T(128)} %reshape.365.tab, bf16[2048,1024]{1,0:T(8,128)(2,1)} %own_ref.5, f32[8,256,1]{2,1,0:T(8,128)} %copy.10.sqc_ref, bf16[2048,1024]{1,0:T(8,128)(2,1)} %collective-permute-done.refs_0_, bf16[2048,1024]{1,0:T(8,128)(2,1)} %collective-permute-done.1.refs_1_, ...), custom_call_target="tpu_custom_call" | custom-call | flops 8589934592 | bytes 20971520 | tf_op jit(solution)/shard_map/pallas_call | solution.py:113
  (22 shorter events, 0.1 us)
Async XLA Ops:
  0.0 15.1 %copy-start.1 = (s32[16,2]{0,1:T(2,128)S(1)}, s32[16,2]{0,1:T(2,128)}, u32[]{:S(2)}) copy-start(s32[16,2]{0,1:T(2,128)} %param.4) | copy-start | bytes 388
  0.0 76.8 %collective-permute-start.4 = (bf16[2048,1024]{1,0:T(8,128)(2,1)}, bf16[2048,1024]{1,0:T(8,128)(2,1)}, u32[]{:S(2)}, u32[]{:S(2)}) collective-permute-start(bf16[2048,1024]{1,0:T(8,128)(2,1)} %own_ref.5), channel_id=1, source_target_pairs={{1,0},{2,1},{3,2},{4,3},{5,4},{6,5},{7,6},{8,7},{9,8},{10,9},{11,1... | collective-permute-start | bytes 12582920 | tf_op jit(solution)/shard_map/ppermute | solution.py:16
  2.7 75.4 %collective-permute-start.5 = (bf16[2048,1024]{1,0:T(8,128)(2,1)}, bf16[2048,1024]{1,0:T(8,128)(2,1)}, u32[]{:S(2)}, u32[]{:S(2)}) collective-permute-start(bf16[2048,1024]{1,0:T(8,128)(2,1)} %own_ref.5), channel_id=1, source_target_pairs={{0,1},{1,2},{2,3},{3,4},{4,5},{5,6},{6,7},{7,8},{8,9},{9,10},{10,1... | collective-permute-start | bytes 12582920 | tf_op jit(solution)/shard_map/ppermute | solution.py:16
  5.7 108.6 %collective-permute-start = (bf16[2048,1024]{1,0:T(8,128)(2,1)}, bf16[2048,1024]{1,0:T(8,128)(2,1)}, u32[]{:S(2)}, u32[]{:S(2)}) collective-permute-start(bf16[2048,1024]{1,0:T(8,128)(2,1)} %own_ref.5), channel_id=1, source_target_pairs={{64,0},{128,64},{192,128},{65,1},{129,65},{193,129},{66,2},{130,66... | collective-permute-start | bytes 12582920 | tf_op jit(solution)/shard_map/ppermute | solution.py:16
  10.0 104.3 %collective-permute-start.1 = (bf16[2048,1024]{1,0:T(8,128)(2,1)}, bf16[2048,1024]{1,0:T(8,128)(2,1)}, u32[]{:S(2)}, u32[]{:S(2)}) collective-permute-start(bf16[2048,1024]{1,0:T(8,128)(2,1)} %own_ref.5), channel_id=1, source_target_pairs={{0,64},{64,128},{128,192},{1,65},{65,129},{129,193},{2,66},{66,130... | collective-permute-start | bytes 12582920 | tf_op jit(solution)/shard_map/ppermute | solution.py:16
  14.4 38.2 %copy-start = (f32[8,256]{1,0:T(8,128)}, f32[8,256]{1,0:T(8,128)S(1)}, u32[]{:S(2)}) copy-start(f32[8,256]{1,0:T(8,128)S(1)} %fusion.refs_1_) | copy-start | bytes 24580
  15.4 35.4 %collective-permute-start.6 = (f32[2081]{0:T(1024)S(1)}, f32[2081]{0:T(1024)S(1)}, u32[]{:S(2)}, u32[]{:S(2)}) collective-permute-start(f32[2081]{0:T(1024)S(1)} %concatenate.128), channel_id=1, source_target_pairs={{1,0},{2,1},{3,2},{4,3},{5,4},{6,5},{7,6},{8,7},{9,8},{10,9},{11,1... | collective-permute-start | bytes 24980 | tf_op jit(solution)/shard_map/ppermute | solution.py:16
  20.0 60.3 %copy-start.2 = (s32[1,32]{1,0:T(1,128)S(1)}, s32[1,32]{1,0:T(1,128)}, u32[]{:S(2)}) copy-start(s32[1,32]{1,0:T(1,128)} %constant.30.clone.1) | copy-start | bytes 388
  50.7 24.8 %collective-permute-start.7 = (f32[2081]{0:T(1024)S(1)}, f32[2081]{0:T(1024)S(1)}, u32[]{:S(2)}, u32[]{:S(2)}) collective-permute-start(f32[2081]{0:T(1024)S(1)} %concatenate.128), channel_id=1, source_target_pairs={{0,1},{1,2},{2,3},{3,4},{4,5},{5,6},{6,7},{7,8},{8,9},{9,10},{10,1... | collective-permute-start | bytes 24980 | tf_op jit(solution)/shard_map/ppermute | solution.py:16
  75.5 38.8 %collective-permute-start.2 = (f32[2081]{0:T(1024)S(1)}, f32[2081]{0:T(1024)S(1)}, u32[]{:S(2)}, u32[]{:S(2)}) collective-permute-start(f32[2081]{0:T(1024)S(1)} %concatenate.128), channel_id=1, source_target_pairs={{64,0},{128,64},{192,128},{65,1},{129,65},{193,129},{66,2},{130,66... | collective-permute-start | bytes 24980 | tf_op jit(solution)/shard_map/ppermute | solution.py:16
  76.8 37.5 %collective-permute-start.3 = (f32[2081]{0:T(1024)S(1)}, f32[2081]{0:T(1024)S(1)}, u32[]{:S(2)}, u32[]{:S(2)}) collective-permute-start(f32[2081]{0:T(1024)S(1)} %concatenate.128), channel_id=1, source_target_pairs={{0,64},{64,128},{128,192},{1,65},{65,129},{129,193},{2,66},{66,130... | collective-permute-start | bytes 24980 | tf_op jit(solution)/shard_map/ppermute | solution.py:16

commit v10 on v8

--- a/solution.py
+++ b/solution.py
@@ -27,7 +27,7 @@
 
 
 def make_kernel(nsrc, n, mode):
-    def kernel(tab, own_ref, sqc_ref, *refs):
+    def kernel(tab, own_ref, ownt_ref, sqc_ref, *refs):
         src_refs = refs[:nsrc]
         sqr_ref = refs[nsrc]
         rest = refs[nsrc + 1:]
@@ -48,16 +48,16 @@
             den_ref[...] = jnp.zeros_like(den_ref)
 
         def contribute(t, prow, p_ref, ix):
-            xt = own_ref[pl.ds(pl.multiple_of(t * BLOCK, BLOCK), BLOCK), :]
+            xt_t = ownt_ref[:, pl.ds(pl.multiple_of(t * BLOCK, BLOCK), BLOCK)]
             xp = p_ref[pl.ds(pl.multiple_of(ix * BLOCK, BLOCK), BLOCK), :]
-            inner = lax.dot_general(xt, xp, (((1,), (1,)), ((), ())),
-                                    preferred_element_type=jnp.float32)
-            sq_t = sqc_ref[t]
-            sq_p = sqr_ref[pl.ds(prow, 1), :]
-            distance = sq_t + sq_p - 2.0 * inner
-            w = jnp.exp(-distance / (scale_factor * width)).astype(jnp.bfloat16)
-            num_ref[t] += jnp.dot(w, xp, preferred_element_type=jnp.float32)
-            den_ref[t] += jnp.sum(w.astype(jnp.float32), axis=1, keepdims=True)
+            inner_t = jnp.dot(xp, xt_t, preferred_element_type=jnp.float32)
+            sq_t = sqc_ref[pl.ds(t, 1), :]
+            sq_p = sqr_ref[prow]
+            distance = sq_p + sq_t - 2.0 * inner_t
+            w_t = jnp.exp(-distance / (scale_factor * width)).astype(jnp.bfloat16)
+            num_ref[t] += lax.dot_general(w_t, xp, (((0,), (0,)), ((), ())),
+                                          preferred_element_type=jnp.float32)
+            den_ref[t] += jnp.sum(w_t.astype(jnp.float32), axis=0, keepdims=True)
 
         def body(j, carry):
             t = tab[j]
@@ -74,23 +74,24 @@
 
         if mode == "final":
             def fin(b, carry):
-                out_ref[b] = (num_ref[b] / den_ref[b]).astype(out_ref.dtype)
+                dcol = jnp.transpose(jnp.broadcast_to(den_ref[b], (8, BLOCK)), (1, 0))[:, 0:1]
+                out_ref[b] = (num_ref[b] / dcol).astype(out_ref.dtype)
                 return carry
             lax.fori_loop(0, nloc, fin, 0)
 
     return kernel
 
 
-def run_phase(mode, tab, n, own, sq_col, sources, sq_rows, num=None, den=None):
+def run_phase(mode, tab, n, own, own_t, sq_row, sources, sq_cols, num=None, den=None):
     rows, width = own.shape
     block = BLOCK
     nloc = rows // block
     nsrc = len(sources)
     vm = pl.BlockSpec(memory_space=pltpu.VMEM)
-    in_specs = [pl.BlockSpec(memory_space=pltpu.SMEM), vm, vm] + [vm] * nsrc + [vm]
-    args = [tab, own, sq_col, *sources, sq_rows]
+    in_specs = [pl.BlockSpec(memory_space=pltpu.SMEM), vm, vm, vm] + [vm] * nsrc + [vm]
+    args = [tab, own, own_t, sq_row, *sources, sq_cols]
     acc_shapes = [jax.ShapeDtypeStruct((nloc, block, width), jnp.float32),
-                  jax.ShapeDtypeStruct((nloc, block, 1), jnp.float32)]
+                  jax.ShapeDtypeStruct((nloc, 1, block), jnp.float32)]
     scratch = []
     if mode != "init":
         in_specs += [vm, vm]
@@ -99,7 +100,7 @@
         out_shape = jax.ShapeDtypeStruct((nloc, block, width), jnp.bfloat16)
         out_specs = vm
         scratch = [pltpu.VMEM((nloc, block, width), jnp.float32),
-                   pltpu.VMEM((nloc, block, 1), jnp.float32)]
+                   pltpu.VMEM((nloc, 1, block), jnp.float32)]
     else:
         out_shape = acc_shapes
         out_specs = [vm, vm]
@@ -157,14 +158,15 @@
     ridx_grp = right - first_block - owners * nloc
     zeros = jnp.zeros((slots,), jnp.int32)
     ones = jnp.ones((slots,), jnp.int32)
-    sq_col = own_sq[:, :, None]
+    own_t = embeddings.T
 
     diag = jnp.arange(nloc, dtype=jnp.int32)
     t1 = jnp.concatenate([diag, left, roff])
     i1 = jnp.concatenate([diag, roff, left])
     v1 = jnp.concatenate([jnp.ones((nloc,), bool), used & r_local, used & r_local])
     tab1 = pack_table(t1, jnp.zeros_like(t1), i1, v1, nloc)
-    num, den = run_phase("init", tab1, t1.shape[0], embeddings, sq_col, [embeddings], own_sq)
+    num, den = run_phase("init", tab1, t1.shape[0], embeddings, own_t, own_sq, [embeddings],
+                         own_sq[:, :, None])
 
     def prev_entries(pairs, count, prev_first):
         u = pos < count[0]
@@ -182,7 +184,8 @@
     v2 = jnp.concatenate([used & r_dev, pu])
     tab2 = pack_table(t2, s2, i2, v2, nloc)
     sq2 = jnp.concatenate([sq_nd, sq_pd], axis=0)
-    num, den = run_phase("accum", tab2, t2.shape[0], embeddings, sq_col, [nd, pd], sq2, num, den)
+    num, den = run_phase("accum", tab2, t2.shape[0], embeddings, own_t, own_sq, [nd, pd],
+                         sq2[:, :, None], num, den)
 
     ng, pg, m_ng, m_pg, num, den = lax.optimization_barrier((ng, pg, m_ng, m_pg, num, den))
     sq_ng, _, _ = decode_meta(m_ng, nloc, slots)
@@ -194,7 +197,8 @@
     v3 = jnp.concatenate([used & r_grp, gu])
     tab3 = pack_table(t3, s3, i3, v3, nloc)
     sq3 = jnp.concatenate([sq_ng, sq_pg], axis=0)
-    smoothed = run_phase("final", tab3, t3.shape[0], embeddings, sq_col, [ng, pg], sq3, num, den)
+    smoothed = run_phase("final", tab3, t3.shape[0], embeddings, own_t, own_sq, [ng, pg],
+                         sq3[:, :, None], num, den)
     return smoothed.reshape(total_rows, width)
 
 

time: 133 us -> 143 us (1.075)
  the two profiles are of different devices: /device:TPU:22 before, /device:TPU:57 now
where the time goes in v10:
time: 143 us; the launch traced here: 142 us
  Pallas kernels  77.8 us (54%)
  waiting for transfers between devices  23.4 us (16%)
  starting transfers between devices  18.7 us (13%)
  local copies, waits for them, and re-layouts  15.5 us (11%)
  other arithmetic  4.77 us (3%)
  between operations  2.16 us (2%)
    pallas_call x3, Pallas kernels, run_phase(): pl.pallas_call(make_kernel(nsrc, n, mode), in_specs=in_specs, out_specs=o...  77.8 us
    ppermute x8, waiting for transfers between devices, shifted(): return lax.ppermute(shard, axis, pairs)  23.4 us
    ppermute x8, starting transfers between devices, shifted(): return lax.ppermute(shard, axis, pairs)  18.7 us
    unnamed x8, local copies, waits for them, and re-layouts  6.52 us
    dot_general x1, other arithmetic, squares_of(): jnp.einsum('bsd,bsd->bs', blocks, blocks, preferred_element_type=jnp.floa...  3.08 us
  transfers between devices with their start and end apart: 8, of which 1 were waited for; matrix products, arithmetic and copies ran while one was open for 11% of the time, Pallas kernels for 41%

profile of v10, /device:TPU:57, one launch (start us, length us, event | category | flops | bytes accessed | tf_op | source)
XLA Modules:
  0.0 142.3 jit_solution(14762018308932304582)
XLA Ops:
  0.0 0.0 copy-start.1
  0.0 2.7 %collective-permute-start.4 = (bf16[2048,1024]{1,0:T(8,128)(2,1)}, bf16[2048,1024]{1,0:T(8,128)(2,1)}, u32[]{:S(2)}, u32[]{:S(2)}) collective-permute-start(bf16[2048,1024]{1,0:T(8,128)(2,1)} %own_ref.5), channel_id=1, source_target_pairs={{1,0},{2,1},{3,2},{4,3},{5,4},{6,5},{7,6},{8,7},{9,8},{10,9},{11,1... | collective-permute-start | bytes 12582920 | tf_op jit(solution)/shard_map/ppermute | solution.py:16
  2.7 3.0 %collective-permute-start.5 = (bf16[2048,1024]{1,0:T(8,128)(2,1)}, bf16[2048,1024]{1,0:T(8,128)(2,1)}, u32[]{:S(2)}, u32[]{:S(2)}) collective-permute-start(bf16[2048,1024]{1,0:T(8,128)(2,1)} %own_ref.5), channel_id=1, source_target_pairs={{0,1},{1,2},{2,3},{3,4},{4,5},{5,6},{6,7},{7,8},{8,9},{9,10},{10,1... | collective-permute-start | bytes 12582920 | tf_op jit(solution)/shard_map/ppermute | solution.py:16
  5.7 4.3 %collective-permute-start = (bf16[2048,1024]{1,0:T(8,128)(2,1)}, bf16[2048,1024]{1,0:T(8,128)(2,1)}, u32[]{:S(2)}, u32[]{:S(2)}) collective-permute-start(bf16[2048,1024]{1,0:T(8,128)(2,1)} %own_ref.5), channel_id=1, source_target_pairs={{64,0},{128,64},{192,128},{65,1},{129,65},{193,129},{66,2},{130,66... | collective-permute-start | bytes 12582920 | tf_op jit(solution)/shard_map/ppermute | solution.py:16
  10.1 1.3 collective-permute-start.1
  11.4 3.1 %fusion.sqc_ref = f32[8,256]{1,0:T(8,128)S(1)} fusion(bf16[8,256,1024]{2,1,0:T(8,128)(2,1)} %bitcast.38), kind=kLoop, calls=%fused_computation.1 | loop fusion | flops 6289408 | bytes 4202496 | tf_op jit(solution)/shard_map/bsd,bsd->bs/dot_general | solution.py:20
  14.5 0.0 copy-start
  15.1 0.0 copy-done.1
  15.2 0.1 copy.10
  15.2 0.1 convert_element_type.60
  15.3 0.1 concatenate.128
  15.4 2.8 %collective-permute-start.6 = (f32[2081]{0:T(1024)S(1)}, f32[2081]{0:T(1024)S(1)}, u32[]{:S(2)}, u32[]{:S(2)}) collective-permute-start(f32[2081]{0:T(1024)S(1)} %concatenate.128), channel_id=1, source_target_pairs={{1,0},{2,1},{3,2},{4,3},{5,4},{6,5},{7,6},{8,7},{9,8},{10,9},{11,1... | collective-permute-start | bytes 24980 | tf_op jit(solution)/shard_map/ppermute | solution.py:16
  18.3 0.1 copy.11
  18.3 0.1 copy.9
  18.4 0.1 and_reduce_fusion
  18.6 0.1 fusion.10
  18.7 0.1 add_reduce_fusion
  18.8 0.1 add_clamp_fusion
  18.9 6.5 %copy.12 = bf16[2048,1024]{0,1:T(8,128)(2,1)} copy(bf16[2048,1024]{1,0:T(8,128)(2,1)} %own_ref.5) | data formatting | bytes 8388608 | tf_op args[0]
  25.4 0.6 reshape.361.tab
  26.0 0.0 copy-done
  26.0 1.3 copy.13.refs_1_
  27.4 23.4 %collective-permute-done.6 = f32[2081]{0:T(1024)S(1)} collective-permute-done((f32[2081]{0:T(1024)S(1)}, f32[2081]{0:T(1024)S(1)}, u32[]{:S(2)}, u32[]{:S(2)}) %collective-permute-start.6) | collective-permute-done | bytes 8356 | tf_op jit(solution)/shard_map/ppermute | solution.py:16
  50.7 1.9 %collective-permute-start.7 = (f32[2081]{0:T(1024)S(1)}, f32[2081]{0:T(1024)S(1)}, u32[]{:S(2)}, u32[]{:S(2)}) collective-permute-start(f32[2081]{0:T(1024)S(1)} %concatenate.128), channel_id=1, source_target_pairs={{0,1},{1,2},{2,3},{3,4},{4,5},{5,6},{6,7},{7,8},{8,9},{9,10},{10,1... | collective-permute-start | bytes 24980 | tf_op jit(solution)/shard_map/ppermute | solution.py:16
  52.6 0.0 copy-start.2
  52.7 28.1 %shard_map.37 = (f32[8,256,1024]{2,1,0:T(8,128)}, f32[8,1,256]{2,1,0:T(1,128)}) custom-call(s32[160]{0:T(256)} %reshape.361.tab, bf16[2048,1024]{1,0:T(8,128)(2,1)} %own_ref.5, bf16[1024,2048]{1,0:T(8,128)(2,1)} %bitcast.39, f32[8,256]{1,0:T(8,128)} %copy-done, bf16[2048,1024]{1,0:T(8,128)(2,1)} %own_ref.5, f32[8,256,1]{2,1,0:T(8,128)} %copy.13.refs_1_), custom_call_target="tpu_custom_call" | custom-call | flops 10737418240 | bytes 16777216 | tf_op jit(solution)/shard_map/pallas_call | solution.py:108
  80.8 0.0 collective-permute-done.7
  80.8 1.3 collective-permute-start.2
  82.1 0.0 collective-permute-done.4.refs_0_
  82.1 1.3 collective-permute-start.3
  83.4 0.0 collective-permute-done.5.refs_1_
  83.4 0.6 slice.47
  84.0 2.0 %copy.14.refs_2_ = f32[16,256,1]{2,1,0:T(8,128)} copy(f32[16,256,1]{1,0,2:T(8,128)S(1)} %maximum_bitcast_fusion) | data formatting | bytes 32768 | tf_op jit(solution)/shard_map/broadcast_in_dim | solution.py:188
  86.0 0.1 convert_element_type.64
  86.6 0.2 fusion.3
  86.8 0.1 add_clamp_fusion.2
  86.9 0.1 add_clamp_fusion.3
  87.0 0.2 compare_reduce_fusion.3
  87.2 0.1 add_convert_fusion
  87.3 0.0 copy-done.2
  87.3 0.6 reshape.362.tab
  87.9 30.4 %shard_map.38 = (f32[8,256,1024]{2,1,0:T(8,128)}, f32[8,1,256]{2,1,0:T(1,128)}) custom-call(s32[128]{0:T(128)} %reshape.362.tab, bf16[2048,1024]{1,0:T(8,128)(2,1)} %own_ref.5, bf16[1024,2048]{1,0:T(8,128)(2,1)} %bitcast.40, f32[8,256]{1,0:T(8,128)} %copy-done, bf16[2048,1024]{1,0:T(8,128)(2,1)} %collective-permute-done.4.refs_0_, ...), custom_call_target="tpu_custom_call" | custom-call | flops 8589934592 | bytes 20971520 | tf_op jit(solution)/shard_map/pallas_call | solution.py:108
  118.3 0.0 collective-permute-done.2
  118.3 0.0 collective-permute-done.3
  118.3 0.0 collective-permute-done.refs_0_
  118.3 0.0 collective-permute-done.1.refs_1_
  118.3 0.6 slice.53
  118.9 2.0 %copy.15.refs_2_ = f32[16,256,1]{2,1,0:T(8,128)} copy(f32[16,256,1]{1,0,2:T(8,128)S(1)} %maximum_bitcast_fusion.1) | data formatting | bytes 32768 | tf_op jit(solution)/shard_map/broadcast_in_dim | solution.py:201
  121.0 0.1 convert_element_type.68
  121.1 0.2 compare_reduce_fusion.1
  121.3 0.2 fusion.4
  121.5 0.1 add_clamp_fusion.4
  122.2 0.1 add_clamp_fusion.5
  122.3 0.1 add_convert_fusion.1
  122.4 0.7 reshape.365.tab
  123.0 19.3 %shard_map.39 = bf16[8,256,1024]{2,1,0:T(8,128)(2,1)} custom-call(s32[128]{0:T(128)} %reshape.365.tab, bf16[2048,1024]{1,0:T(8,128)(2,1)} %own_ref.5, bf16[1024,2048]{1,0:T(8,128)(2,1)} %bitcast.41, f32[8,256]{1,0:T(8,128)} %copy-done, bf16[2048,1024]{1,0:T(8,128)(2,1)} %collective-permute-done.refs_0_, bf16[2048,1024]{1,0:T(8,128)(2,1)} %collective-permute-done.1.refs_1_, ...), custom_call_target="tpu_custom_call" | custom-call | flops 8589934592 | bytes 20971520 | tf_op jit(solution)/shard_map/pallas_call | solution.py:108
  (24 shorter events, 0.1 us)
Async XLA Ops:
  0.0 15.1 %copy-start.1 = (s32[16,2]{0,1:T(2,128)S(1)}, s32[16,2]{0,1:T(2,128)}, u32[]{:S(2)}) copy-start(s32[16,2]{0,1:T(2,128)} %param.4) | copy-start | bytes 388
  0.0 82.1 %collective-permute-start.4 = (bf16[2048,1024]{1,0:T(8,128)(2,1)}, bf16[2048,1024]{1,0:T(8,128)(2,1)}, u32[]{:S(2)}, u32[]{:S(2)}) collective-permute-start(bf16[2048,1024]{1,0:T(8,128)(2,1)} %own_ref.5), channel_id=1, source_target_pairs={{1,0},{2,1},{3,2},{4,3},{5,4},{6,5},{7,6},{8,7},{9,8},{10,9},{11,1... | collective-permute-start | bytes 12582920 | tf_op jit(solution)/shard_map/ppermute | solution.py:16
  2.7 80.7 %collective-permute-start.5 = (bf16[2048,1024]{1,0:T(8,128)(2,1)}, bf16[2048,1024]{1,0:T(8,128)(2,1)}, u32[]{:S(2)}, u32[]{:S(2)}) collective-permute-start(bf16[2048,1024]{1,0:T(8,128)(2,1)} %own_ref.5), channel_id=1, source_target_pairs={{0,1},{1,2},{2,3},{3,4},{4,5},{5,6},{6,7},{7,8},{8,9},{9,10},{10,1... | collective-permute-start | bytes 12582920 | tf_op jit(solution)/shard_map/ppermute | solution.py:16
  5.7 112.6 %collective-permute-start = (bf16[2048,1024]{1,0:T(8,128)(2,1)}, bf16[2048,1024]{1,0:T(8,128)(2,1)}, u32[]{:S(2)}, u32[]{:S(2)}) collective-permute-start(bf16[2048,1024]{1,0:T(8,128)(2,1)} %own_ref.5), channel_id=1, source_target_pairs={{64,0},{128,64},{192,128},{65,1},{129,65},{193,129},{66,2},{130,66... | collective-permute-start | bytes 12582920 | tf_op jit(solution)/shard_map/ppermute | solution.py:16
  10.1 108.2 %collective-permute-start.1 = (bf16[2048,1024]{1,0:T(8,128)(2,1)}, bf16[2048,1024]{1,0:T(8,128)(2,1)}, u32[]{:S(2)}, u32[]{:S(2)}) collective-permute-start(bf16[2048,1024]{1,0:T(8,128)(2,1)} %own_ref.5), channel_id=1, source_target_pairs={{0,64},{64,128},{128,192},{1,65},{65,129},{129,193},{2,66},{66,130... | collective-permute-start | bytes 12582920 | tf_op jit(solution)/shard_map/ppermute | solution.py:16
  14.5 11.6 %copy-start = (f32[8,256]{1,0:T(8,128)}, f32[8,256]{1,0:T(8,128)S(1)}, u32[]{:S(2)}) copy-start(f32[8,256]{1,0:T(8,128)S(1)} %fusion.sqc_ref) | copy-start | bytes 24580
  15.4 35.3 %collective-permute-start.6 = (f32[2081]{0:T(1024)S(1)}, f32[2081]{0:T(1024)S(1)}, u32[]{:S(2)}, u32[]{:S(2)}) collective-permute-start(f32[2081]{0:T(1024)S(1)} %concatenate.128), channel_id=1, source_target_pairs={{1,0},{2,1},{3,2},{4,3},{5,4},{6,5},{7,6},{8,7},{9,8},{10,9},{11,1... | collective-permute-start | bytes 24980 | tf_op jit(solution)/shard_map/ppermute | solution.py:16
  50.7 30.1 %collective-permute-start.7 = (f32[2081]{0:T(1024)S(1)}, f32[2081]{0:T(1024)S(1)}, u32[]{:S(2)}, u32[]{:S(2)}) collective-permute-start(f32[2081]{0:T(1024)S(1)} %concatenate.128), channel_id=1, source_target_pairs={{0,1},{1,2},{2,3},{3,4},{4,5},{5,6},{6,7},{7,8},{8,9},{9,10},{10,1... | collective-permute-start | bytes 24980 | tf_op jit(solution)/shard_map/ppermute | solution.py:16
  52.6 34.6 %copy-start.2 = (s32[1,32]{1,0:T(1,128)S(1)}, s32[1,32]{1,0:T(1,128)}, u32[]{:S(2)}) copy-start(s32[1,32]{1,0:T(1,128)} %constant.30.clone.1) | copy-start | bytes 388
  80.8 37.5 %collective-permute-start.2 = (f32[2081]{0:T(1024)S(1)}, f32[2081]{0:T(1024)S(1)}, u32[]{:S(2)}, u32[]{:S(2)}) collective-permute-start(f32[2081]{0:T(1024)S(1)} %concatenate.128), channel_id=1, source_target_pairs={{64,0},{128,64},{192,128},{65,1},{129,65},{193,129},{66,2},{130,66... | collective-permute-start | bytes 24980 | tf_op jit(solution)/shard_map/ppermute | solution.py:16
  82.1 36.2 %collective-permute-start.3 = (f32[2081]{0:T(1024)S(1)}, f32[2081]{0:T(1024)S(1)}, u32[]{:S(2)}, u32[]{:S(2)}) collective-permute-start(f32[2081]{0:T(1024)S(1)} %concatenate.128), channel_id=1, source_target_pairs={{0,64},{64,128},{128,192},{1,65},{65,129},{129,193},{2,66},{66,130... | collective-permute-start | bytes 24980 | tf_op jit(solution)/shard_map/ppermute | solution.py:16

commit v11 on v8

--- a/solution.py
+++ b/solution.py
@@ -74,7 +74,8 @@
 
         if mode == "final":
             def fin(b, carry):
-                out_ref[b] = (num_ref[b] / den_ref[b]).astype(out_ref.dtype)
+                inv = 1.0 / den_ref[b]
+                out_ref[b] = (num_ref[b] * inv).astype(out_ref.dtype)
                 return carry
             lax.fori_loop(0, nloc, fin, 0)
 

time: 133 us -> 135 us (1.015)
  the two profiles are of different devices: /device:TPU:22 before, /device:TPU:254 now
where the time goes in v11:
time: 135 us; the launch traced here: 134 us
  Pallas kernels  73.9 us (55%)
  waiting for transfers between devices  27.7 us (21%)
  starting transfers between devices  18.7 us (14%)
  other arithmetic  5.96 us (4%)
  local copies, waits for them, and re-layouts  5.19 us (4%)
  between operations  2.28 us (2%)
    pallas_call x3, Pallas kernels, run_phase(): pl.pallas_call(make_kernel(nsrc, n, mode), in_specs=in_specs, out_specs=o...  73.9 us
    ppermute x8, waiting for transfers between devices, shifted(): return lax.ppermute(shard, axis, pairs)  27.7 us
    ppermute x8, starting transfers between devices, shifted(): return lax.ppermute(shard, axis, pairs)  18.7 us
    dot_general x1, other arithmetic, squares_of(): jnp.einsum('bsd,bsd->bs', blocks, blocks, preferred_element_type=jnp.floa...  3.08 us
  transfers between devices with their start and end apart: 8, of which 1 were waited for; matrix products, arithmetic and copies ran while one was open for 6% of the time, Pallas kernels for 42%

profile of v11, /device:TPU:254, one launch (start us, length us, event | category | flops | bytes accessed | tf_op | source)
XLA Modules:
  0.0 133.7 jit_solution(16115424178278902967)
XLA Ops:
  0.0 0.0 copy-start.1
  0.0 2.3 %collective-permute-start.4 = (bf16[2048,1024]{1,0:T(8,128)(2,1)}, bf16[2048,1024]{1,0:T(8,128)(2,1)}, u32[]{:S(2)}, u32[]{:S(2)}) collective-permute-start(bf16[2048,1024]{1,0:T(8,128)(2,1)} %own_ref.5), channel_id=1, source_target_pairs={{1,0},{2,1},{3,2},{4,3},{5,4},{6,5},{7,6},{8,7},{9,8},{10,9},{11,1... | collective-permute-start | bytes 12582920 | tf_op jit(solution)/shard_map/ppermute | solution.py:16
  2.3 4.1 %collective-permute-start.5 = (bf16[2048,1024]{1,0:T(8,128)(2,1)}, bf16[2048,1024]{1,0:T(8,128)(2,1)}, u32[]{:S(2)}, u32[]{:S(2)}) collective-permute-start(bf16[2048,1024]{1,0:T(8,128)(2,1)} %own_ref.5), channel_id=1, source_target_pairs={{0,1},{1,2},{2,3},{3,4},{4,5},{5,6},{6,7},{7,8},{8,9},{9,10},{10,1... | collective-permute-start | bytes 12582920 | tf_op jit(solution)/shard_map/ppermute | solution.py:16
  6.4 4.6 %collective-permute-start = (bf16[2048,1024]{1,0:T(8,128)(2,1)}, bf16[2048,1024]{1,0:T(8,128)(2,1)}, u32[]{:S(2)}, u32[]{:S(2)}) collective-permute-start(bf16[2048,1024]{1,0:T(8,128)(2,1)} %own_ref.5), channel_id=1, source_target_pairs={{64,0},{128,64},{192,128},{65,1},{129,65},{193,129},{66,2},{130,66... | collective-permute-start | bytes 12582920 | tf_op jit(solution)/shard_map/ppermute | solution.py:16
  11.0 1.3 collective-permute-start.1
  12.3 3.1 %fusion.refs_1_ = f32[8,256]{1,0:T(8,128)S(1)} fusion(bf16[8,256,1024]{2,1,0:T(8,128)(2,1)} %bitcast.33), kind=kLoop, calls=%fused_computation.1 | loop fusion | flops 6289408 | bytes 4202496 | tf_op jit(solution)/shard_map/bsd,bsd->bs/dot_general | solution.py:20
  15.4 0.0 copy-start
  16.1 0.0 copy-done.1
  16.1 0.1 copy.8
  16.2 0.1 convert_element_type.60
  16.2 0.1 concatenate.128
  16.3 1.9 %collective-permute-start.6 = (f32[2081]{0:T(1024)S(1)}, f32[2081]{0:T(1024)S(1)}, u32[]{:S(2)}, u32[]{:S(2)}) collective-permute-start(f32[2081]{0:T(1024)S(1)} %concatenate.128), channel_id=1, source_target_pairs={{1,0},{2,1},{3,2},{4,3},{5,4},{6,5},{7,6},{8,7},{9,8},{10,9},{11,1... | collective-permute-start | bytes 24980 | tf_op jit(solution)/shard_map/ppermute | solution.py:16
  18.3 0.1 copy.9
  18.4 0.1 copy.7
  18.4 0.1 and_reduce_fusion
  18.6 0.1 fusion.10
  18.7 0.1 add_reduce_fusion
  18.8 0.1 add_clamp_fusion
  18.9 0.7 reshape.361.tab
  19.6 1.4 %copy.10.sqc_ref = f32[8,256,1]{2,1,0:T(8,128)} copy(f32[8,256,1]{1,0,2:T(8,128)S(1)} %bitcast.35) | data formatting | bytes 16384 | tf_op jit(solution)/shard_map/broadcast_in_dim | solution.py:161
  20.9 0.0 copy-start.2
  20.9 27.7 %collective-permute-done.6 = f32[2081]{0:T(1024)S(1)} collective-permute-done((f32[2081]{0:T(1024)S(1)}, f32[2081]{0:T(1024)S(1)}, u32[]{:S(2)}, u32[]{:S(2)}) %collective-permute-start.6) | collective-permute-done | bytes 8356 | tf_op jit(solution)/shard_map/ppermute | solution.py:16
  48.7 1.9 %collective-permute-start.7 = (f32[2081]{0:T(1024)S(1)}, f32[2081]{0:T(1024)S(1)}, u32[]{:S(2)}, u32[]{:S(2)}) collective-permute-start(f32[2081]{0:T(1024)S(1)} %concatenate.128), channel_id=1, source_target_pairs={{0,1},{1,2},{2,3},{3,4},{4,5},{5,6},{6,7},{7,8},{8,9},{9,10},{10,1... | collective-permute-start | bytes 24980 | tf_op jit(solution)/shard_map/ppermute | solution.py:16
  50.6 0.0 copy-done
  50.6 24.4 %shard_map.37 = (f32[8,256,1024]{2,1,0:T(8,128)}, f32[8,256,1]{2,1,0:T(8,128)}) custom-call(s32[160]{0:T(256)} %reshape.361.tab, bf16[2048,1024]{1,0:T(8,128)(2,1)} %own_ref.5, f32[8,256,1]{2,1,0:T(8,128)} %copy.10.sqc_ref, bf16[2048,1024]{1,0:T(8,128)(2,1)} %own_ref.5, f32[8,256]{1,0:T(8,128)} %copy-done), custom_call_target="tpu_custom_call" | custom-call | flops 10737418240 | bytes 16777216 | tf_op jit(solution)/shard_map/pallas_call | solution.py:108
  75.0 0.0 collective-permute-done.7
  75.0 1.3 collective-permute-start.2
  76.3 0.0 collective-permute-done.4.refs_0_
  76.3 1.3 collective-permute-start.3
  77.6 0.0 collective-permute-done.5.refs_1_
  77.6 0.7 slice.47
  78.3 0.1 convert_element_type.64
  79.1 0.2 fusion.3
  79.3 0.1 add_clamp_fusion.2
  79.4 0.1 add_clamp_fusion.3
  79.4 0.2 compare_reduce_fusion.3
  79.7 0.1 add_convert_fusion
  79.7 0.0 copy-done.2
  79.8 0.7 reshape.362.tab
  80.4 0.6 pad_maximum_fusion.refs_2_
  81.0 31.2 %shard_map.38 = (f32[8,256,1024]{2,1,0:T(8,128)}, f32[8,256,1]{2,1,0:T(8,128)}) custom-call(s32[128]{0:T(128)} %reshape.362.tab, bf16[2048,1024]{1,0:T(8,128)(2,1)} %own_ref.5, f32[8,256,1]{2,1,0:T(8,128)} %copy.10.sqc_ref, bf16[2048,1024]{1,0:T(8,128)(2,1)} %collective-permute-done.4.refs_0_, bf16[2048,1024]{1,0:T(8,128)(2,1)} %collective-permute-done.5.refs_1_, ...), custom_call_target="tpu_custom_call" | custom-call | flops 8589934592 | bytes 20971520 | tf_op jit(solution)/shard_map/pallas_call | solution.py:108
  112.3 0.0 collective-permute-done.2
  112.3 0.0 collective-permute-done.3
  112.3 0.0 collective-permute-done.refs_0_
  112.3 0.0 collective-permute-done.1.refs_1_
  112.3 0.6 slice.53
  112.9 0.1 convert_element_type.68
  113.0 0.2 compare_reduce_fusion.1
  113.2 0.2 fusion.4
  113.4 0.1 add_clamp_fusion.4
  114.1 0.1 add_clamp_fusion.5
  114.2 0.1 add_convert_fusion.1
  114.3 0.6 reshape.365.tab
  114.9 0.6 pad_maximum_fusion.1.refs_2_
  115.5 18.2 %shard_map.39 = bf16[8,256,1024]{2,1,0:T(8,128)(2,1)} custom-call(s32[128]{0:T(128)} %reshape.365.tab, bf16[2048,1024]{1,0:T(8,128)(2,1)} %own_ref.5, f32[8,256,1]{2,1,0:T(8,128)} %copy.10.sqc_ref, bf16[2048,1024]{1,0:T(8,128)(2,1)} %collective-permute-done.refs_0_, bf16[2048,1024]{1,0:T(8,128)(2,1)} %collective-permute-done.1.refs_1_, ...), custom_call_target="tpu_custom_call" | custom-call | flops 8589934592 | bytes 20971520 | tf_op jit(solution)/shard_map/pallas_call | solution.py:108
  (22 shorter events, 0.1 us)
Async XLA Ops:
  0.0 16.1 %copy-start.1 = (s32[16,2]{0,1:T(2,128)S(1)}, s32[16,2]{0,1:T(2,128)}, u32[]{:S(2)}) copy-start(s32[16,2]{0,1:T(2,128)} %param.4) | copy-start | bytes 388
  0.0 76.3 %collective-permute-start.4 = (bf16[2048,1024]{1,0:T(8,128)(2,1)}, bf16[2048,1024]{1,0:T(8,128)(2,1)}, u32[]{:S(2)}, u32[]{:S(2)}) collective-permute-start(bf16[2048,1024]{1,0:T(8,128)(2,1)} %own_ref.5), channel_id=1, source_target_pairs={{1,0},{2,1},{3,2},{4,3},{5,4},{6,5},{7,6},{8,7},{9,8},{10,9},{11,1... | collective-permute-start | bytes 12582920 | tf_op jit(solution)/shard_map/ppermute | solution.py:16
  2.3 75.3 %collective-permute-start.5 = (bf16[2048,1024]{1,0:T(8,128)(2,1)}, bf16[2048,1024]{1,0:T(8,128)(2,1)}, u32[]{:S(2)}, u32[]{:S(2)}) collective-permute-start(bf16[2048,1024]{1,0:T(8,128)(2,1)} %own_ref.5), channel_id=1, source_target_pairs={{0,1},{1,2},{2,3},{3,4},{4,5},{5,6},{6,7},{7,8},{8,9},{9,10},{10,1... | collective-permute-start | bytes 12582920 | tf_op jit(solution)/shard_map/ppermute | solution.py:16
  6.4 105.9 %collective-permute-start = (bf16[2048,1024]{1,0:T(8,128)(2,1)}, bf16[2048,1024]{1,0:T(8,128)(2,1)}, u32[]{:S(2)}, u32[]{:S(2)}) collective-permute-start(bf16[2048,1024]{1,0:T(8,128)(2,1)} %own_ref.5), channel_id=1, source_target_pairs={{64,0},{128,64},{192,128},{65,1},{129,65},{193,129},{66,2},{130,66... | collective-permute-start | bytes 12582920 | tf_op jit(solution)/shard_map/ppermute | solution.py:16
  11.0 101.3 %collective-permute-start.1 = (bf16[2048,1024]{1,0:T(8,128)(2,1)}, bf16[2048,1024]{1,0:T(8,128)(2,1)}, u32[]{:S(2)}, u32[]{:S(2)}) collective-permute-start(bf16[2048,1024]{1,0:T(8,128)(2,1)} %own_ref.5), channel_id=1, source_target_pairs={{0,64},{64,128},{128,192},{1,65},{65,129},{129,193},{2,66},{66,130... | collective-permute-start | bytes 12582920 | tf_op jit(solution)/shard_map/ppermute | solution.py:16
  15.4 35.2 %copy-start = (f32[8,256]{1,0:T(8,128)}, f32[8,256]{1,0:T(8,128)S(1)}, u32[]{:S(2)}) copy-start(f32[8,256]{1,0:T(8,128)S(1)} %fusion.refs_1_) | copy-start | bytes 24580
  16.3 32.3 %collective-permute-start.6 = (f32[2081]{0:T(1024)S(1)}, f32[2081]{0:T(1024)S(1)}, u32[]{:S(2)}, u32[]{:S(2)}) collective-permute-start(f32[2081]{0:T(1024)S(1)} %concatenate.128), channel_id=1, source_target_pairs={{1,0},{2,1},{3,2},{4,3},{5,4},{6,5},{7,6},{8,7},{9,8},{10,9},{11,1... | collective-permute-start | bytes 24980 | tf_op jit(solution)/shard_map/ppermute | solution.py:16
  20.9 58.8 %copy-start.2 = (s32[1,32]{1,0:T(1,128)S(1)}, s32[1,32]{1,0:T(1,128)}, u32[]{:S(2)}) copy-start(s32[1,32]{1,0:T(1,128)} %constant.30.clone.1) | copy-start | bytes 388
  48.7 26.4 %collective-permute-start.7 = (f32[2081]{0:T(1024)S(1)}, f32[2081]{0:T(1024)S(1)}, u32[]{:S(2)}, u32[]{:S(2)}) collective-permute-start(f32[2081]{0:T(1024)S(1)} %concatenate.128), channel_id=1, source_target_pairs={{0,1},{1,2},{2,3},{3,4},{4,5},{5,6},{6,7},{7,8},{8,9},{9,10},{10,1... | collective-permute-start | bytes 24980 | tf_op jit(solution)/shard_map/ppermute | solution.py:16
  75.0 37.3 %collective-permute-start.2 = (f32[2081]{0:T(1024)S(1)}, f32[2081]{0:T(1024)S(1)}, u32[]{:S(2)}, u32[]{:S(2)}) collective-permute-start(f32[2081]{0:T(1024)S(1)} %concatenate.128), channel_id=1, source_target_pairs={{64,0},{128,64},{192,128},{65,1},{129,65},{193,129},{66,2},{130,66... | collective-permute-start | bytes 24980 | tf_op jit(solution)/shard_map/ppermute | solution.py:16
  76.3 36.0 %collective-permute-start.3 = (f32[2081]{0:T(1024)S(1)}, f32[2081]{0:T(1024)S(1)}, u32[]{:S(2)}, u32[]{:S(2)}) collective-permute-start(f32[2081]{0:T(1024)S(1)} %concatenate.128), channel_id=1, source_target_pairs={{0,64},{64,128},{128,192},{1,65},{65,129},{129,193},{2,66},{66,130... | collective-permute-start | bytes 24980 | tf_op jit(solution)/shard_map/ppermute | solution.py:16
